TPU v7x, 32 devices: a whole 2x2x4 slice. The times are simulated.
32 devices in a mesh: seq: 16 (over z, x, core), mlp: 2 (over y).
Axes of the slice: x: 2, y: 2, z: 4, core: 2. Of those that a mesh axis runs over, the one named last changes fastest.
Arguments:
- patches: bfloat16 [16384, 768], P(('seq', 'mlp')), may hold values from -6 to 6
- segments: int32 [16384], P(('seq', 'mlp')), may hold values from 0 to 5, as said below
- prompt_slots: int32 [16384], P(('seq', 'mlp')), may hold values from 0 to 50, as said below
- norm_gains: float32 [2, 2, 768], replicated, may hold values from 0.25 to 1.75
- qkv_weight: bfloat16 [2, 768, 2304], P(None, 'seq'), may hold values from -0.21875 to 0.21875
- out_weight: bfloat16 [2, 768, 768], P(None, 'seq'), may hold values from -0.875 to 0.875
- up_weight: bfloat16 [2, 768, 3072], P(None, 'seq', 'mlp'), may hold values from -0.21875 to 0.21875
- down_weight: bfloat16 [2, 3072, 768], P(None, 'mlp', 'seq'), may hold values from -0.15625 to 0.15625
- cotangent: bfloat16 [16384, 768], P(('seq', 'mlp')), may hold values from -6 to 6
- prompts: float32 [76800], P(('seq', 'mlp')), may hold values from -5 to 5
- first_moment: float32 [76800], P(('seq', 'mlp')), may hold values from -0.24 to 0.24
- second_moment: float32 [76800], P(('seq', 'mlp')), may hold values from 1e-05 to 0.015
- adam_betas: float32 [2], replicated, may hold values from 0.4 to 0.6
- learn_rate: float32 [1], replicated, may hold values from 0.2 to 0.6
Outputs:
- block_output: bfloat16 [16384, 768], P(('seq', 'mlp'))
- input_grad: float32 [16384, 768], P(('seq', 'mlp'))
- new_prompts: float32 [76800], P(('seq', 'mlp'))
- new_first: float32 [76800], P(('seq', 'mlp'))
- new_second: float32 [76800], P(('seq', 'mlp'))
- grad_norm: float32 [1], replicated
Inputs may be any that keep to these rules, and one draw needn't show every extreme that they name: `segments`: the 512 tokens of one device form aligned blocks in which whole images lie one after another, numbered 0, 1, 2 and so on; each image has 51 to 247 tokens, and every block holds an image of exactly 247 tokens. `prompt_slots`: the first 50 tokens of each image hold slots 0 to 49 in order; all other tokens hold 50.
All inputs are finite; a program needn't handle non-finite values.
Results may differ from a plain program's by a relative error of at most 0.02.
Values may be sent and summed in bfloat16 or wider, within the bound.
No kernel may reach another device: no remote copies, remote signals or barrier semaphores. Data moves between devices by JAX's collectives and lax.ppermute only.
A program may use at most 192 MiB of HBM per device.

v0:
```python
import math
from functools import partial

import jax
import jax.numpy as jnp
import numpy as np
from jax import lax
from jax.experimental import pallas as pl
from jax.experimental.pallas import tpu as pltpu
from jax.sharding import Mesh
from jax.sharding import PartitionSpec as P

HEADS = 12
HEAD_DIM = 64
ADAM_STEP = 2

ln_eps = 1e-06
masked_score = -1e30
clip_ratio = 0.05
adam_eps = 1e-08
decay_rate = 0.1
ALL = ("z", "x", "core", "y")
f32 = jnp.float32
bf16 = jnp.bfloat16
LANES = 128
TILE = 256
FORWARD_VMEM = 30 * 2**20
BACKWARD_VMEM = 56 * 2**20

TAIL_SLOPE = 0.275
TAIL_POLY = (
    0.10971068582446765,
    0.1096543595961662,
    0.10219045697718625,
    0.07893593678575173,
    0.08800740710695068,
    -0.03516190352887128,
    0.13017028940734943,
    -0.11067510560848658,
    0.027167870070925505,
)


def mm(a, b):
    return jnp.dot(a, b, preferred_element_type=f32)


def mm_t(a, b):
    return lax.dot_general(a, b, (((1,), (1,)), ((), ())), preferred_element_type=f32)


def gelu_parts(v):
    a = jnp.abs(v)
    bell = jnp.exp(v * v * -0.5)
    t = 1.0 / (1.0 + TAIL_SLOPE * a)
    poly = jnp.full_like(v, TAIL_POLY[-1])
    for factor in TAIL_POLY[-2::-1]:
        poly = poly * t + factor
    tail = poly * t * bell
    return jnp.where(v >= 0.0, 1.0 - tail, tail), bell * (1.0 / math.sqrt(2.0 * math.pi))


def norm_stats(values):
    center = values - jnp.mean(values, axis=-1, keepdims=True)
    rstd = lax.rsqrt(jnp.mean(center * center, axis=-1, keepdims=True) + ln_eps)
    return center * rstd, rstd


def norm_back(grad, values, gain_row):
    unit, rstd = norm_stats(values)
    grad = grad * gain_row
    mean_grad = jnp.mean(grad, axis=-1, keepdims=True)
    mean_dot = jnp.mean(grad * unit, axis=-1, keepdims=True)
    return rstd * (grad - mean_grad - unit * mean_dot)


class Copies:
    def __init__(self, pairs, sems):
        self.copies = [
            pltpu.make_async_copy(source, target, sems.at[i])
            for i, (source, target) in enumerate(pairs)
        ]

    def start(self):
        for copy in self.copies:
            copy.start()
        return self

    def wait(self):
        for copy in self.copies:
            copy.wait()


def shards(refs):
    z, x, core, y = (lax.axis_index(axis) for axis in ALL)
    found = []
    for i, ref in enumerate(refs):
        c = core ^ i
        for step in range(4):
            to_x, to_y = ((x, y), (x ^ 1 ^ c, y ^ c), (x ^ c, y ^ 1 ^ c), (x ^ 1, y ^ 1))[step]
            for back in range(4):
                found.append((ref.at[step // 2, step % 2, back], (z ^ back, to_x, c, to_y)))
    return found


def weight_copies(refs, column, width, dest, sems):
    if refs[0].ndim == 2:
        y_size = dest.shape[-1] // width
        columns = pl.ds(column * y_size, dest.shape[-1])
        return Copies([(refs[0].at[:, columns], dest)], sems)
    rows = refs[0].shape[-2]
    pairs = []
    for ref, (z, x, core, y) in shards(refs):
        to_rows = pl.ds(pl.multiple_of((x * 2 + core) * rows, 16), rows)
        to_columns = pl.ds(pl.multiple_of(y * width, LANES), width)
        pairs.append((ref.at[:, pl.ds(column, width)], dest.at[z, to_rows, to_columns]))
    return Copies(pairs, sems)


def rider_copies(refs, column, dest, sems):
    pairs = []
    for ref, (z, x, core, y) in shards(refs):
        source = ref.at[:, pl.ds(column, LANES)]
        pairs.append((source, dest.at[((z * 2 + x) * 2 + core) * 2 + y]))
    return Copies(pairs, sems)


def rows_view(ref, columns=None):
    value = ref[...] if columns is None else ref[..., columns]
    return value.reshape(-1, value.shape[-1])


def head_of(pair, head):
    lane = lax.broadcasted_iota(jnp.int32, pair.shape, 1)
    keep = (lane < HEAD_DIM) if head == 0 else (lane >= HEAD_DIM)
    return jnp.where(keep, pair, jnp.zeros_like(pair))


def as_column(row):
    return jnp.broadcast_to(row.astype(f32), (8, row.shape[1])).T[:, :1]


def fill_bias(bias_ref, seg_ref):
    seg = seg_ref[...]
    bias_ref[...] = jnp.where(as_column(seg) == seg.astype(f32), 0.0, masked_score)


def copy_out(source, target, sem):
    copy = pltpu.make_async_copy(source, target, sem)
    copy.start()
    return copy


def attention(qkv_ref, bias_ref, mixed_ref, lse_ref):
    tokens, width = mixed_ref.shape
    pairs = width // LANES
    lane = lax.broadcasted_iota(jnp.int32, (tokens, LANES), 1)
    low = lane < HEAD_DIM
    lse = jnp.zeros((tokens, LANES), f32)
    for at in range(pairs):
        query, key, value = (
            qkv_ref[:, i * width + at * LANES : i * width + (at + 1) * LANES] for i in range(3)
        )
        ones = jnp.ones_like(value)
        values = (jnp.where(low, value, ones), jnp.where(low, ones, value))
        parts, tops = [], []
        for head in range(2):
            scores = mm_t(head_of(query, head), key) + bias_ref[...]
            top = jnp.max(scores, axis=1, keepdims=True)
            parts.append(mm(jnp.exp(scores - top).astype(bf16), values[head]))
            tops.append(top)
        total = pltpu.roll(jnp.where(low, parts[1], parts[0]), HEAD_DIM, 1)
        mixed = jnp.where(low, parts[0], parts[1]) / total
        mixed_ref[:, at * LANES : (at + 1) * LANES] = mixed.astype(bf16)
        pair_lse = jnp.where(low, tops[0], tops[1]) + jnp.log(total)
        lse = jnp.where((lane & (HEAD_DIM - 1)) == at, pair_lse, lse)
    lse_ref[...] = lse.T


def attention_back(qkv_ref, mixed_ref, lse_ref, bias_ref, dqkv_ref):
    tokens, width = mixed_ref.shape
    pairs = width // LANES
    for at in range(pairs):
        places = [slice(i * width + at * LANES, i * width + (at + 1) * LANES) for i in range(3)]
        query, key, value = (qkv_ref[:, place] for place in places)
        grad = mixed_ref[:, at * LANES : (at + 1) * LANES]
        found = [None, None, None]
        for head in range(2):
            query_head, key_head, grad_head = (head_of(v, head) for v in (query, key, grad))
            row = head * HEAD_DIM + at
            scores = mm_t(key, query_head) + bias_ref[...]
            probs = jnp.exp(scores - lse_ref[row : row + 1, :])
            grad_probs = mm_t(value, grad_head)
            inner = jnp.sum(probs * grad_probs, axis=0, keepdims=True)
            d_scores = (probs * (grad_probs - inner)).astype(bf16)
            for i, part in enumerate(
                (
                    mm(d_scores.T, key_head),
                    mm(d_scores, query_head),
                    mm(probs.astype(bf16), grad_head),
                )
            ):
                found[i] = part if head == 0 else found[i] + part
        found[0] = found[0] * HEAD_DIM**-0.5
        for place, part in zip(places, found):
            dqkv_ref[:, place] = part.astype(bf16)


def attn_forward_body(plan, *refs):
    count, layer_at, slot_total, takes_riders, has_down = plan
    pieces, refs = refs[:count], refs[count:]
    if has_down:
        (middle_in, active_in), refs = refs[:2], refs[2:]
    else:
        x_ref, refs = refs[0], refs[1:]
    slot_ref, base_ref, seg_ref, gain_ref = refs[:4]
    refs = refs[4:]
    if not takes_riders:
        rider_ref, refs = refs[0], refs[1:]
    mixed_ref, lse_ref, entry_out, qkv_out, weight_out = refs[:5]
    refs = refs[5:]
    if takes_riders:
        (rider_out, rider_ref), refs = (refs[0], refs[1]), refs[2:]
    if has_down:
        (down_out, w_down, middle_ref, active_ref, sem_down), refs = refs[:5], refs[5:]
    w_qkv, norm_ref, bias_ref, entry_ref, qkv_ref, sem_a, sem_b, sem_c = refs
    tokens, width = mixed_ref.shape
    parts = 1 if pieces[0].ndim == 2 else 2
    cut = 3 * width // parts
    qkv_pieces, column = pieces, 0
    copies = []
    if has_down:
        units = active_ref.shape[1]
        load_middle = copy_out(middle_in, middle_ref, sem_c.at[3])
        load_active = copy_out(active_in, active_ref, sem_c.at[4])
        down_pieces = pieces
        if parts == 1:
            down_pieces, qkv_pieces = pieces[:1], pieces[1:]
        else:
            column = units // parts
        load_down = weight_copies(down_pieces, 0, units // parts, w_down, sem_down).start()
    if takes_riders:
        load_riders = rider_copies(pieces, cut, rider_ref, sem_b).start()
    load_qkv = weight_copies(qkv_pieces, column, cut, w_qkv, sem_a).start()
    fill_bias(bias_ref, seg_ref)
    slots = as_column(slot_ref[...])
    onehot = (slots == base_ref[...]).astype(bf16)
    is_prompt = slots < slot_total
    if takes_riders:
        load_riders.wait()
        copies.append(copy_out(rider_ref, rider_out, sem_c.at[3]))
    holders = base_ref.shape[1] // 8
    windows = rider_ref[layer_at * holders : (layer_at + 1) * holders].astype(f32)
    if has_down:
        load_middle.wait()
        load_active.wait()
        load_down.wait()
        copies.append(copy_out(w_down, down_out, sem_c.at[3]))
        entry_ref[...] = middle_ref[...] + mm_t(active_ref[...], rows_view(w_down))
        x_ref = entry_ref
    for at in range(width // LANES):
        lanes = slice(at * LANES, (at + 1) * LANES)
        part = windows[:, at * 8 : (at + 1) * 8, :].reshape(-1, LANES)
        inject = mm(onehot, part.astype(bf16))
        entry_ref[:, lanes] = jnp.where(is_prompt, inject, x_ref[:, lanes].astype(f32))
    copies.append(copy_out(entry_ref, entry_out, sem_c.at[0]))
    norm_ref[...] = (norm_stats(entry_ref[...])[0] * gain_ref[layer_at, :1]).astype(bf16)
    load_qkv.wait()
    copies.append(copy_out(w_qkv, weight_out, sem_c.at[1]))
    for at in range(3 * width // TILE):
        columns = slice(at * TILE, (at + 1) * TILE)
        out = mm(norm_ref[...], rows_view(w_qkv, columns))
        if at < width // TILE:
            out = out.astype(bf16).astype(f32) * HEAD_DIM**-0.5
        qkv_ref[:, columns] = out.astype(bf16)
    copies.append(copy_out(qkv_ref, qkv_out, sem_c.at[2]))
    attention(qkv_ref, bias_ref, mixed_ref, lse_ref)
    for copy in copies:
        copy.wait()


def mlp_up_body(count, layer_at, *refs):
    pieces, refs = refs[:count], refs[count:]
    entry_in, mixed_ref, gain_ref = refs[:3]
    middle_out, slope_out, out_out, up_out, active_out = refs[3:8]
    w_out, w_up, norm_ref, middle_ref, active_ref, slope_ref, sem_a, sem_b, sem_d = refs[8:]
    units = slope_ref.shape[1]
    width = middle_ref.shape[1]
    parts = 1 if pieces[0].ndim == 2 else 2
    load_entry = copy_out(entry_in, middle_ref, sem_d.at[0])
    load_out = weight_copies(pieces, 0, width // parts, w_out, sem_a).start()
    load_up = weight_copies(pieces, width // parts, units // parts, w_up, sem_b).start()
    load_entry.wait()
    load_out.wait()
    middle_ref[...] = middle_ref[...] + mm(mixed_ref[...], rows_view(w_out))
    copies = [copy_out(middle_ref, middle_out, sem_d.at[0])]
    copies.append(copy_out(w_out, out_out, sem_d.at[1]))
    norm_ref[...] = (norm_stats(middle_ref[...])[0] * gain_ref[layer_at, 1:]).astype(bf16)
    load_up.wait()
    copies.append(copy_out(w_up, up_out, sem_d.at[2]))
    for at in range(units // TILE):
        columns = slice(at * TILE, (at + 1) * TILE)
        before = mm(norm_ref[...], rows_view(w_up, columns))
        phi_sum, phi = gelu_parts(before)
        active_ref[:, columns] = (before * phi_sum).astype(bf16)
        slope_ref[:, columns] = (phi_sum + before * phi).astype(bf16)
    copies.append(copy_out(slope_ref, slope_out, sem_d.at[3]))
    copies.append(copy_out(active_ref, active_out, sem_d.at[4]))
    for copy in copies:
        copy.wait()


STATE = ("slope", "middle", "qkv", "lse", "entry")
WEIGHTS = ("down", "up", "out", "qkv_weight")


def backward_body(layers, count, *refs):
    down_pieces, refs = refs[:count], refs[count:]
    sources = []
    for layer_at in range(layers):
        names = STATE + (WEIGHTS if layer_at < layers - 1 else WEIGHTS[1:])
        sources.append(dict(zip(names, refs)))
        refs = refs[len(names) :]
    active_in, refs = refs[0], refs[1:]
    cotangent_ref, slot_ref, seg_ref, gain_ref = refs[:4]
    out_ref, prompt_ref, block_ref = refs[4:7]
    refs = refs[7:]
    held = dict(zip(STATE + WEIGHTS, refs))
    refs = refs[len(held) :]
    active_ref, low_ref, before_ref, grad_ref, mixed_ref, dqkv_ref, bias_ref = refs[:7]
    sem, sem_down = refs[7:]
    order = list(held)
    units = active_ref.shape[1]
    tokens, width = grad_ref.shape

    class Fetch:
        def __init__(self, name, layer_at):
            if name == "down" and layer_at == layers - 1:
                cut = units // (1 if down_pieces[0].ndim == 2 else 2)
                self.copies = weight_copies(down_pieces, 0, cut, held[name], sem_down).copies
            else:
                source, at = sources[layer_at][name], order.index(name)
                self.copies = [pltpu.make_async_copy(source, held[name], sem.at[at])]
            for copy in self.copies:
                copy.start()

        def wait(self):
            for copy in self.copies:
                copy.wait()

    names = ("down", "slope", "up", "middle", "out", "qkv", "lse", "qkv_weight", "entry")
    load_active = None
    coming = {}
    for name in names:
        coming[name] = Fetch(name, layers - 1)
        if name == "slope":
            load_active = copy_out(active_in, active_ref, sem.at[len(order)])
    fill_bias(bias_ref, seg_ref)
    low_ref[...] = cotangent_ref[...]
    slot_total = prompt_ref.shape[1]
    is_prompt = as_column(slot_ref[...]) < slot_total
    onehot_t = (
        slot_ref[...] == lax.broadcasted_iota(jnp.int32, (slot_total, tokens), 0)
    ).astype(bf16)

    for layer_at in reversed(range(layers)):
        top = layer_at == layers - 1

        def refill(*names):
            if layer_at > 0:
                for name in names:
                    coming[name] = Fetch(name, layer_at - 1)

        coming["down"].wait()
        coming["slope"].wait()
        for at in range(units // TILE):
            columns = slice(at * TILE, (at + 1) * TILE)
            grad_active = mm(low_ref[...], rows_view(held["down"], columns))
            slope = held["slope"][:, columns].astype(f32)
            before_ref[:, columns] = (grad_active * slope).astype(bf16)
        coming["middle"].wait()
        if top:
            load_active.wait()
            branch = mm_t(active_ref[...], rows_view(held["down"]))
            block_ref[...] = (held["middle"][...] + branch).astype(bf16)
        refill("down", "slope")
        coming["up"].wait()
        grad_norm = mm_t(before_ref[...], rows_view(held["up"]))
        refill("up")
        back = norm_back(grad_norm, held["middle"][...], gain_ref[layer_at, 1:])
        grad = cotangent_ref[...].astype(f32) if top else grad_ref[...]
        grad_middle = grad + back
        grad_ref[...] = grad_middle
        low_ref[...] = grad_middle.astype(bf16)
        refill("middle")
        coming["out"].wait()
        mixed_ref[...] = mm_t(low_ref[...], rows_view(held["out"])).astype(bf16)
        refill("out")
        coming["qkv"].wait()
        coming["lse"].wait()
        attention_back(held["qkv"], mixed_ref, held["lse"], bias_ref, dqkv_ref)
        refill("qkv", "lse")
        coming["qkv_weight"].wait()
        grad_norm = mm_t(dqkv_ref[...], rows_view(held["qkv_weight"]))
        refill("qkv_weight")
        coming["entry"].wait()
        back = norm_back(grad_norm, held["entry"][...], gain_ref[layer_at, :1])
        grad_entry = grad_ref[...] + back
        refill("entry")
        high, low = halves(grad_entry)
        prompt_ref[layer_at] = mm(onehot_t, high) + mm(onehot_t, low)
        passed = jnp.where(is_prompt, 0.0, grad_entry)
        if layer_at > 0:
            grad_ref[...] = passed
            low_ref[...] = passed.astype(bf16)
        else:
            out_ref[...] = passed


def halves(values):
    high = values.astype(bf16)
    return high, (values - high.astype(f32)).astype(bf16)


def shape(dims, dtype):
    return jax.ShapeDtypeStruct(dims, dtype)


def skipping(body, taken, needed, results):
    def kernel(*refs):
        ends = taken + needed, taken + needed + results
        body(*refs[:taken], *refs[ends[0] : ends[1]], *refs[ends[1] + 1 :])
        refs[ends[1]][...] = jnp.zeros((1, 1), f32)

    return kernel


def run(body, away, near, outputs, outputs_away, scratch, flops, name, needs=(), vmem=FORWARD_VMEM):
    here = pl.BlockSpec(memory_space=pltpu.VMEM)
    anywhere = pl.BlockSpec(memory_space=pl.ANY)
    results = (*outputs, *outputs_away)
    moved = sum(math.prod(a.shape) * a.dtype.itemsize for a in (*away, *near, *results))
    return pl.pallas_call(
        skipping(body, len(away) + len(near), len(needs), len(results)),
        out_shape=(*results, shape((1, 1), f32)),
        in_specs=[anywhere] * len(away) + [here] * len(near) + [anywhere] * len(needs),
        out_specs=[here] * len(outputs) + [anywhere] * len(outputs_away) + [here],
        scratch_shapes=scratch,
        compiler_params=pltpu.CompilerParams(vmem_limit_bytes=vmem),
        cost_estimate=pl.CostEstimate(flops=flops, transcendentals=0, bytes_accessed=moved),
        name=name,
    )(*away, *near, *needs)


def zero_body(*refs):
    refs[-1][...] = jnp.zeros((1, 1), f32)


def zero_after(values):
    return pl.pallas_call(
        zero_body,
        out_shape=shape((1, 1), f32),
        in_specs=[pl.BlockSpec(memory_space=pl.ANY)] * len(values),
        out_specs=pl.BlockSpec(memory_space=pltpu.VMEM),
        compiler_params=pltpu.CompilerParams(vmem_limit_bytes=2**20),
        cost_estimate=pl.CostEstimate(flops=0, transcendentals=0, bytes_accessed=4),
        name="zero_after",
    )(*values)


def piece_sems(pieces):
    count = 1 if pieces[0].ndim == 2 else 32
    return pltpu.SemaphoreType.DMA((count,))


def weight_shape(pieces, width, columns):
    return (width, columns) if pieces[0].ndim == 2 else (4, width // 4, columns)


def attn_forward(pieces, layer_at, slot_total, x, below, riders, marks, gains, needs=()):
    tokens = marks["seg"].shape[1]
    width = gains.shape[2]
    takes_riders, has_down = riders is None, below is not None
    weight = weight_shape(pieces, width, 3 * width)
    near_out = (shape((tokens, width), bf16), shape((LANES, tokens), f32))
    away_out = (
        shape((tokens, width), f32),
        shape((tokens, 3 * width), bf16),
        shape(weight, bf16),
    )
    away = tuple(pieces)
    near = (marks["slot"], marks["base"], marks["seg"], gains)
    scratch = []
    if not takes_riders:
        near += (riders,)
    else:
        rider_shape = (math.prod(axis_sizes()), 8 * width // LANES, LANES)
        away_out += (shape(rider_shape, bf16),)
        scratch.append(pltpu.VMEM(rider_shape, bf16))
    if has_down:
        units = below["active"].shape[1]
        away += (below["middle"], below["active"])
        down = weight_shape(pieces, width, units)
        away_out += (shape(down, bf16),)
        scratch += [
            pltpu.VMEM(down, bf16),
            pltpu.VMEM((tokens, width), f32),
            pltpu.VMEM((tokens, units), bf16),
            piece_sems(pieces),
        ]
    else:
        near = (x, *near)
    scratch += [
        pltpu.VMEM(weight, bf16),
        pltpu.VMEM((tokens, width), bf16),
        pltpu.VMEM((tokens, tokens), f32),
        pltpu.VMEM((tokens, width), f32),
        pltpu.VMEM((tokens, 3 * width), bf16),
        piece_sems(pieces),
        piece_sems(pieces),
        pltpu.SemaphoreType.DMA((5,)),
    ]
    flops = 2 * tokens * width * (7 * width + 2 * tokens)
    body = partial(attn_forward_body, (len(pieces), layer_at, slot_total, takes_riders, has_down))
    found = run(body, away, near, near_out, away_out, scratch, flops, "attn_forward", needs)
    names = ("mixed", "lse", "entry", "qkv", "qkv_weight")
    layer = dict(zip(names, found))
    found = found[5:]
    if takes_riders:
        riders, found = found[0], found[1:]
    if has_down:
        below["down"], found = found[0], found[1:]
    return layer, riders, found[0]


def mlp_up(pieces, layer_at, layer, gains, units, needs=()):
    tokens, width = layer["mixed"].shape
    out_shape, up_shape = (weight_shape(pieces, width, n) for n in (width, units))
    results = {
        "middle": shape((tokens, width), f32),
        "slope": shape((tokens, units), bf16),
        "out": shape(out_shape, bf16),
        "up": shape(up_shape, bf16),
        "active": shape((tokens, units), bf16),
    }
    scratch = [
        pltpu.VMEM(out_shape, bf16),
        pltpu.VMEM(up_shape, bf16),
        pltpu.VMEM((tokens, width), bf16),
        pltpu.VMEM((tokens, width), f32),
        pltpu.VMEM((tokens, units), bf16),
        pltpu.VMEM((tokens, units), bf16),
        piece_sems(pieces),
        piece_sems(pieces),
        pltpu.SemaphoreType.DMA((5,)),
    ]
    flops = 2 * tokens * width * (units + width)
    away = (*pieces, layer["entry"])
    near = (layer["mixed"], gains)
    body = partial(mlp_up_body, len(pieces), layer_at)
    away_out = tuple(results.values())
    found = run(body, away, near, (), away_out, scratch, flops, "mlp_up", needs)
    layer.update(zip(results, found))
    return found[-1]


def backward(down_pieces, kept, cotangent, marks, gains, slot_total):
    layers = len(kept)
    tokens, width = cotangent.shape
    units = kept[0]["slope"].shape[1]
    away = list(down_pieces)
    for layer_at, layer in enumerate(kept):
        names = STATE + (WEIGHTS if layer_at < layers - 1 else WEIGHTS[1:])
        away += [layer[name] for name in names]
    away.append(kept[-1]["active"])
    near = (cotangent, marks["slot"], marks["seg"], gains)
    outputs = (
        shape((tokens, width), f32),
        shape((layers, slot_total, width), f32),
        shape((tokens, width), bf16),
    )
    held = [kept[0][name] for name in STATE + WEIGHTS]
    scratch = [pltpu.VMEM(a.shape, a.dtype) for a in held]
    scratch += [
        pltpu.VMEM((tokens, units), bf16),
        pltpu.VMEM((tokens, width), bf16),
        pltpu.VMEM((tokens, units), bf16),
        pltpu.VMEM((tokens, width), f32),
        pltpu.VMEM((tokens, width), bf16),
        pltpu.VMEM((tokens, 3 * width), bf16),
        pltpu.VMEM((tokens, tokens), f32),
        pltpu.SemaphoreType.DMA((len(held) + 1,)),
        piece_sems(down_pieces),
    ]
    flops = 2 * layers * tokens * width * (4 * width + 3 * units + 5 * tokens)
    body = partial(backward_body, layers, len(down_pieces))
    return run(body, away, near, outputs, (), scratch, flops, "backward", vmem=BACKWARD_VMEM)[:3]


def axis_sizes():
    return tuple(lax.axis_size(axis) for axis in ALL)


def is_block():
    return axis_sizes() == (4, 2, 2, 2)


def flip(value, axis):
    return lax.ppermute(value, axis, [(0, 1), (1, 0)])


def turn(value, core_of_x):
    moves = []
    z_size, x_size, core_size, y_size = axis_sizes()
    for z in range(z_size):
        for x in range(x_size):
            for core in range(core_size):
                for y in range(y_size):
                    at = ((z * x_size + x) * core_size + core) * y_size + y
                    along_x = core == core_of_x
                    to_x, to_y = (1 - x, y) if along_x else (x, 1 - y)
                    moves.append((at, ((z * x_size + to_x) * core_size + core) * y_size + to_y))
    return lax.ppermute(value, ALL, moves)


def swap_z(value, distance):
    return lax.ppermute(value, "z", [(i, i ^ distance) for i in range(lax.axis_size("z"))])


class Steps:
    def __init__(self):
        self.zero = None

    def needs(self):
        return [] if self.zero is None else [self.zero]

    def behind(self, value):
        return value if self.zero is None else value + self.zero[0, 0].astype(value.dtype)

    def join(self, parts):
        return self.behind(jnp.stack(parts))

    def wait(self, arrays):
        self.zero = zero_after([*arrays, *self.needs()])


class Gather:
    def __init__(self, steps, shard):
        self.steps, self.own = steps, shard

    def start_ring(self):
        own = self.steps.behind(self.own)
        self.parts = [own] + [swap_z(own, i) for i in (1, 2, 3)]
        return self.parts[1:]

    def first_turn(self):
        self.parts = [self.steps.join(self.parts)]
        self.parts.append(turn(self.parts[0], 0))
        return self.parts[1:]

    def second_turn(self):
        self.parts = [self.steps.join(self.parts)]
        self.parts.append(turn(self.parts[0], 1))
        return self.parts[1:]

    def last_turn(self):
        whole = self.steps.join(self.parts)
        self.pieces = [whole, flip(whole, "core")]
        return []


def total_over(value):
    if not is_block():
        return lax.psum(value, ALL)
    core = lax.axis_index("core")
    low = value.astype(bf16)
    mine = jnp.where(core == 0, value[0], value[1])
    theirs = jnp.where(core == 0, low[1], low[0])
    total = mine + flip(theirs, "core").astype(f32)
    for axis in ("x", "y"):
        total = total + flip(total.astype(bf16), axis).astype(f32)
    for pairs in ([(0, 1), (1, 0), (2, 3), (3, 2)], [(0, 2), (2, 0), (1, 3), (3, 1)]):
        total = total + lax.ppermute(total.astype(bf16), "z", pairs).astype(f32)
    other = flip(total.astype(bf16), "core").astype(f32)
    return jnp.stack([jnp.where(core == 0, total, other), jnp.where(core == 0, other, total)])


def window_rows(count, width):
    step = math.gcd(count, width)
    return -(-(width - step + count) // width)


def prompt_window(prompts, width):
    count = prompts.shape[0]
    assert window_rows(count, width) <= 4
    shift = lax.axis_index(ALL) * count % width
    flat = lax.dynamic_update_slice(jnp.zeros((4 * width,), f32), prompts, (shift,))
    rows = flat.reshape(4, width // LANES, LANES).transpose(1, 0, 2)
    return jnp.concatenate(halves(rows), axis=1).reshape(-1, LANES)


def window_slots(count, width, layers):
    holders = math.prod(axis_sizes()) // layers
    base = np.arange(holders, dtype=np.int32) * count // width
    both = base[:, None] + np.arange(8, dtype=np.int32)[None, :] % 4
    return jnp.asarray(both.reshape(1, -1), f32)


def gather_any(qkv, out, up, down):
    seq = ("z", "x", "core")
    layers = qkv.shape[0]
    qkvs = [lax.all_gather(qkv[layer_at], seq, tiled=True) for layer_at in range(layers)]
    groups = [[qkvs[0]]]
    for layer_at in range(layers):
        whole_up = lax.all_gather(up[layer_at], "y", axis=1, tiled=True)
        out_up = jnp.concatenate([out[layer_at], whole_up], axis=1)
        groups.append([lax.all_gather(out_up, seq, tiled=True)])
        whole_down = lax.all_gather(down[layer_at].T, "y", axis=1, tiled=True)
        groups.append([lax.all_gather(whole_down, seq, tiled=True)] + qkvs[layer_at + 1 :][:1])
    return groups


def block_groups(qkv_weight, out_weight, up_weight, down_weight, window):
    y_size, y_at = lax.axis_size("y"), lax.axis_index("y")
    layers, rows, qkv_width = qkv_weight.shape
    cut, out_cut = qkv_width // y_size, out_weight.shape[2] // y_size
    qkv = lax.dynamic_slice(qkv_weight, (0, 0, y_at * cut), (layers, rows, cut))
    out = lax.dynamic_slice(out_weight, (0, 0, y_at * out_cut), (layers, rows, out_cut))
    groups = [jnp.concatenate([qkv[0], window], axis=1)]
    for layer_at in range(layers):
        groups.append(jnp.concatenate([out[layer_at], up_weight[layer_at]], axis=1))
        down = down_weight[layer_at].T
        if layer_at < layers - 1:
            down = jnp.concatenate([down, qkv[layer_at + 1]], axis=1)
        groups.append(down)
    return groups


def per_device(
    patches,
    segments,
    prompt_slots,
    norm_gains,
    qkv_weight,
    out_weight,
    up_weight,
    down_weight,
    cotangent,
    prompts,
    first_moment,
    second_moment,
    adam_betas,
    learn_rate,
):
    layers, _, width = norm_gains.shape
    tokens = patches.shape[0]
    units = up_weight.shape[2] * lax.axis_size("y")
    total_prompts = prompts.shape[0] * math.prod(axis_sizes())
    slot_total = total_prompts // (layers * width)
    window = prompt_window(prompts, width)
    marks = {
        "base": window_slots(prompts.shape[0], width, layers),
        "slot": prompt_slots.reshape(1, tokens),
        "seg": segments.reshape(1, tokens),
    }
    kept = []
    pieces = []
    state = {"riders": None}

    def forward_step(at, needs=()):
        layer_at, part = divmod(at, 2)
        if part == 1:
            return mlp_up(pieces[at], layer_at, kept[layer_at], norm_gains, units, needs)
        layer, state["riders"], zero = attn_forward(
            pieces[at],
            layer_at,
            slot_total,
            patches if layer_at == 0 else None,
            kept[layer_at - 1] if layer_at > 0 else None,
            state["riders"],
            marks,
            norm_gains,
            needs,
        )
        kept.append(layer)
        return zero

    block = is_block()
    if block:
        steps = Steps()
        groups = block_groups(qkv_weight, out_weight, up_weight, down_weight, window)
        gathers = [Gather(steps, shard) for shard in groups]

        def kernel(at):
            pieces.append(gathers[at].pieces)
            steps.zero = forward_step(at, steps.needs())

        ring, first, second, last = (
            Gather.start_ring,
            Gather.first_turn,
            Gather.second_turn,
            Gather.last_turn,
        )
        for moves, beside in (
            ([(ring, 0)], None),
            ([(first, 0)], None),
            ([(second, 0), (ring, 1)], None),
            ([(last, 0), (first, 1), (ring, 2)], 0),
            ([(second, 1), (first, 2), (ring, 3)], None),
            ([(last, 1), (second, 2), (first, 3), (ring, 4)], 1),
            ([(last, 2), (second, 3), (first, 4)], 2),
            ([(last, 3), (second, 4)], 3),
            ([(last, 4)], None),
        ):
            coming = [array for move, at in moves for array in move(gathers[at])]
            if beside is not None:
                kernel(beside)
            if coming:
                steps.wait(coming)
        pieces.append(gathers[4].pieces)
    else:
        state["riders"] = lax.all_gather(window, ALL)
        pieces = gather_any(qkv_weight, out_weight, up_weight, down_weight)
        for at in range(2 * layers):
            forward_step(at)

    gradient, layer_grads, block_output = backward(
        pieces[-1], kept, cotangent, marks, norm_gains, slot_total
    )

    prompt_grad = total_over(layer_grads)
    grad_norm = jnp.sqrt(jnp.sum(prompt_grad * prompt_grad))
    clip_limit = clip_ratio * math.sqrt(total_prompts)
    own_grads = lax.dynamic_slice(
        prompt_grad.reshape(-1), (lax.axis_index(ALL) * prompts.shape[0],), prompts.shape
    )
    clipped = own_grads * jnp.minimum(1.0, clip_limit / (grad_norm + 1e-06))
    beta_one = adam_betas[0]
    beta_two = adam_betas[1]
    step_value = float(ADAM_STEP)
    new_first = beta_one * first_moment + (1.0 - beta_one) * clipped
    new_second = beta_two * second_moment + (1.0 - beta_two) * clipped * clipped
    first_hat = new_first / (1.0 - beta_one**step_value)
    second_hat = new_second / (1.0 - beta_two**step_value)
    new_prompts = prompts - learn_rate[0] * (
        first_hat / (jnp.sqrt(second_hat) + adam_eps) + decay_rate * prompts
    )
    return (block_output, gradient, new_prompts, new_first, new_second, grad_norm.reshape(1))


def solution(mesh):
    seq_size, mlp_size = mesh.shape["seq"], mesh.shape["mlp"]
    grid = Mesh(mesh.devices.reshape(seq_size // 4, 2, 2, mlp_size), ALL)
    seq, mlp = ("z", "x", "core"), "y"
    in_specs = (
        P(ALL, None),
        P(ALL),
        P(ALL),
        P(),
        P(None, seq, None),
        P(None, seq, None),
        P(None, seq, mlp),
        P(None, mlp, seq),
        P(ALL, None),
        P(ALL),
        P(ALL),
        P(ALL),
        P(),
        P(),
    )
    out_specs = (P(ALL, None), P(ALL, None), P(ALL), P(ALL), P(ALL), P())
    return jax.shard_map(
        per_device, mesh=grid, in_specs=in_specs, out_specs=out_specs, check_vma=False
    )
```

profile of v0, /device:TPU:1, one launch (start us, length us, event | category | flops | bytes accessed | tf_op | source)
XLA Modules:
  0.0 305.7 jit_solution(16669679339222164142)
XLA Ops:
  2.7 2.2 collective-permute-start
  4.8 2.3 collective-permute-start.1
  9.6 5.5 %collective-permute-done.2.refs_2_ = bf16[48,1280]{1,0:T(8,128)(2,1)S(1)} collective-permute-done((bf16[48,1280]{1,0:T(8,128)(2,1)S(1)}, bf16[48,1280]{1,0:T(8,128)(2,1)S(1)}, u32[]{:S(2)}, u32[]{:S(2)}) %collective-permute-start.2) | collective-permute-done | bytes 122912 | tf_op jit(solution)/shard_map/ppermute | solution.py:627
  17.7 6.7 %collective-permute-done.3.refs_0_ = bf16[4,48,1280]{2,1,0:T(8,128)(2,1)S(1)} collective-permute-done((bf16[4,48,1280]{2,1,0:T(8,128)(2,1)S(1)}, bf16[4,48,1280]{2,1,0:T(8,128)(2,1)S(1)}, u32[]{:S(2)}, u32[]{:S(2)}) %collective-permute-start.3) | collective-permute-done | bytes 491552 | tf_op jit(solution)/shard_map/ppermute | solution.py:623
  28.4 2.6 collective-permute-start.4
  34.3 2.1 collective-permute-done.5.refs_2_
  36.5 6.8 %collective-permute-done.6.refs_3_ = bf16[48,1920]{1,0:T(8,128)(2,1)S(1)} collective-permute-done((bf16[48,1920]{1,0:T(8,128)(2,1)S(1)}, bf16[48,1920]{1,0:T(8,128)(2,1)S(1)}, u32[]{:S(2)}, u32[]{:S(2)}) %collective-permute-start.6) | collective-permute-done | bytes 184352 | tf_op jit(solution)/shard_map/ppermute | solution.py:627
  45.3 5.7 %collective-permute-start.12 = (bf16[2,2,4,48,1280]{4,3,2,1,0:T(8,128)(2,1)S(1)}, bf16[2,2,4,48,1280]{4,3,2,1,0:T(8,128)(2,1)S(1)}, u32[]{:S(2)}, u32[]{:S(2)}) collective-permute-start(bf16[2,2,4,48,1280]{4,3,2,1,0:T(8,128)(2,1)S(1)} %maximum_add_fusion.6.refs_0_), channel_id=1, source_target_pairs={{0,2},{2,0},{1,3},{3,1},{4,6},{6,4},{5,7},{7,5},{8,10},{10,8},{9,1... | collective-permute-start | bytes 5898248 | tf_op jit(solution)/shard_map/ppermute | solution.py:609
  52.6 3.7 %collective-permute-start.10 = (bf16[48,2688]{1,0:T(8,128)(2,1)S(1)}, bf16[48,2688]{1,0:T(8,128)(2,1)S(1)}, u32[]{:S(2)}, u32[]{:S(2)}) collective-permute-start(bf16[48,2688]{1,0:T(8,128)(2,1)S(1)} %maximum_add_fusion.25), channel_id=1, source_target_pairs={{0,16},{8,24},{16,0},{24,8},{1,17},{9,25},{17,1},{25,9},{2,18},{10... | collective-permute-start | bytes 774152 | tf_op jit(solution)/shard_map/ppermute | solution.py:627
  57.2 12.5 %attn_forward.2 = (bf16[512,768]{1,0:T(8,128)(2,1)S(1)}, f32[128,512]{1,0:T(8,128)S(1)}, f32[512,768]{1,0:T(8,128)S(1)}, bf16[512,2304]{1,0:T(8,128)(2,1)S(1)}, ...) custom-call(bf16[2,2,4,48,1280]{4,3,2,1,0:T(8,128)(2,1)S(1)} %maximum_add_fusion.6.refs_0_, ...), custom_call_target="tpu_custom_call" | custom-call | flops 5033164800 | bytes 13648384 | tf_op jit(solution)/shard_map/attn_forward/pallas_call | solution.py:443
  71.6 2.5 collective-permute-done.10.refs_2_
  77.7 5.3 %collective-permute-start.15 = (bf16[48,1920]{1,0:T(8,128)(2,1)S(1)}, bf16[48,1920]{1,0:T(8,128)(2,1)S(1)}, u32[]{:S(2)}, u32[]{:S(2)}) collective-permute-start(bf16[48,1920]{1,0:T(8,128)(2,1)S(1)} %maximum_add_fusion.29), channel_id=1, source_target_pairs={{0,8},{8,0},{16,24},{24,16},{1,9},{9,1},{17,25},{25,17},{2,10},{10... | collective-permute-start | bytes 552968 | tf_op jit(solution)/shard_map/ppermute | solution.py:627
  83.0 2.2 collective-permute-start.17
  85.3 2.1 collective-permute-done.15.refs_2_
  87.4 9.7 %collective-permute-done.16.refs_3_ = bf16[48,1920]{1,0:T(8,128)(2,1)S(1)} collective-permute-done((bf16[48,1920]{1,0:T(8,128)(2,1)S(1)}, bf16[48,1920]{1,0:T(8,128)(2,1)S(1)}, u32[]{:S(2)}, u32[]{:S(2)}) %collective-permute-start.16) | collective-permute-done | bytes 184352 | tf_op jit(solution)/shard_map/ppermute | solution.py:627
  97.1 3.2 %collective-permute-done.14.refs_1_ = bf16[4,48,2688]{2,1,0:T(8,128)(2,1)S(1)} collective-permute-done((bf16[4,48,2688]{2,1,0:T(8,128)(2,1)S(1)}, bf16[4,48,2688]{2,1,0:T(8,128)(2,1)S(1)}, u32[]{:S(2)}, u32[]{:S(2)}) %collective-permute-start.14) | collective-permute-done | bytes 1032224 | tf_op jit(solution)/shard_map/ppermute | solution.py:623
  100.3 6.0 %collective-permute-done.13.refs_0_ = bf16[2,4,48,1920]{3,2,1,0:T(8,128)(2,1)S(1)} collective-permute-done((bf16[2,4,48,1920]{3,2,1,0:T(8,128)(2,1)S(1)}, bf16[2,4,48,1920]{3,2,1,0:T(8,128)(2,1)S(1)}, u32[]{:S(2)}, u32[]{:S(2)}) %collective-permute-start.13) | collective-permute-done | bytes 1474592 | tf_op jit(solution)/shard_map/ppermute | solution.py:623
  111.7 5.1 %collective-permute-start.18 = (bf16[48,1536]{1,0:T(8,128)(2,1)S(1)}, bf16[48,1536]{1,0:T(8,128)(2,1)S(1)}, u32[]{:S(2)}, u32[]{:S(2)}) collective-permute-start(bf16[48,1536]{1,0:T(8,128)(2,1)S(1)} %get-tuple-element.79), channel_id=1, source_target_pairs={{0,8},{8,0},{16,24},{24,16},{1,9},{9,1},{17,25},{25,17},{2,10},{10... | collective-permute-start | bytes 442376 | tf_op jit(solution)/shard_map/ppermute | solution.py:627
  117.1 2.2 collective-permute-start.20
  119.3 14.8 %mlp_up.2 = (f32[512,768]{1,0:T(8,128)S(1)}, bf16[512,3072]{1,0:T(8,128)(2,1)S(1)}, bf16[4,192,768]{2,1,0:T(8,128)(2,1)S(1)}, bf16[4,192,3072]{2,1,0:T(8,128)(2,...) custom-call(bf16[2,2,4,48,1920]{4,3,2,1,0:T(8,128)(2,1)S(1)} %maximum_add_fusion.1.refs_0_, ...), custom_call_target="tpu_custom_call" | custom-call | flops 3019898880 | bytes 22032384 | tf_op jit(solution)/shard_map/mlp_up/pallas_call | solution.py:443
  135.2 7.3 %collective-permute-done.21.refs_0_ = bf16[2,4,48,2688]{3,2,1,0:T(8,128)(2,1)S(1)} collective-permute-done((bf16[2,4,48,2688]{3,2,1,0:T(8,128)(2,1)S(1)}, bf16[2,4,48,2688]{3,2,1,0:T(8,128)(2,1)S(1)}, u32[]{:S(2)}, u32[]{:S(2)}) %collective-permute-start.21) | collective-permute-done | bytes 2064416 | tf_op jit(solution)/shard_map/ppermute | solution.py:623
  148.1 4.4 %collective-permute-done.26.refs_1_ = bf16[2,2,4,48,2688]{4,3,2,1,0:T(8,128)(2,1)S(1)} collective-permute-done((bf16[2,2,4,48,2688]{4,3,2,1,0:T(8,128)(2,1)S(1)}, bf16[2,2,4,48,2688]{4,3,2,1,0:T(8,128)(2,1)S(1)}, u32[]{:S(2)}, u32[]{:S(2)}) %collective-permute-start.26) | collective-permute-done | bytes 4128800 | tf_op jit(solution)/shard_map/ppermute | solution.py:609
  152.5 16.6 %attn_forward.3 = (bf16[512,768]{1,0:T(8,128)(2,1)S(1)}, f32[128,512]{1,0:T(8,128)S(1)}, f32[512,768]{1,0:T(8,128)S(1)}, bf16[512,2304]{1,0:T(8,128)(2,1)S(1)}, ...) custom-call(bf16[2,2,4,48,2688]{4,3,2,1,0:T(8,128)(2,1)S(1)} %maximum_add_fusion.refs_0_, ...), custom_call_target="tpu_custom_call" | custom-call | flops 5033164800 | bytes 26624512 | tf_op jit(solution)/shard_map/attn_forward/pallas_call | solution.py:443
  176.1 3.1 %collective-permute-done.28.refs_1_ = bf16[2,2,4,48,1920]{4,3,2,1,0:T(8,128)(2,1)S(1)} collective-permute-done((bf16[2,2,4,48,1920]{4,3,2,1,0:T(8,128)(2,1)S(1)}, bf16[2,2,4,48,1920]{4,3,2,1,0:T(8,128)(2,1)S(1)}, u32[]{:S(2)}, u32[]{:S(2)}) %collective-permute-start.28) | collective-permute-done | bytes 2949152 | tf_op jit(solution)/shard_map/ppermute | solution.py:609
  179.2 15.2 %mlp_up.3 = (f32[512,768]{1,0:T(8,128)S(1)}, bf16[512,3072]{1,0:T(8,128)(2,1)S(1)}, bf16[4,192,768]{2,1,0:T(8,128)(2,1)S(1)}, bf16[4,192,3072]{2,1,0:T(8,128)(2,...) custom-call(bf16[2,2,4,48,1920]{4,3,2,1,0:T(8,128)(2,1)S(1)} %maximum_add_fusion.2.refs_0_, ...), custom_call_target="tpu_custom_call" | custom-call | flops 3019898880 | bytes 22032384 | tf_op jit(solution)/shard_map/mlp_up/pallas_call | solution.py:443
  203.2 4.4 %collective-permute-done.29.refs_1_ = bf16[2,2,4,48,1536]{4,3,2,1,0:T(8,128)(2,1)S(1)} collective-permute-done((bf16[2,2,4,48,1536]{4,3,2,1,0:T(8,128)(2,1)}, bf16[2,2,4,48,1536]{4,3,2,1,0:T(8,128)(2,1)S(1)}, u32[]{:S(2)}, u32[]{:S(2)}) %collective-permute-start.29) | collective-permute-done | bytes 2359328 | tf_op jit(solution)/shard_map/ppermute | solution.py:609
  209.0 59.8 %backward.1 = (f32[512,768]{1,0:T(8,128)}, f32[2,50,768]{2,1,0:T(8,128)}, bf16[512,768]{1,0:T(8,128)(2,1)}, f32[1,1]{1,0:T(1,128)}) custom-call(bf16[2,2,4,48,1536]{4,3,2,1,0:T(8,128)(2,1)} %maximum_add_fusion.3.refs_0_, bf16[2,2,4,48,1536]{4,3,2,1,0:T(8,128)(2,1)} %copy-done.33, bf16[512,3072]{1,0:T(8,128)(2,1)} %copy-done.7, f32[512,768]{1,0:T(8,128)} %copy-done.13, ...), custom_call_target="tpu_custom_call" | custom-call | flops 23353884672 | bytes 52752384 | tf_op jit(solution)/shard_map/backward/pallas_call | solution.py:443
  273.8 2.3 collective-permute-done.31
  276.3 3.3 %collective-permute-done.32 = bf16[50,768]{1,0:T(8,128)(2,1)S(1)} collective-permute-done((bf16[50,768]{1,0:T(8,128)(2,1)S(1)}, bf16[50,768]{1,0:T(8,128)(2,1)S(1)}, u32[]{:S(2)}, u32[]{:S(2)}) %collective-permute-start.32) | collective-permute-done | bytes 76832 | tf_op jit(solution)/shard_map/ppermute | solution.py:609
  279.6 5.3 %collective-permute-start.33 = (bf16[50,768]{1,0:T(8,128)(2,1)S(1)}, bf16[50,768]{1,0:T(8,128)(2,1)S(1)}, u32[]{:S(2)}, u32[]{:S(2)}) collective-permute-start(bf16[50,768]{1,0:T(8,128)(2,1)S(1)} %fusion.10), channel_id=1, source_target_pairs={{0,8},{8,0},{16,24},{24,16},{1,9},{9,1},{17,25},{25,17},{2,10},{10... | collective-permute-start | bytes 230408 | tf_op jit(solution)/shard_map/ppermute | solution.py:683
  287.9 3.3 %collective-permute-done.34 = bf16[50,768]{1,0:T(8,128)(2,1)S(1)} collective-permute-done((bf16[50,768]{1,0:T(8,128)(2,1)S(1)}, bf16[50,768]{1,0:T(8,128)(2,1)S(1)}, u32[]{:S(2)}, u32[]{:S(2)}) %collective-permute-start.34) | collective-permute-done | bytes 76832 | tf_op jit(solution)/shard_map/ppermute | solution.py:683
  291.2 4.7 %collective-permute-start.35 = (bf16[50,768]{1,0:T(8,128)(2,1)S(1)}, bf16[50,768]{1,0:T(8,128)(2,1)S(1)}, u32[]{:S(2)}, u32[]{:S(2)}) collective-permute-start(bf16[50,768]{1,0:T(8,128)(2,1)S(1)} %get-tuple-element.67), channel_id=1, source_target_pairs={{0,2},{2,0},{1,3},{3,1},{4,6},{6,4},{5,7},{7,5},{8,10},{10,8},{9,1... | collective-permute-start | bytes 230408 | tf_op jit(solution)/shard_map/ppermute | solution.py:609
  (181 shorter events, 59.6 us)
Async XLA Ops:
  2.7 5.2 %collective-permute-start = (bf16[48,1280]{1,0:T(8,128)(2,1)S(1)}, bf16[48,1280]{1,0:T(8,128)(2,1)S(1)}, u32[]{:S(2)}, u32[]{:S(2)}) collective-permute-start(bf16[48,1280]{1,0:T(8,128)(2,1)S(1)} %get-tuple-element.92), channel_id=1, source_target_pairs={{0,8},{8,0},{16,24},{24,16},{1,9},{9,1},{17,25},{25,17},{2,10},{10... | collective-permute-start | bytes 368648 | tf_op jit(solution)/shard_map/ppermute | solution.py:627
  4.8 4.7 %collective-permute-start.1 = (bf16[48,1280]{1,0:T(8,128)(2,1)S(1)}, bf16[48,1280]{1,0:T(8,128)(2,1)S(1)}, u32[]{:S(2)}, u32[]{:S(2)}) collective-permute-start(bf16[48,1280]{1,0:T(8,128)(2,1)S(1)} %get-tuple-element.92), channel_id=1, source_target_pairs={{0,16},{8,24},{16,0},{24,8},{1,17},{9,25},{17,1},{25,9},{2,18},{10... | collective-permute-start | bytes 368648 | tf_op jit(solution)/shard_map/ppermute | solution.py:627
  7.2 7.9 %collective-permute-start.2 = (bf16[48,1280]{1,0:T(8,128)(2,1)S(1)}, bf16[48,1280]{1,0:T(8,128)(2,1)S(1)}, u32[]{:S(2)}, u32[]{:S(2)}) collective-permute-start(bf16[48,1280]{1,0:T(8,128)(2,1)S(1)} %get-tuple-element.92), channel_id=1, source_target_pairs={{0,24},{8,16},{16,8},{24,0},{1,25},{9,17},{17,9},{25,1},{2,26},{10... | collective-permute-start | bytes 368648 | tf_op jit(solution)/shard_map/ppermute | solution.py:627
  16.3 8.0 %collective-permute-start.3 = (bf16[4,48,1280]{2,1,0:T(8,128)(2,1)S(1)}, bf16[4,48,1280]{2,1,0:T(8,128)(2,1)S(1)}, u32[]{:S(2)}, u32[]{:S(2)}) collective-permute-start(bf16[4,48,1280]{2,1,0:T(8,128)(2,1)S(1)} %maximum_add_fusion.23), channel_id=1, source_target_pairs={{0,4},{1,5},{2,3},{3,2},{4,0},{5,1},{6,7},{7,6},{8,12},{9,13},{10,... | collective-permute-start | bytes 1474568 | tf_op jit(solution)/shard_map/ppermute | solution.py:623
  26.3 17.0 %collective-permute-start.7 = (bf16[2,4,48,1280]{3,2,1,0:T(8,128)(2,1)S(1)}, bf16[2,4,48,1280]{3,2,1,0:T(8,128)(2,1)S(1)}, u32[]{:S(2)}, u32[]{:S(2)}) collective-permute-start(bf16[2,4,48,1280]{3,2,1,0:T(8,128)(2,1)S(1)} %maximum_add_fusion.15), channel_id=1, source_target_pairs={{0,1},{1,0},{2,6},{3,7},{4,5},{5,4},{6,2},{7,3},{8,9},{9,8},{10,14... | collective-permute-start | bytes 2949128 | tf_op jit(solution)/shard_map/ppermute | solution.py:623
  28.4 5.9 %collective-permute-start.4 = (bf16[48,1920]{1,0:T(8,128)(2,1)S(1)}, bf16[48,1920]{1,0:T(8,128)(2,1)S(1)}, u32[]{:S(2)}, u32[]{:S(2)}) collective-permute-start(bf16[48,1920]{1,0:T(8,128)(2,1)S(1)} %maximum_add_fusion.28), channel_id=1, source_target_pairs={{0,8},{8,0},{16,24},{24,16},{1,9},{9,1},{17,25},{25,17},{2,10},{10... | collective-permute-start | bytes 552968 | tf_op jit(solution)/shard_map/ppermute | solution.py:627
  31.1 5.4 %collective-permute-start.5 = (bf16[48,1920]{1,0:T(8,128)(2,1)S(1)}, bf16[48,1920]{1,0:T(8,128)(2,1)S(1)}, u32[]{:S(2)}, u32[]{:S(2)}) collective-permute-start(bf16[48,1920]{1,0:T(8,128)(2,1)S(1)} %maximum_add_fusion.28), channel_id=1, source_target_pairs={{0,16},{8,24},{16,0},{24,8},{1,17},{9,25},{17,1},{25,9},{2,18},{10... | collective-permute-start | bytes 552968 | tf_op jit(solution)/shard_map/ppermute | solution.py:627
  32.6 10.7 %collective-permute-start.6 = (bf16[48,1920]{1,0:T(8,128)(2,1)S(1)}, bf16[48,1920]{1,0:T(8,128)(2,1)S(1)}, u32[]{:S(2)}, u32[]{:S(2)}) collective-permute-start(bf16[48,1920]{1,0:T(8,128)(2,1)S(1)} %maximum_add_fusion.28), channel_id=1, source_target_pairs={{0,24},{8,16},{16,8},{24,0},{1,25},{9,17},{17,9},{25,1},{2,26},{10... | collective-permute-start | bytes 552968 | tf_op jit(solution)/shard_map/ppermute | solution.py:627
  45.3 11.9 %collective-permute-start.12 = (bf16[2,2,4,48,1280]{4,3,2,1,0:T(8,128)(2,1)S(1)}, bf16[2,2,4,48,1280]{4,3,2,1,0:T(8,128)(2,1)S(1)}, u32[]{:S(2)}, u32[]{:S(2)}) collective-permute-start(bf16[2,2,4,48,1280]{4,3,2,1,0:T(8,128)(2,1)S(1)} %maximum_add_fusion.6.refs_0_), channel_id=1, source_target_pairs={{0,2},{2,0},{1,3},{3,1},{4,6},{6,4},{5,7},{7,5},{8,10},{10,8},{9,1... | collective-permute-start | bytes 5898248 | tf_op jit(solution)/shard_map/ppermute | solution.py:609
  51.3 23.3 %collective-permute-start.8 = (bf16[4,48,1920]{2,1,0:T(8,128)(2,1)S(1)}, bf16[4,48,1920]{2,1,0:T(8,128)(2,1)S(1)}, u32[]{:S(2)}, u32[]{:S(2)}) collective-permute-start(bf16[4,48,1920]{2,1,0:T(8,128)(2,1)S(1)} %maximum_add_fusion.18), channel_id=1, source_target_pairs={{0,4},{1,5},{2,3},{3,2},{4,0},{5,1},{6,7},{7,6},{8,12},{9,13},{10,... | collective-permute-start | bytes 2211848 | tf_op jit(solution)/shard_map/ppermute | solution.py:623
  52.6 21.4 %collective-permute-start.10 = (bf16[48,2688]{1,0:T(8,128)(2,1)S(1)}, bf16[48,2688]{1,0:T(8,128)(2,1)S(1)}, u32[]{:S(2)}, u32[]{:S(2)}) collective-permute-start(bf16[48,2688]{1,0:T(8,128)(2,1)S(1)} %maximum_add_fusion.25), channel_id=1, source_target_pairs={{0,16},{8,24},{16,0},{24,8},{1,17},{9,25},{17,1},{25,9},{2,18},{10... | collective-permute-start | bytes 774152 | tf_op jit(solution)/shard_map/ppermute | solution.py:627
  56.4 17.7 %collective-permute-start.11 = (bf16[48,2688]{1,0:T(8,128)(2,1)S(1)}, bf16[48,2688]{1,0:T(8,128)(2,1)S(1)}, u32[]{:S(2)}, u32[]{:S(2)}) collective-permute-start(bf16[48,2688]{1,0:T(8,128)(2,1)S(1)} %maximum_add_fusion.25), channel_id=1, source_target_pairs={{0,24},{8,16},{16,8},{24,0},{1,25},{9,17},{17,9},{25,1},{2,26},{10... | collective-permute-start | bytes 774152 | tf_op jit(solution)/shard_map/ppermute | solution.py:627
  57.0 17.6 %collective-permute-start.9 = (bf16[48,2688]{1,0:T(8,128)(2,1)S(1)}, bf16[48,2688]{1,0:T(8,128)(2,1)S(1)}, u32[]{:S(2)}, u32[]{:S(2)}) collective-permute-start(bf16[48,2688]{1,0:T(8,128)(2,1)S(1)} %maximum_add_fusion.25), channel_id=1, source_target_pairs={{0,8},{8,0},{16,24},{24,16},{1,9},{9,1},{17,25},{25,17},{2,10},{10... | collective-permute-start | bytes 774152 | tf_op jit(solution)/shard_map/ppermute | solution.py:627
  76.6 29.6 %collective-permute-start.13 = (bf16[2,4,48,1920]{3,2,1,0:T(8,128)(2,1)S(1)}, bf16[2,4,48,1920]{3,2,1,0:T(8,128)(2,1)S(1)}, u32[]{:S(2)}, u32[]{:S(2)}) collective-permute-start(bf16[2,4,48,1920]{3,2,1,0:T(8,128)(2,1)S(1)} %maximum_add_fusion.7), channel_id=1, source_target_pairs={{0,1},{1,0},{2,6},{3,7},{4,5},{5,4},{6,2},{7,3},{8,9},{9,8},{10,14... | collective-permute-start | bytes 4423688 | tf_op jit(solution)/shard_map/ppermute | solution.py:623
  77.0 23.3 %collective-permute-start.14 = (bf16[4,48,2688]{2,1,0:T(8,128)(2,1)S(1)}, bf16[4,48,2688]{2,1,0:T(8,128)(2,1)S(1)}, u32[]{:S(2)}, u32[]{:S(2)}) collective-permute-start(bf16[4,48,2688]{2,1,0:T(8,128)(2,1)S(1)} %maximum_add_fusion.13), channel_id=1, source_target_pairs={{0,4},{1,5},{2,3},{3,2},{4,0},{5,1},{6,7},{7,6},{8,12},{9,13},{10,... | collective-permute-start | bytes 3096584 | tf_op jit(solution)/shard_map/ppermute | solution.py:623
  77.7 9.8 %collective-permute-start.15 = (bf16[48,1920]{1,0:T(8,128)(2,1)S(1)}, bf16[48,1920]{1,0:T(8,128)(2,1)S(1)}, u32[]{:S(2)}, u32[]{:S(2)}) collective-permute-start(bf16[48,1920]{1,0:T(8,128)(2,1)S(1)} %maximum_add_fusion.29), channel_id=1, source_target_pairs={{0,8},{8,0},{16,24},{24,16},{1,9},{9,1},{17,25},{25,17},{2,10},{10... | collective-permute-start | bytes 552968 | tf_op jit(solution)/shard_map/ppermute | solution.py:627
  83.0 14.1 %collective-permute-start.16 = (bf16[48,1920]{1,0:T(8,128)(2,1)S(1)}, bf16[48,1920]{1,0:T(8,128)(2,1)S(1)}, u32[]{:S(2)}, u32[]{:S(2)}) collective-permute-start(bf16[48,1920]{1,0:T(8,128)(2,1)S(1)} %maximum_add_fusion.29), channel_id=1, source_target_pairs={{0,16},{8,24},{16,0},{24,8},{1,17},{9,25},{17,1},{25,9},{2,18},{10... | collective-permute-start | bytes 552968 | tf_op jit(solution)/shard_map/ppermute | solution.py:627
  83.0 14.1 %collective-permute-start.17 = (bf16[48,1920]{1,0:T(8,128)(2,1)S(1)}, bf16[48,1920]{1,0:T(8,128)(2,1)S(1)}, u32[]{:S(2)}, u32[]{:S(2)}) collective-permute-start(bf16[48,1920]{1,0:T(8,128)(2,1)S(1)} %maximum_add_fusion.29), channel_id=1, source_target_pairs={{0,24},{8,16},{16,8},{24,0},{1,25},{9,17},{17,9},{25,1},{2,26},{10... | collective-permute-start | bytes 552968 | tf_op jit(solution)/shard_map/ppermute | solution.py:627
  108.4 8.6 %collective-permute-start.23 = (bf16[2,2,4,48,1920]{4,3,2,1,0:T(8,128)(2,1)S(1)}, bf16[2,2,4,48,1920]{4,3,2,1,0:T(8,128)(2,1)S(1)}, u32[]{:S(2)}, u32[]{:S(2)}) collective-permute-start(bf16[2,2,4,48,1920]{4,3,2,1,0:T(8,128)(2,1)S(1)} %maximum_add_fusion.1.refs_0_), channel_id=1, source_target_pairs={{0,2},{2,0},{1,3},{3,1},{4,6},{6,4},{5,7},{7,5},{8,10},{10,8},{9,1... | collective-permute-start | bytes 8847368 | tf_op jit(solution)/shard_map/ppermute | solution.py:609
  109.7 32.8 %collective-permute-start.21 = (bf16[2,4,48,2688]{3,2,1,0:T(8,128)(2,1)S(1)}, bf16[2,4,48,2688]{3,2,1,0:T(8,128)(2,1)S(1)}, u32[]{:S(2)}, u32[]{:S(2)}) collective-permute-start(bf16[2,4,48,2688]{3,2,1,0:T(8,128)(2,1)S(1)} %maximum_add_fusion.4), channel_id=1, source_target_pairs={{0,1},{1,0},{2,6},{3,7},{4,5},{5,4},{6,2},{7,3},{8,9},{9,8},{10,14... | collective-permute-start | bytes 6193160 | tf_op jit(solution)/shard_map/ppermute | solution.py:623
  111.6 23.6 %collective-permute-start.22 = (bf16[4,48,1920]{2,1,0:T(8,128)(2,1)S(1)}, bf16[4,48,1920]{2,1,0:T(8,128)(2,1)S(1)}, u32[]{:S(2)}, u32[]{:S(2)}) collective-permute-start(bf16[4,48,1920]{2,1,0:T(8,128)(2,1)S(1)} %maximum_add_fusion.19), channel_id=1, source_target_pairs={{0,4},{1,5},{2,3},{3,2},{4,0},{5,1},{6,7},{7,6},{8,12},{9,13},{10,... | collective-permute-start | bytes 2211848 | tf_op jit(solution)/shard_map/ppermute | solution.py:623
  111.7 23.5 %collective-permute-start.18 = (bf16[48,1536]{1,0:T(8,128)(2,1)S(1)}, bf16[48,1536]{1,0:T(8,128)(2,1)S(1)}, u32[]{:S(2)}, u32[]{:S(2)}) collective-permute-start(bf16[48,1536]{1,0:T(8,128)(2,1)S(1)} %get-tuple-element.79), channel_id=1, source_target_pairs={{0,8},{8,0},{16,24},{24,16},{1,9},{9,1},{17,25},{25,17},{2,10},{10... | collective-permute-start | bytes 442376 | tf_op jit(solution)/shard_map/ppermute | solution.py:627
  116.8 18.4 %collective-permute-start.19 = (bf16[48,1536]{1,0:T(8,128)(2,1)S(1)}, bf16[48,1536]{1,0:T(8,128)(2,1)S(1)}, u32[]{:S(2)}, u32[]{:S(2)}) collective-permute-start(bf16[48,1536]{1,0:T(8,128)(2,1)S(1)} %get-tuple-element.79), channel_id=1, source_target_pairs={{0,16},{8,24},{16,0},{24,8},{1,17},{9,25},{17,1},{25,9},{2,18},{10... | collective-permute-start | bytes 442376 | tf_op jit(solution)/shard_map/ppermute | solution.py:627
  117.1 18.1 %collective-permute-start.20 = (bf16[48,1536]{1,0:T(8,128)(2,1)S(1)}, bf16[48,1536]{1,0:T(8,128)(2,1)S(1)}, u32[]{:S(2)}, u32[]{:S(2)}) collective-permute-start(bf16[48,1536]{1,0:T(8,128)(2,1)S(1)} %get-tuple-element.79), channel_id=1, source_target_pairs={{0,24},{8,16},{16,8},{24,0},{1,25},{9,17},{17,9},{25,1},{2,26},{10... | collective-permute-start | bytes 442376 | tf_op jit(solution)/shard_map/ppermute | solution.py:627
  144.8 7.6 %collective-permute-start.26 = (bf16[2,2,4,48,2688]{4,3,2,1,0:T(8,128)(2,1)S(1)}, bf16[2,2,4,48,2688]{4,3,2,1,0:T(8,128)(2,1)S(1)}, u32[]{:S(2)}, u32[]{:S(2)}) collective-permute-start(bf16[2,2,4,48,2688]{4,3,2,1,0:T(8,128)(2,1)S(1)} %maximum_add_fusion.refs_0_), channel_id=1, source_target_pairs={{0,2},{2,0},{1,3},{3,1},{4,6},{6,4},{5,7},{7,5},{8,10},{10,8},{9,1... | collective-permute-start | bytes 12386312 | tf_op jit(solution)/shard_map/ppermute | solution.py:609
  146.1 24.9 %collective-permute-start.25 = (bf16[2,4,48,1920]{3,2,1,0:T(8,128)(2,1)S(1)}, bf16[2,4,48,1920]{3,2,1,0:T(8,128)(2,1)S(1)}, u32[]{:S(2)}, u32[]{:S(2)}) collective-permute-start(bf16[2,4,48,1920]{3,2,1,0:T(8,128)(2,1)S(1)} %maximum_add_fusion.9), channel_id=1, source_target_pairs={{0,1},{1,0},{2,6},{3,7},{4,5},{5,4},{6,2},{7,3},{8,9},{9,8},{10,14... | collective-permute-start | bytes 4423688 | tf_op jit(solution)/shard_map/ppermute | solution.py:623
  147.8 22.0 %collective-permute-start.24 = (bf16[4,48,1536]{2,1,0:T(8,128)(2,1)S(1)}, bf16[4,48,1536]{2,1,0:T(8,128)(2,1)S(1)}, u32[]{:S(2)}, u32[]{:S(2)}) collective-permute-start(bf16[4,48,1536]{2,1,0:T(8,128)(2,1)S(1)} %maximum_add_fusion.22), channel_id=1, source_target_pairs={{0,4},{1,5},{2,3},{3,2},{4,0},{5,1},{6,7},{7,6},{8,12},{9,13},{10,... | collective-permute-start | bytes 1769480 | tf_op jit(solution)/shard_map/ppermute | solution.py:623
  173.8 5.4 %collective-permute-start.28 = (bf16[2,2,4,48,1920]{4,3,2,1,0:T(8,128)(2,1)S(1)}, bf16[2,2,4,48,1920]{4,3,2,1,0:T(8,128)(2,1)S(1)}, u32[]{:S(2)}, u32[]{:S(2)}) collective-permute-start(bf16[2,2,4,48,1920]{4,3,2,1,0:T(8,128)(2,1)S(1)} %maximum_add_fusion.2.refs_0_), channel_id=1, source_target_pairs={{0,2},{2,0},{1,3},{3,1},{4,6},{6,4},{5,7},{7,5},{8,10},{10,8},{9,1... | collective-permute-start | bytes 8847368 | tf_op jit(solution)/shard_map/ppermute | solution.py:609
  174.4 24.5 %collective-permute-start.27 = (bf16[2,4,48,1536]{3,2,1,0:T(8,128)(2,1)S(1)}, bf16[2,4,48,1536]{3,2,1,0:T(8,128)(2,1)S(1)}, u32[]{:S(2)}, u32[]{:S(2)}) collective-permute-start(bf16[2,4,48,1536]{3,2,1,0:T(8,128)(2,1)S(1)} %maximum_add_fusion.12), channel_id=1, source_target_pairs={{0,1},{1,0},{2,6},{3,7},{4,5},{5,4},{6,2},{7,3},{8,9},{9,8},{10,14... | collective-permute-start | bytes 3538952 | tf_op jit(solution)/shard_map/ppermute | solution.py:623
  202.9 4.8 %collective-permute-start.29 = (bf16[2,2,4,48,1536]{4,3,2,1,0:T(8,128)(2,1)}, bf16[2,2,4,48,1536]{4,3,2,1,0:T(8,128)(2,1)S(1)}, u32[]{:S(2)}, u32[]{:S(2)}) collective-permute-start(bf16[2,2,4,48,1536]{4,3,2,1,0:T(8,128)(2,1)} %maximum_add_fusion.3.refs_0_), channel_id=1, source_target_pairs={{0,2},{2,0},{1,3},{3,1},{4,6},{6,4},{5,7},{7,5},{8,10},{10,8},{9,1... | collective-permute-start | bytes 7077896 | tf_op jit(solution)/shard_map/ppermute | solution.py:609
  279.6 7.2 %collective-permute-start.33 = (bf16[50,768]{1,0:T(8,128)(2,1)S(1)}, bf16[50,768]{1,0:T(8,128)(2,1)S(1)}, u32[]{:S(2)}, u32[]{:S(2)}) collective-permute-start(bf16[50,768]{1,0:T(8,128)(2,1)S(1)} %fusion.10), channel_id=1, source_target_pairs={{0,8},{8,0},{16,24},{24,16},{1,9},{9,1},{17,25},{25,17},{2,10},{10... | collective-permute-start | bytes 230408 | tf_op jit(solution)/shard_map/ppermute | solution.py:683
  291.2 9.7 %collective-permute-start.35 = (bf16[50,768]{1,0:T(8,128)(2,1)S(1)}, bf16[50,768]{1,0:T(8,128)(2,1)S(1)}, u32[]{:S(2)}, u32[]{:S(2)}) collective-permute-start(bf16[50,768]{1,0:T(8,128)(2,1)S(1)} %get-tuple-element.67), channel_id=1, source_target_pairs={{0,2},{2,0},{1,3},{3,1},{4,6},{6,4},{5,7},{7,5},{8,10},{10,8},{9,1... | collective-permute-start | bytes 230408 | tf_op jit(solution)/shard_map/ppermute | solution.py:609
  (38 other events, 323.6 us)
where the time goes:
time: 311 us; the launch traced here: 306 us
  Pallas kernels  129 us (41%)
  waiting for transfers between devices  80.1 us (26%)
  starting transfers between devices  59.1 us (19%)
  local copies, waits for them, and re-layouts  13.2 us (4%)
  between operations  13 us (4%)
  other arithmetic  11.6 us (4%)
    pallas_call x5, Pallas kernels, run(): pl.pallas_call(skipping(body, len(away) + len(near), len(needs), len(resu...  119 us
    ppermute x15, waiting for transfers between devices, swap_z(): lax.ppermute(value, 'z', [(i, i ^ distance) for i in range(lax.axis_size(...  32.2 us
    ppermute x15, starting transfers between devices, swap_z(): lax.ppermute(value, 'z', [(i, i ^ distance) for i in range(lax.axis_size(...  29 us
    ppermute x10, waiting for transfers between devices, turn(): return lax.ppermute(value, ALL, moves)  24.3 us
    ppermute x9, waiting for transfers between devices, flip(): return lax.ppermute(value, axis, [(0, 1), (1, 0)])  18.4 us
    ppermute x9, starting transfers between devices, flip(): return lax.ppermute(value, axis, [(0, 1), (1, 0)])  15 us
    unnamed x68, local copies, waits for them, and re-layouts  9.9 us
    pallas_call x8, Pallas kernels, zero_after(): pl.pallas_call(zero_body, out_shape=shape((1, 1), f32), in_specs=[pl.Bloc...  9.63 us
  transfers between devices with their start and end apart: 36, of which 23 were waited for; matrix products, arithmetic and copies ran while one was open for 2% of the time, Pallas kernels for 19%

commit v1 on v0

--- a/solution.py
+++ b/solution.py
@@ -25,7 +25,7 @@
 LANES = 128
 TILE = 256
 FORWARD_VMEM = 30 * 2**20
-BACKWARD_VMEM = 56 * 2**20
+BACKWARD_VMEM = 41 * 2**20
 
 TAIL_SLOPE = 0.275
 TAIL_POLY = (
@@ -91,7 +91,7 @@
             copy.wait()
 
 
-def shards(refs):
+def shards(refs, late):
     z, x, core, y = (lax.axis_index(axis) for axis in ALL)
     found = []
     for i, ref in enumerate(refs):
@@ -99,18 +99,20 @@
         for step in range(4):
             to_x, to_y = ((x, y), (x ^ 1 ^ c, y ^ c), (x ^ c, y ^ 1 ^ c), (x ^ 1, y ^ 1))[step]
             for back in range(4):
-                found.append((ref.at[step // 2, step % 2, back], (z ^ back, to_x, c, to_y)))
+                at = (step // 2, step % 2)
+                at = (back, *at) if late else (*at, back)
+                found.append((ref.at[at], (z ^ back, to_x, c, to_y)))
     return found
 
 
-def weight_copies(refs, column, width, dest, sems):
+def weight_copies(refs, column, width, dest, sems, late=False):
     if refs[0].ndim == 2:
         y_size = dest.shape[-1] // width
         columns = pl.ds(column * y_size, dest.shape[-1])
         return Copies([(refs[0].at[:, columns], dest)], sems)
     rows = refs[0].shape[-2]
     pairs = []
-    for ref, (z, x, core, y) in shards(refs):
+    for ref, (z, x, core, y) in shards(refs, late):
         to_rows = pl.ds(pl.multiple_of((x * 2 + core) * rows, 16), rows)
         to_columns = pl.ds(pl.multiple_of(y * width, LANES), width)
         pairs.append((ref.at[:, pl.ds(column, width)], dest.at[z, to_rows, to_columns]))
@@ -119,7 +121,7 @@
 
 def rider_copies(refs, column, dest, sems):
     pairs = []
-    for ref, (z, x, core, y) in shards(refs):
+    for ref, (z, x, core, y) in shards(refs, False):
         source = ref.at[:, pl.ds(column, LANES)]
         pairs.append((source, dest.at[((z * 2 + x) * 2 + core) * 2 + y]))
     return Copies(pairs, sems)
@@ -279,65 +281,81 @@
         copy.wait()
 
 
-def mlp_up_body(count, layer_at, *refs):
+def mlp_up_body(layer_at, top, *refs):
+    count = 1 if refs[0].ndim == 2 else 2
     pieces, refs = refs[:count], refs[count:]
     entry_in, mixed_ref, gain_ref = refs[:3]
-    middle_out, slope_out, out_out, up_out, active_out = refs[3:8]
-    w_out, w_up, norm_ref, middle_ref, active_ref, slope_ref, sem_a, sem_b, sem_d = refs[8:]
+    refs = refs[3:]
+    if top:
+        (middle_ref, slope_ref, active_ref), refs = refs[:3], refs[3:]
+        w_out, w_up, norm_ref, sem_a, sem_b, sem_d = refs
+    else:
+        middle_out, slope_out, out_out, up_out, active_out = refs[:5]
+        w_out, w_up, norm_ref, sem_a, sem_b, sem_d, middle_ref, slope_ref, active_ref = refs[5:]
     units = slope_ref.shape[1]
     width = middle_ref.shape[1]
-    parts = 1 if pieces[0].ndim == 2 else 2
     load_entry = copy_out(entry_in, middle_ref, sem_d.at[0])
-    load_out = weight_copies(pieces, 0, width // parts, w_out, sem_a).start()
-    load_up = weight_copies(pieces, width // parts, units // parts, w_up, sem_b).start()
+    load_out = weight_copies(pieces, 0, width // count, w_out, sem_a).start()
+    load_up = weight_copies(pieces, width // count, units // count, w_up, sem_b).start()
     load_entry.wait()
     load_out.wait()
     middle_ref[...] = middle_ref[...] + mm(mixed_ref[...], rows_view(w_out))
-    copies = [copy_out(middle_ref, middle_out, sem_d.at[0])]
-    copies.append(copy_out(w_out, out_out, sem_d.at[1]))
+    copies = []
+    if not top:
+        copies.append(copy_out(middle_ref, middle_out, sem_d.at[0]))
+        copies.append(copy_out(w_out, out_out, sem_d.at[1]))
     norm_ref[...] = (norm_stats(middle_ref[...])[0] * gain_ref[layer_at, 1:]).astype(bf16)
     load_up.wait()
-    copies.append(copy_out(w_up, up_out, sem_d.at[2]))
+    if not top:
+        copies.append(copy_out(w_up, up_out, sem_d.at[2]))
     for at in range(units // TILE):
         columns = slice(at * TILE, (at + 1) * TILE)
         before = mm(norm_ref[...], rows_view(w_up, columns))
         phi_sum, phi = gelu_parts(before)
         active_ref[:, columns] = (before * phi_sum).astype(bf16)
         slope_ref[:, columns] = (phi_sum + before * phi).astype(bf16)
-    copies.append(copy_out(slope_ref, slope_out, sem_d.at[3]))
-    copies.append(copy_out(active_ref, active_out, sem_d.at[4]))
+    if not top:
+        copies.append(copy_out(slope_ref, slope_out, sem_d.at[3]))
+        copies.append(copy_out(active_ref, active_out, sem_d.at[4]))
     for copy in copies:
         copy.wait()
 
 
 STATE = ("slope", "middle", "qkv", "lse", "entry")
 WEIGHTS = ("down", "up", "out", "qkv_weight")
-
-
-def backward_body(layers, count, *refs):
-    down_pieces, refs = refs[:count], refs[count:]
+TOP = (*STATE, "qkv_weight")
+
+
+def backward_body(layers, counts, *refs):
+    down_pieces, refs = refs[: counts[0]], refs[counts[0] :]
+    up_pieces, refs = refs[: counts[1]], refs[counts[1] :]
     sources = []
     for layer_at in range(layers):
-        names = STATE + (WEIGHTS if layer_at < layers - 1 else WEIGHTS[1:])
+        names = STATE + WEIGHTS if layer_at < layers - 1 else TOP
         sources.append(dict(zip(names, refs)))
         refs = refs[len(names) :]
-    active_in, refs = refs[0], refs[1:]
-    cotangent_ref, slot_ref, seg_ref, gain_ref = refs[:4]
-    out_ref, prompt_ref, block_ref = refs[4:7]
-    refs = refs[7:]
+    active_in, cotangent_ref, slot_ref, seg_ref, gain_ref = refs[:5]
+    out_ref, prompt_ref, block_ref = refs[5:8]
+    refs = refs[8:]
     held = dict(zip(STATE + WEIGHTS, refs))
     refs = refs[len(held) :]
-    active_ref, low_ref, before_ref, grad_ref, mixed_ref, dqkv_ref, bias_ref = refs[:7]
-    sem, sem_down = refs[7:]
+    low_ref, before_ref, grad_ref, mixed_ref, dqkv_ref, bias_ref = refs[:6]
+    sem, sem_down, sem_up, sem_out = refs[6:]
     order = list(held)
-    units = active_ref.shape[1]
     tokens, width = grad_ref.shape
+    units = before_ref.shape[1]
+    parts = 1 if down_pieces[0].ndim == 2 else 2
+    top_weights = {
+        "down": (down_pieces, 0, units // parts, sem_down, True),
+        "up": (up_pieces, width // parts, units // parts, sem_up, False),
+        "out": (up_pieces, 0, width // parts, sem_out, False),
+    }
 
     class Fetch:
         def __init__(self, name, layer_at):
-            if name == "down" and layer_at == layers - 1:
-                cut = units // (1 if down_pieces[0].ndim == 2 else 2)
-                self.copies = weight_copies(down_pieces, 0, cut, held[name], sem_down).copies
+            if layer_at == layers - 1 and name in top_weights:
+                refs, column, count, sems, late = top_weights[name]
+                self.copies = weight_copies(refs, column, count, held[name], sems, late).copies
             else:
                 source, at = sources[layer_at][name], order.index(name)
                 self.copies = [pltpu.make_async_copy(source, held[name], sem.at[at])]
@@ -348,13 +366,19 @@
             for copy in self.copies:
                 copy.wait()
 
-    names = ("down", "slope", "up", "middle", "out", "qkv", "lse", "qkv_weight", "entry")
-    load_active = None
     coming = {}
-    for name in names:
-        coming[name] = Fetch(name, layers - 1)
-        if name == "slope":
-            load_active = copy_out(active_in, active_ref, sem.at[len(order)])
+
+    def fetch(layer_at, *names):
+        for name in names if layer_at >= 0 else ():
+            coming[name] = Fetch(name, layer_at)
+
+    def arrived(*names):
+        for name in names:
+            if name in coming:
+                coming.pop(name).wait()
+
+    load_active = copy_out(active_in, before_ref, sem.at[len(order)])
+    fetch(layers - 1, "down", "middle", "slope")
     fill_bias(bias_ref, seg_ref)
     low_ref[...] = cotangent_ref[...]
     slot_total = prompt_ref.shape[1]
@@ -366,47 +390,37 @@
     for layer_at in reversed(range(layers)):
         top = layer_at == layers - 1
 
-        def refill(*names):
-            if layer_at > 0:
-                for name in names:
-                    coming[name] = Fetch(name, layer_at - 1)
-
-        coming["down"].wait()
-        coming["slope"].wait()
+        below = layer_at - 1
+        arrived("down")
+        fetch(layer_at, "up")
+        if top:
+            arrived("middle")
+            load_active.wait()
+            branch = mm_t(before_ref[...], rows_view(held["down"]))
+            block_ref[...] = (held["middle"][...] + branch).astype(bf16)
+        arrived("slope")
         for at in range(units // TILE):
             columns = slice(at * TILE, (at + 1) * TILE)
             grad_active = mm(low_ref[...], rows_view(held["down"], columns))
             slope = held["slope"][:, columns].astype(f32)
             before_ref[:, columns] = (grad_active * slope).astype(bf16)
-        coming["middle"].wait()
-        if top:
-            load_active.wait()
-            branch = mm_t(active_ref[...], rows_view(held["down"]))
-            block_ref[...] = (held["middle"][...] + branch).astype(bf16)
-        refill("down", "slope")
-        coming["up"].wait()
+        arrived("up", "middle")
+        fetch(layer_at, "out", "qkv", "lse")
         grad_norm = mm_t(before_ref[...], rows_view(held["up"]))
-        refill("up")
         back = norm_back(grad_norm, held["middle"][...], gain_ref[layer_at, 1:])
         grad = cotangent_ref[...].astype(f32) if top else grad_ref[...]
         grad_middle = grad + back
         grad_ref[...] = grad_middle
         low_ref[...] = grad_middle.astype(bf16)
-        refill("middle")
-        coming["out"].wait()
+        arrived("out", "qkv", "lse")
+        fetch(layer_at, "qkv_weight", "entry")
+        fetch(below, "down", "slope", "middle")
         mixed_ref[...] = mm_t(low_ref[...], rows_view(held["out"])).astype(bf16)
-        refill("out")
-        coming["qkv"].wait()
-        coming["lse"].wait()
         attention_back(held["qkv"], mixed_ref, held["lse"], bias_ref, dqkv_ref)
-        refill("qkv", "lse")
-        coming["qkv_weight"].wait()
+        arrived("qkv_weight", "entry")
         grad_norm = mm_t(dqkv_ref[...], rows_view(held["qkv_weight"]))
-        refill("qkv_weight")
-        coming["entry"].wait()
         back = norm_back(grad_norm, held["entry"][...], gain_ref[layer_at, :1])
         grad_entry = grad_ref[...] + back
-        refill("entry")
         high, low = halves(grad_entry)
         prompt_ref[layer_at] = mm(onehot_t, high) + mm(onehot_t, low)
         passed = jnp.where(is_prompt, 0.0, grad_entry)
@@ -437,6 +451,7 @@
 
 def run(body, away, near, outputs, outputs_away, scratch, flops, name, needs=(), vmem=FORWARD_VMEM):
     here = pl.BlockSpec(memory_space=pltpu.VMEM)
+    hbm = pl.BlockSpec(memory_space=pltpu.HBM)
     anywhere = pl.BlockSpec(memory_space=pl.ANY)
     results = (*outputs, *outputs_away)
     moved = sum(math.prod(a.shape) * a.dtype.itemsize for a in (*away, *near, *results))
@@ -444,7 +459,7 @@
         skipping(body, len(away) + len(near), len(needs), len(results)),
         out_shape=(*results, shape((1, 1), f32)),
         in_specs=[anywhere] * len(away) + [here] * len(near) + [anywhere] * len(needs),
-        out_specs=[here] * len(outputs) + [anywhere] * len(outputs_away) + [here],
+        out_specs=[here] * len(outputs) + [hbm] * len(outputs_away) + [here],
         scratch_shapes=scratch,
         compiler_params=pltpu.CompilerParams(vmem_limit_bytes=vmem),
         cost_estimate=pl.CostEstimate(flops=flops, transcendentals=0, bytes_accessed=moved),
@@ -533,45 +548,46 @@
     return layer, riders, found[0]
 
 
-def mlp_up(pieces, layer_at, layer, gains, units, needs=()):
+def mlp_up(pieces, layer_at, layer, gains, units, top, needs=()):
     tokens, width = layer["mixed"].shape
     out_shape, up_shape = (weight_shape(pieces, width, n) for n in (width, units))
-    results = {
+    state = {
         "middle": shape((tokens, width), f32),
         "slope": shape((tokens, units), bf16),
-        "out": shape(out_shape, bf16),
-        "up": shape(up_shape, bf16),
         "active": shape((tokens, units), bf16),
     }
     scratch = [
         pltpu.VMEM(out_shape, bf16),
         pltpu.VMEM(up_shape, bf16),
         pltpu.VMEM((tokens, width), bf16),
-        pltpu.VMEM((tokens, width), f32),
-        pltpu.VMEM((tokens, units), bf16),
-        pltpu.VMEM((tokens, units), bf16),
         piece_sems(pieces),
         piece_sems(pieces),
         pltpu.SemaphoreType.DMA((5,)),
     ]
+    if top:
+        results, outputs, away_out = state, tuple(state.values()), ()
+    else:
+        weights = {"out": shape(out_shape, bf16), "up": shape(up_shape, bf16)}
+        names = ("middle", "slope", "out", "up", "active")
+        results = {name: {**state, **weights}[name] for name in names}
+        outputs, away_out = (), tuple(results.values())
+        scratch += [pltpu.VMEM(a.shape, a.dtype) for a in state.values()]
     flops = 2 * tokens * width * (units + width)
     away = (*pieces, layer["entry"])
     near = (layer["mixed"], gains)
-    body = partial(mlp_up_body, len(pieces), layer_at)
-    away_out = tuple(results.values())
-    found = run(body, away, near, (), away_out, scratch, flops, "mlp_up", needs)
+    body = partial(mlp_up_body, layer_at, top)
+    found = run(body, away, near, outputs, away_out, scratch, flops, "mlp_up", needs)
     layer.update(zip(results, found))
     return found[-1]
 
 
-def backward(down_pieces, kept, cotangent, marks, gains, slot_total):
+def backward(down_pieces, up_pieces, kept, cotangent, marks, gains, slot_total):
     layers = len(kept)
     tokens, width = cotangent.shape
     units = kept[0]["slope"].shape[1]
-    away = list(down_pieces)
+    away = [*down_pieces, *up_pieces]
     for layer_at, layer in enumerate(kept):
-        names = STATE + (WEIGHTS if layer_at < layers - 1 else WEIGHTS[1:])
-        away += [layer[name] for name in names]
+        away += [layer[name] for name in (STATE + WEIGHTS if layer_at < layers - 1 else TOP)]
     away.append(kept[-1]["active"])
     near = (cotangent, marks["slot"], marks["seg"], gains)
     outputs = (
@@ -582,7 +598,6 @@
     held = [kept[0][name] for name in STATE + WEIGHTS]
     scratch = [pltpu.VMEM(a.shape, a.dtype) for a in held]
     scratch += [
-        pltpu.VMEM((tokens, units), bf16),
         pltpu.VMEM((tokens, width), bf16),
         pltpu.VMEM((tokens, units), bf16),
         pltpu.VMEM((tokens, width), f32),
@@ -591,10 +606,13 @@
         pltpu.VMEM((tokens, tokens), f32),
         pltpu.SemaphoreType.DMA((len(held) + 1,)),
         piece_sems(down_pieces),
+        piece_sems(up_pieces),
+        piece_sems(up_pieces),
     ]
     flops = 2 * layers * tokens * width * (4 * width + 3 * units + 5 * tokens)
-    body = partial(backward_body, layers, len(down_pieces))
-    return run(body, away, near, outputs, (), scratch, flops, "backward", vmem=BACKWARD_VMEM)[:3]
+    body = partial(backward_body, layers, (len(down_pieces), len(up_pieces)))
+    found = run(body, away, near, outputs, (), scratch, flops, "backward", vmem=BACKWARD_VMEM)
+    return found[:3]
 
 
 def axis_sizes():
@@ -609,18 +627,23 @@
     return lax.ppermute(value, axis, [(0, 1), (1, 0)])
 
 
+def move_all(value, to):
+    sizes = axis_sizes()
+    moves = []
+    for at in np.ndindex(*sizes):
+        moves.append(tuple(int(np.ravel_multi_index(place, sizes)) for place in (at, to(*at))))
+    return lax.ppermute(value, ALL, moves)
+
+
 def turn(value, core_of_x):
-    moves = []
-    z_size, x_size, core_size, y_size = axis_sizes()
-    for z in range(z_size):
-        for x in range(x_size):
-            for core in range(core_size):
-                for y in range(y_size):
-                    at = ((z * x_size + x) * core_size + core) * y_size + y
-                    along_x = core == core_of_x
-                    to_x, to_y = (1 - x, y) if along_x else (x, 1 - y)
-                    moves.append((at, ((z * x_size + to_x) * core_size + core) * y_size + to_y))
-    return lax.ppermute(value, ALL, moves)
+    return move_all(
+        value,
+        lambda z, x, core, y: (z, 1 - x, core, y) if core == core_of_x else (z, x, core, 1 - y),
+    )
+
+
+def near_xy(value, dx, dy):
+    return move_all(value, lambda z, x, core, y: (z, x ^ dx, core, y ^ dy))
 
 
 def swap_z(value, distance):
@@ -667,6 +690,20 @@
         whole = self.steps.join(self.parts)
         self.pieces = [whole, flip(whole, "core")]
         return []
+
+
+class LateGather(Gather):
+    def late_first(self):
+        self.parts = [self.steps.behind(self.own)]
+        self.parts.append(turn(self.parts[0], 0))
+        return self.parts[1:]
+
+    def late_ring(self, distances):
+        if len(self.parts) == 2:
+            self.parts = [self.steps.join(self.parts)]
+        own = self.parts[0]
+        self.parts += [swap_z(own, i) for i in distances]
+        return self.parts[-len(distances) :]
 
 
 def total_over(value):
@@ -677,10 +714,10 @@
     mine = jnp.where(core == 0, value[0], value[1])
     theirs = jnp.where(core == 0, low[1], low[0])
     total = mine + flip(theirs, "core").astype(f32)
-    for axis in ("x", "y"):
-        total = total + flip(total.astype(bf16), axis).astype(f32)
-    for pairs in ([(0, 1), (1, 0), (2, 3), (3, 2)], [(0, 2), (2, 0), (1, 3), (3, 1)]):
-        total = total + lax.ppermute(total.astype(bf16), "z", pairs).astype(f32)
+    low = total.astype(bf16)
+    total = total + sum(near_xy(low, *to).astype(f32) for to in ((1, 0), (0, 1), (1, 1)))
+    low = total.astype(bf16)
+    total = total + sum(swap_z(low, distance).astype(f32) for distance in (1, 2, 3))
     other = flip(total.astype(bf16), "core").astype(f32)
     return jnp.stack([jnp.where(core == 0, total, other), jnp.where(core == 0, other, total)])
 
@@ -770,7 +807,8 @@
     def forward_step(at, needs=()):
         layer_at, part = divmod(at, 2)
         if part == 1:
-            return mlp_up(pieces[at], layer_at, kept[layer_at], norm_gains, units, needs)
+            top = layer_at == layers - 1
+            return mlp_up(pieces[at], layer_at, kept[layer_at], norm_gains, units, top, needs)
         layer, state["riders"], zero = attn_forward(
             pieces[at],
             layer_at,
@@ -789,7 +827,8 @@
     if block:
         steps = Steps()
         groups = block_groups(qkv_weight, out_weight, up_weight, down_weight, window)
-        gathers = [Gather(steps, shard) for shard in groups]
+        *early, final = groups
+        gathers = [Gather(steps, shard) for shard in early] + [LateGather(steps, final)]
 
         def kernel(at):
             pieces.append(gathers[at].pieces)
@@ -801,16 +840,17 @@
             Gather.second_turn,
             Gather.last_turn,
         )
+        late_first = LateGather.late_first
+        late_ring = LateGather.late_ring
         for moves, beside in (
             ([(ring, 0)], None),
-            ([(first, 0)], None),
-            ([(second, 0), (ring, 1)], None),
+            ([(first, 0), (late_first, 4)], None),
+            ([(second, 0), (second, 4), (ring, 1)], None),
             ([(last, 0), (first, 1), (ring, 2)], 0),
             ([(second, 1), (first, 2), (ring, 3)], None),
-            ([(last, 1), (second, 2), (first, 3), (ring, 4)], 1),
-            ([(last, 2), (second, 3), (first, 4)], 2),
-            ([(last, 3), (second, 4)], 3),
-            ([(last, 4)], None),
+            ([(last, 1), (second, 2), (first, 3), (partial(late_ring, distances=(1, 2)), 4)], 1),
+            ([(last, 2), (second, 3), (partial(late_ring, distances=(3,)), 4)], 2),
+            ([(last, 3), (last, 4)], 3),
         ):
             coming = [array for move, at in moves for array in move(gathers[at])]
             if beside is not None:
@@ -825,7 +865,7 @@
             forward_step(at)
 
     gradient, layer_grads, block_output = backward(
-        pieces[-1], kept, cotangent, marks, norm_gains, slot_total
+        pieces[-1], pieces[-2], kept, cotangent, marks, norm_gains, slot_total
     )
 
     prompt_grad = total_over(layer_grads)

time: 311 us -> 300 us (0.965)
  waiting for transfers between devices: 80.1 us -> 65.9 us
  starting transfers between devices: 59.1 us -> 70.9 us
  Pallas kernels: 129 us -> 120 us
    ppermute x15 -> x18, starting transfers between devices: 29 us -> 46.9 us  [swap_z(): lax.ppermute(value, 'z', [(i, i ^ distance) for i in range(lax.axis_size(...]
    ppermute x9 -> x7, waiting for transfers between devices: 18.4 us -> 3.93 us  [flip(): return lax.ppermute(value, axis, [(0, 1), (1, 0)])]
    ppermute x15 -> x18, waiting for transfers between devices: 32.2 us -> 42.6 us  [swap_z(): lax.ppermute(value, 'z', [(i, i ^ distance) for i in range(lax.axis_size(...]
    ppermute x12 -> x13, waiting for transfers between devices: 29.5 us -> 19.4 us  [move_all(): return lax.ppermute(value, ALL, moves)]
    pallas_call x5, Pallas kernels: 119 us -> 112 us  [run(): pl.pallas_call(skipping(body, len(away) + len(near), len(needs), len(resu...]
    ppermute x12 -> x13, starting transfers between devices: 15 us -> 9.87 us  [move_all(): return lax.ppermute(value, ALL, moves)]
    pallas_call x8 -> x7, Pallas kernels: 9.63 us -> 7.91 us  [zero_after(): pl.pallas_call(zero_body, out_shape=shape((1, 1), f32), in_specs=[pl.Bloc...]
    ppermute x9 -> x7, starting transfers between devices: 15 us -> 14.1 us  [flip(): return lax.ppermute(value, axis, [(0, 1), (1, 0)])]
  transfers between devices with their start and end apart: 36 -> 38, of which waited for: 23 -> 22; matrix products, arithmetic and copies ran while one was open for 2% -> 3% of each run, Pallas kernels for 19% -> 20%
where the time goes in v1:
time: 300 us; the launch traced here: 294 us
  Pallas kernels  120 us (40%)
  starting transfers between devices  70.9 us (24%)
  waiting for transfers between devices  65.9 us (22%)
  local copies, waits for them, and re-layouts  14.1 us (5%)
  between operations  12.8 us (4%)
  other arithmetic  10.7 us (4%)
    pallas_call x5, Pallas kernels, run(): pl.pallas_call(skipping(body, len(away) + len(near), len(needs), len(resu...  112 us
    ppermute x18, starting transfers between devices, swap_z(): lax.ppermute(value, 'z', [(i, i ^ distance) for i in range(lax.axis_size(...  46.9 us
    ppermute x18, waiting for transfers between devices, swap_z(): lax.ppermute(value, 'z', [(i, i ^ distance) for i in range(lax.axis_size(...  42.6 us
    ppermute x13, waiting for transfers between devices, move_all(): return lax.ppermute(value, ALL, moves)  19.4 us
    ppermute x7, starting transfers between devices, flip(): return lax.ppermute(value, axis, [(0, 1), (1, 0)])  14.1 us
    unnamed x70, local copies, waits for them, and re-layouts  10.5 us
    ppermute x13, starting transfers between devices, move_all(): return lax.ppermute(value, ALL, moves)  9.87 us
    pallas_call x7, Pallas kernels, zero_after(): pl.pallas_call(zero_body, out_shape=shape((1, 1), f32), in_specs=[pl.Bloc...  7.91 us
  transfers between devices with their start and end apart: 38, of which 22 were waited for; matrix products, arithmetic and copies ran while one was open for 3% of the time, Pallas kernels for 20%

profile of v1, /device:TPU:1, one launch (start us, length us, event | category | flops | bytes accessed | tf_op | source)
XLA Modules:
  0.0 294.3 jit_solution(13080555860700079173)
XLA Ops:
  2.7 2.2 collective-permute-start
  4.9 2.3 collective-permute-start.1
  9.6 5.5 %collective-permute-done.2.refs_2_ = bf16[48,1280]{1,0:T(8,128)(2,1)S(1)} collective-permute-done((bf16[48,1280]{1,0:T(8,128)(2,1)S(1)}, bf16[48,1280]{1,0:T(8,128)(2,1)S(1)}, u32[]{:S(2)}, u32[]{:S(2)}) %collective-permute-start.2) | collective-permute-done | bytes 122912 | tf_op jit(solution)/shard_map/ppermute | solution.py:650
  18.1 7.9 %collective-permute-done.3.refs_1_ = bf16[48,1536]{1,0:T(8,128)(2,1)S(1)} collective-permute-done((bf16[48,1536]{1,0:T(8,128)(2,1)S(1)}, bf16[48,1536]{1,0:T(8,128)(2,1)S(1)}, u32[]{:S(2)}, u32[]{:S(2)}) %collective-permute-start.3) | collective-permute-done | bytes 147488 | tf_op jit(solution)/shard_map/ppermute | solution.py:635
  29.6 2.6 collective-permute-start.6
  35.5 2.1 collective-permute-done.7.refs_3_
  37.6 6.6 %collective-permute-done.8.refs_4_ = bf16[48,1920]{1,0:T(8,128)(2,1)S(1)} collective-permute-done((bf16[48,1920]{1,0:T(8,128)(2,1)S(1)}, bf16[48,1920]{1,0:T(8,128)(2,1)S(1)}, u32[]{:S(2)}, u32[]{:S(2)}) %collective-permute-start.8) | collective-permute-done | bytes 184352 | tf_op jit(solution)/shard_map/ppermute | solution.py:650
  46.4 5.8 %collective-permute-start.14 = (bf16[2,2,4,48,1280]{4,3,2,1,0:T(8,128)(2,1)S(1)}, bf16[2,2,4,48,1280]{4,3,2,1,0:T(8,128)(2,1)S(1)}, u32[]{:S(2)}, u32[]{:S(2)}) collective-permute-start(bf16[2,2,4,48,1280]{4,3,2,1,0:T(8,128)(2,1)S(1)} %maximum_add_fusion.6.refs_0_), channel_id=1, source_target_pairs={{0,2},{2,0},{1,3},{3,1},{4,6},{6,4},{5,7},{7,5},{8,10},{10,8},{9,1... | collective-permute-start | bytes 5898248 | tf_op jit(solution)/shard_map/ppermute | solution.py:627
  53.8 2.3 collective-permute-start.11
  59.0 12.2 %attn_forward.2 = (bf16[512,768]{1,0:T(8,128)(2,1)S(1)}, f32[128,512]{1,0:T(8,128)S(1)}, f32[512,768]{1,0:T(8,128)S(1)}, bf16[512,2304]{1,0:T(8,128)(2,1)S(1)}, ...) custom-call(bf16[2,2,4,48,1280]{4,3,2,1,0:T(8,128)(2,1)S(1)} %maximum_add_fusion.6.refs_0_, ...), custom_call_target="tpu_custom_call" | custom-call | flops 5033164800 | bytes 13648384 | tf_op jit(solution)/shard_map/attn_forward/pallas_call | solution.py:458
  71.2 1.9 copy-done.27
  73.1 2.9 collective-permute-done.13.refs_3_
  80.0 6.0 %collective-permute-start.17 = (bf16[48,1920]{1,0:T(8,128)(2,1)S(1)}, bf16[48,1920]{1,0:T(8,128)(2,1)S(1)}, u32[]{:S(2)}, u32[]{:S(2)}) collective-permute-start(bf16[48,1920]{1,0:T(8,128)(2,1)S(1)} %maximum_add_fusion.29), channel_id=1, source_target_pairs={{0,8},{8,0},{16,24},{24,16},{1,9},{9,1},{17,25},{25,17},{2,10},{10... | collective-permute-start | bytes 552968 | tf_op jit(solution)/shard_map/ppermute | solution.py:650
  88.8 2.9 collective-permute-done.17.refs_2_
  92.6 7.4 %collective-permute-done.19.refs_4_ = bf16[48,1920]{1,0:T(8,128)(2,1)S(1)} collective-permute-done((bf16[48,1920]{1,0:T(8,128)(2,1)S(1)}, bf16[48,1920]{1,0:T(8,128)(2,1)S(1)}, u32[]{:S(2)}, u32[]{:S(2)}) %collective-permute-start.19) | collective-permute-done | bytes 184352 | tf_op jit(solution)/shard_map/ppermute | solution.py:650
  100.0 4.2 %collective-permute-done.16.refs_1_ = bf16[4,48,2688]{2,1,0:T(8,128)(2,1)S(1)} collective-permute-done((bf16[4,48,2688]{2,1,0:T(8,128)(2,1)S(1)}, bf16[4,48,2688]{2,1,0:T(8,128)(2,1)S(1)}, u32[]{:S(2)}, u32[]{:S(2)}) %collective-permute-start.16) | collective-permute-done | bytes 1032224 | tf_op jit(solution)/shard_map/ppermute | solution.py:635
  104.2 3.4 %collective-permute-done.15.refs_0_ = bf16[2,4,48,1920]{3,2,1,0:T(8,128)(2,1)S(1)} collective-permute-done((bf16[2,4,48,1920]{3,2,1,0:T(8,128)(2,1)S(1)}, bf16[2,4,48,1920]{3,2,1,0:T(8,128)(2,1)S(1)}, u32[]{:S(2)}, u32[]{:S(2)}) %collective-permute-start.15) | collective-permute-done | bytes 1474592 | tf_op jit(solution)/shard_map/ppermute | solution.py:635
  109.8 2.2 collective-permute-start.25
  114.3 6.0 %collective-permute-start.20 = (bf16[2,2,48,1536]{3,2,1,0:T(8,128)(2,1)S(1)}, bf16[2,2,48,1536]{3,2,1,0:T(8,128)(2,1)S(1)}, u32[]{:S(2)}, u32[]{:S(2)}) collective-permute-start(bf16[2,2,48,1536]{3,2,1,0:T(8,128)(2,1)S(1)} %maximum_add_fusion.20), channel_id=1, source_target_pairs={{0,8},{8,0},{16,24},{24,16},{1,9},{9,1},{17,25},{25,17},{2,10},{10... | collective-permute-start | bytes 1769480 | tf_op jit(solution)/shard_map/ppermute | solution.py:650
  122.1 15.1 %mlp_up.2 = (f32[512,768]{1,0:T(8,128)S(1)}, bf16[512,3072]{1,0:T(8,128)(2,1)S(1)}, bf16[4,192,768]{2,1,0:T(8,128)(2,1)S(1)}, bf16[4,192,3072]{2,1,0:T(8,128)(2,...) custom-call(bf16[2,2,4,48,1920]{4,3,2,1,0:T(8,128)(2,1)S(1)} %maximum_add_fusion.1.refs_0_, ...), custom_call_target="tpu_custom_call" | custom-call | flops 3019898880 | bytes 22032384 | tf_op jit(solution)/shard_map/mlp_up/pallas_call | solution.py:458
  138.4 7.7 %collective-permute-done.20.refs_2_ = bf16[2,2,48,1536]{3,2,1,0:T(8,128)(2,1)S(1)} collective-permute-done((bf16[2,2,48,1536]{3,2,1,0:T(8,128)(2,1)S(1)}, bf16[2,2,48,1536]{3,2,1,0:T(8,128)(2,1)S(1)}, u32[]{:S(2)}, u32[]{:S(2)}) %collective-permute-start.20) | collective-permute-done | bytes 589856 | tf_op jit(solution)/shard_map/ppermute | solution.py:650
  151.1 5.1 %collective-permute-start.22 = (bf16[2,2,48,1536]{3,2,1,0:T(8,128)(2,1)S(1)}, bf16[2,2,48,1536]{3,2,1,0:T(8,128)(2,1)S(1)}, u32[]{:S(2)}, u32[]{:S(2)}) collective-permute-start(bf16[2,2,48,1536]{3,2,1,0:T(8,128)(2,1)S(1)} %maximum_add_fusion.20), channel_id=1, source_target_pairs={{0,24},{8,16},{16,8},{24,0},{1,25},{9,17},{17,9},{25,1},{2,26},{10... | collective-permute-start | bytes 1769480 | tf_op jit(solution)/shard_map/ppermute | solution.py:650
  156.5 16.6 %attn_forward.3 = (bf16[512,768]{1,0:T(8,128)(2,1)S(1)}, f32[128,512]{1,0:T(8,128)S(1)}, f32[512,768]{1,0:T(8,128)S(1)}, bf16[512,2304]{1,0:T(8,128)(2,1)S(1)}, ...) custom-call(bf16[2,2,4,48,2688]{4,3,2,1,0:T(8,128)(2,1)S(1)} %maximum_add_fusion.refs_0_, ...), custom_call_target="tpu_custom_call" | custom-call | flops 5033164800 | bytes 26624512 | tf_op jit(solution)/shard_map/attn_forward/pallas_call | solution.py:458
  180.5 3.0 %collective-permute-done.29.refs_1_.refs_3_ = bf16[2,2,4,48,1920]{4,3,2,1,0:T(8,128)(2,1)} collective-permute-done((bf16[2,2,4,48,1920]{4,3,2,1,0:T(8,128)(2,1)S(1)}, bf16[2,2,4,48,1920]{4,3,2,1,0:T(8,128)(2,1)}, u32[]{:S(2)}, u32[]{:S(2)}) %collective-permute-start.29) | collective-permute-done | bytes 2949152 | tf_op jit(solution)/shard_map/ppermute | solution.py:627
  186.0 13.8 %mlp_up.3 = (f32[512,768]{1,0:T(8,128)S(1)}, bf16[512,3072]{1,0:T(8,128)(2,1)S(1)}, bf16[512,3072]{1,0:T(8,128)(2,1)S(1)}, f32[1,1]{1,0:T(1,128)}) custom-call(bf16[2,2,4,48,1920]{4,3,2,1,0:T(8,128)(2,1)S(1)} %maximum_add_fusion.2.refs_0_.refs_2_, bf16[2,2,4,48,1920]{4,3,2,1,0:T(8,128)(2,1)} %collective-permute-done.29.refs_1_.refs_3_, ...), custom_call_target="tpu_custom_call" | custom-call | flops 3019898880 | bytes 16134144 | tf_op jit(solution)/shard_map/mlp_up/pallas_call | solution.py:458
  201.5 1.7 copy-done.12
  203.3 54.4 %backward.1 = (f32[512,768]{1,0:T(8,128)}, f32[2,50,768]{2,1,0:T(8,128)S(1)}, bf16[512,768]{1,0:T(8,128)(2,1)}, f32[1,1]{1,0:T(1,128)}) custom-call(bf16[4,2,2,48,1536]{4,3,2,1,0:T(8,128)(2,1)} %maximum_add_fusion.3.refs_0_, bf16[4,2,2,48,1536]{4,3,2,1,0:T(8,128)(2,1)} %collective-permute-done.28.refs_1_, bf16[2,2,4,48,1920]{4,3,2,1,0:T(8,128)(2,1)} %copy-done, ...), custom_call_target="tpu_custom_call" | custom-call | flops 23353884672 | bytes 52752384 | tf_op jit(solution)/shard_map/backward/pallas_call | solution.py:458
  265.1 7.7 %collective-permute-start.34 = (bf16[50,768]{1,0:T(8,128)(2,1)S(1)}, bf16[50,768]{1,0:T(8,128)(2,1)S(1)}, u32[]{:S(2)}, u32[]{:S(2)}) collective-permute-start(bf16[50,768]{1,0:T(8,128)(2,1)S(1)} %fusion.7), channel_id=1, source_target_pairs={{0,8},{8,0},{16,24},{24,16},{1,9},{9,1},{17,25},{25,17},{2,10},{10... | collective-permute-start | bytes 230408 | tf_op jit(solution)/shard_map/ppermute | solution.py:650
  272.8 2.0 collective-permute-start.35
  277.2 3.4 %collective-permute-done.36 = bf16[50,768]{1,0:T(8,128)(2,1)S(1)} collective-permute-done((bf16[50,768]{1,0:T(8,128)(2,1)S(1)}, bf16[50,768]{1,0:T(8,128)(2,1)S(1)}, u32[]{:S(2)}, u32[]{:S(2)}) %collective-permute-start.36) | collective-permute-done | bytes 76832 | tf_op jit(solution)/shard_map/ppermute | solution.py:650
  280.7 3.5 %collective-permute-start.37 = (bf16[50,768]{1,0:T(8,128)(2,1)S(1)}, bf16[50,768]{1,0:T(8,128)(2,1)S(1)}, u32[]{:S(2)}, u32[]{:S(2)}) collective-permute-start(bf16[50,768]{1,0:T(8,128)(2,1)S(1)} %get-tuple-element.61), channel_id=1, source_target_pairs={{0,2},{2,0},{1,3},{3,1},{4,6},{6,4},{5,7},{7,5},{8,10},{10,8},{9,1... | collective-permute-start | bytes 230408 | tf_op jit(solution)/shard_map/ppermute | solution.py:627
  290.8 2.0 multiply_subtract_fusion
  (183 shorter events, 59.2 us)
Async XLA Ops:
  2.7 5.5 %collective-permute-start = (bf16[48,1280]{1,0:T(8,128)(2,1)S(1)}, bf16[48,1280]{1,0:T(8,128)(2,1)S(1)}, u32[]{:S(2)}, u32[]{:S(2)}) collective-permute-start(bf16[48,1280]{1,0:T(8,128)(2,1)S(1)} %get-tuple-element.86), channel_id=1, source_target_pairs={{0,8},{8,0},{16,24},{24,16},{1,9},{9,1},{17,25},{25,17},{2,10},{10... | collective-permute-start | bytes 368648 | tf_op jit(solution)/shard_map/ppermute | solution.py:650
  7.2 7.9 %collective-permute-start.2 = (bf16[48,1280]{1,0:T(8,128)(2,1)S(1)}, bf16[48,1280]{1,0:T(8,128)(2,1)S(1)}, u32[]{:S(2)}, u32[]{:S(2)}) collective-permute-start(bf16[48,1280]{1,0:T(8,128)(2,1)S(1)} %get-tuple-element.86), channel_id=1, source_target_pairs={{0,24},{8,16},{16,8},{24,0},{1,25},{9,17},{17,9},{25,1},{2,26},{10... | collective-permute-start | bytes 368648 | tf_op jit(solution)/shard_map/ppermute | solution.py:650
  16.3 9.6 %collective-permute-start.4 = (bf16[4,48,1280]{2,1,0:T(8,128)(2,1)S(1)}, bf16[4,48,1280]{2,1,0:T(8,128)(2,1)S(1)}, u32[]{:S(2)}, u32[]{:S(2)}) collective-permute-start(bf16[4,48,1280]{2,1,0:T(8,128)(2,1)S(1)} %maximum_add_fusion.21), channel_id=1, source_target_pairs={{0,4},{1,5},{2,3},{3,2},{4,0},{5,1},{6,7},{7,6},{8,12},{9,13},{10,... | collective-permute-start | bytes 1474568 | tf_op jit(solution)/shard_map/ppermute | solution.py:635
  17.7 8.3 %collective-permute-start.3 = (bf16[48,1536]{1,0:T(8,128)(2,1)S(1)}, bf16[48,1536]{1,0:T(8,128)(2,1)S(1)}, u32[]{:S(2)}, u32[]{:S(2)}) collective-permute-start(bf16[48,1536]{1,0:T(8,128)(2,1)S(1)} %get-tuple-element.79), channel_id=1, source_target_pairs={{0,4},{1,5},{2,3},{3,2},{4,0},{5,1},{6,7},{7,6},{8,12},{9,13},{10,... | collective-permute-start | bytes 442376 | tf_op jit(solution)/shard_map/ppermute | solution.py:635
  27.9 16.5 %collective-permute-start.9 = (bf16[2,4,48,1280]{3,2,1,0:T(8,128)(2,1)S(1)}, bf16[2,4,48,1280]{3,2,1,0:T(8,128)(2,1)S(1)}, u32[]{:S(2)}, u32[]{:S(2)}) collective-permute-start(bf16[2,4,48,1280]{3,2,1,0:T(8,128)(2,1)S(1)} %maximum_add_fusion.13), channel_id=1, source_target_pairs={{0,1},{1,0},{2,6},{3,7},{4,5},{5,4},{6,2},{7,3},{8,9},{9,8},{10,14... | collective-permute-start | bytes 2949128 | tf_op jit(solution)/shard_map/ppermute | solution.py:635
  29.3 15.1 %collective-permute-start.5 = (bf16[2,48,1536]{2,1,0:T(8,128)(2,1)S(1)}, bf16[2,48,1536]{2,1,0:T(8,128)(2,1)S(1)}, u32[]{:S(2)}, u32[]{:S(2)}) collective-permute-start(bf16[2,48,1536]{2,1,0:T(8,128)(2,1)S(1)} %maximum_add_fusion.24), channel_id=1, source_target_pairs={{0,1},{1,0},{2,6},{3,7},{4,5},{5,4},{6,2},{7,3},{8,9},{9,8},{10,14... | collective-permute-start | bytes 884744 | tf_op jit(solution)/shard_map/ppermute | solution.py:635
  29.6 5.9 %collective-permute-start.6 = (bf16[48,1920]{1,0:T(8,128)(2,1)S(1)}, bf16[48,1920]{1,0:T(8,128)(2,1)S(1)}, u32[]{:S(2)}, u32[]{:S(2)}) collective-permute-start(bf16[48,1920]{1,0:T(8,128)(2,1)S(1)} %maximum_add_fusion.28), channel_id=1, source_target_pairs={{0,8},{8,0},{16,24},{24,16},{1,9},{9,1},{17,25},{25,17},{2,10},{10... | collective-permute-start | bytes 552968 | tf_op jit(solution)/shard_map/ppermute | solution.py:650
  32.3 5.3 %collective-permute-start.7 = (bf16[48,1920]{1,0:T(8,128)(2,1)S(1)}, bf16[48,1920]{1,0:T(8,128)(2,1)S(1)}, u32[]{:S(2)}, u32[]{:S(2)}) collective-permute-start(bf16[48,1920]{1,0:T(8,128)(2,1)S(1)} %maximum_add_fusion.28), channel_id=1, source_target_pairs={{0,16},{8,24},{16,0},{24,8},{1,17},{9,25},{17,1},{25,9},{2,18},{10... | collective-permute-start | bytes 552968 | tf_op jit(solution)/shard_map/ppermute | solution.py:650
  33.8 10.4 %collective-permute-start.8 = (bf16[48,1920]{1,0:T(8,128)(2,1)S(1)}, bf16[48,1920]{1,0:T(8,128)(2,1)S(1)}, u32[]{:S(2)}, u32[]{:S(2)}) collective-permute-start(bf16[48,1920]{1,0:T(8,128)(2,1)S(1)} %maximum_add_fusion.28), channel_id=1, source_target_pairs={{0,24},{8,16},{16,8},{24,0},{1,25},{9,17},{17,9},{25,1},{2,26},{10... | collective-permute-start | bytes 552968 | tf_op jit(solution)/shard_map/ppermute | solution.py:650
  46.4 12.5 %collective-permute-start.14 = (bf16[2,2,4,48,1280]{4,3,2,1,0:T(8,128)(2,1)S(1)}, bf16[2,2,4,48,1280]{4,3,2,1,0:T(8,128)(2,1)S(1)}, u32[]{:S(2)}, u32[]{:S(2)}) collective-permute-start(bf16[2,2,4,48,1280]{4,3,2,1,0:T(8,128)(2,1)S(1)} %maximum_add_fusion.6.refs_0_), channel_id=1, source_target_pairs={{0,2},{2,0},{1,3},{3,1},{4,6},{6,4},{5,7},{7,5},{8,10},{10,8},{9,1... | collective-permute-start | bytes 5898248 | tf_op jit(solution)/shard_map/ppermute | solution.py:627
  52.4 23.5 %collective-permute-start.10 = (bf16[4,48,1920]{2,1,0:T(8,128)(2,1)S(1)}, bf16[4,48,1920]{2,1,0:T(8,128)(2,1)S(1)}, u32[]{:S(2)}, u32[]{:S(2)}) collective-permute-start(bf16[4,48,1920]{2,1,0:T(8,128)(2,1)S(1)} %maximum_add_fusion.16), channel_id=1, source_target_pairs={{0,4},{1,5},{2,3},{3,2},{4,0},{5,1},{6,7},{7,6},{8,12},{9,13},{10,... | collective-permute-start | bytes 2211848 | tf_op jit(solution)/shard_map/ppermute | solution.py:635
  53.8 19.3 %collective-permute-start.11 = (bf16[48,2688]{1,0:T(8,128)(2,1)S(1)}, bf16[48,2688]{1,0:T(8,128)(2,1)S(1)}, u32[]{:S(2)}, u32[]{:S(2)}) collective-permute-start(bf16[48,2688]{1,0:T(8,128)(2,1)S(1)} %maximum_add_fusion.25), channel_id=1, source_target_pairs={{0,8},{8,0},{16,24},{24,16},{1,9},{9,1},{17,25},{25,17},{2,10},{10... | collective-permute-start | bytes 774152 | tf_op jit(solution)/shard_map/ppermute | solution.py:650
  56.1 17.0 %collective-permute-start.12 = (bf16[48,2688]{1,0:T(8,128)(2,1)S(1)}, bf16[48,2688]{1,0:T(8,128)(2,1)S(1)}, u32[]{:S(2)}, u32[]{:S(2)}) collective-permute-start(bf16[48,2688]{1,0:T(8,128)(2,1)S(1)} %maximum_add_fusion.25), channel_id=1, source_target_pairs={{0,16},{8,24},{16,0},{24,8},{1,17},{9,25},{17,1},{25,9},{2,18},{10... | collective-permute-start | bytes 774152 | tf_op jit(solution)/shard_map/ppermute | solution.py:650
  57.7 18.3 %collective-permute-start.13 = (bf16[48,2688]{1,0:T(8,128)(2,1)S(1)}, bf16[48,2688]{1,0:T(8,128)(2,1)S(1)}, u32[]{:S(2)}, u32[]{:S(2)}) collective-permute-start(bf16[48,2688]{1,0:T(8,128)(2,1)S(1)} %maximum_add_fusion.25), channel_id=1, source_target_pairs={{0,24},{8,16},{16,8},{24,0},{1,25},{9,17},{17,9},{25,1},{2,26},{10... | collective-permute-start | bytes 774152 | tf_op jit(solution)/shard_map/ppermute | solution.py:650
  78.0 29.6 %collective-permute-start.15 = (bf16[2,4,48,1920]{3,2,1,0:T(8,128)(2,1)S(1)}, bf16[2,4,48,1920]{3,2,1,0:T(8,128)(2,1)S(1)}, u32[]{:S(2)}, u32[]{:S(2)}) collective-permute-start(bf16[2,4,48,1920]{3,2,1,0:T(8,128)(2,1)S(1)} %maximum_add_fusion.7), channel_id=1, source_target_pairs={{0,1},{1,0},{2,6},{3,7},{4,5},{5,4},{6,2},{7,3},{8,9},{9,8},{10,14... | collective-permute-start | bytes 4423688 | tf_op jit(solution)/shard_map/ppermute | solution.py:635
  79.7 24.5 %collective-permute-start.16 = (bf16[4,48,2688]{2,1,0:T(8,128)(2,1)S(1)}, bf16[4,48,2688]{2,1,0:T(8,128)(2,1)S(1)}, u32[]{:S(2)}, u32[]{:S(2)}) collective-permute-start(bf16[4,48,2688]{2,1,0:T(8,128)(2,1)S(1)} %maximum_add_fusion.11), channel_id=1, source_target_pairs={{0,4},{1,5},{2,3},{3,2},{4,0},{5,1},{6,7},{7,6},{8,12},{9,13},{10,... | collective-permute-start | bytes 3096584 | tf_op jit(solution)/shard_map/ppermute | solution.py:635
  80.0 11.7 %collective-permute-start.17 = (bf16[48,1920]{1,0:T(8,128)(2,1)S(1)}, bf16[48,1920]{1,0:T(8,128)(2,1)S(1)}, u32[]{:S(2)}, u32[]{:S(2)}) collective-permute-start(bf16[48,1920]{1,0:T(8,128)(2,1)S(1)} %maximum_add_fusion.29), channel_id=1, source_target_pairs={{0,8},{8,0},{16,24},{24,16},{1,9},{9,1},{17,25},{25,17},{2,10},{10... | collective-permute-start | bytes 552968 | tf_op jit(solution)/shard_map/ppermute | solution.py:650
  85.9 6.7 %collective-permute-start.18 = (bf16[48,1920]{1,0:T(8,128)(2,1)S(1)}, bf16[48,1920]{1,0:T(8,128)(2,1)S(1)}, u32[]{:S(2)}, u32[]{:S(2)}) collective-permute-start(bf16[48,1920]{1,0:T(8,128)(2,1)S(1)} %maximum_add_fusion.29), channel_id=1, source_target_pairs={{0,16},{8,24},{16,0},{24,8},{1,17},{9,25},{17,1},{25,9},{2,18},{10... | collective-permute-start | bytes 552968 | tf_op jit(solution)/shard_map/ppermute | solution.py:650
  87.5 12.5 %collective-permute-start.19 = (bf16[48,1920]{1,0:T(8,128)(2,1)S(1)}, bf16[48,1920]{1,0:T(8,128)(2,1)S(1)}, u32[]{:S(2)}, u32[]{:S(2)}) collective-permute-start(bf16[48,1920]{1,0:T(8,128)(2,1)S(1)} %maximum_add_fusion.29), channel_id=1, source_target_pairs={{0,24},{8,16},{16,8},{24,0},{1,25},{9,17},{17,9},{25,1},{2,26},{10... | collective-permute-start | bytes 552968 | tf_op jit(solution)/shard_map/ppermute | solution.py:650
  109.8 12.3 %collective-permute-start.25 = (bf16[2,2,4,48,1920]{4,3,2,1,0:T(8,128)(2,1)S(1)}, bf16[2,2,4,48,1920]{4,3,2,1,0:T(8,128)(2,1)S(1)}, u32[]{:S(2)}, u32[]{:S(2)}) collective-permute-start(bf16[2,2,4,48,1920]{4,3,2,1,0:T(8,128)(2,1)S(1)} %maximum_add_fusion.1.refs_0_), channel_id=1, source_target_pairs={{0,2},{2,0},{1,3},{3,1},{4,6},{6,4},{5,7},{7,5},{8,10},{10,8},{9,1... | collective-permute-start | bytes 8847368 | tf_op jit(solution)/shard_map/ppermute | solution.py:627
  113.7 32.9 %collective-permute-start.24 = (bf16[2,4,48,2688]{3,2,1,0:T(8,128)(2,1)}, bf16[2,4,48,2688]{3,2,1,0:T(8,128)(2,1)S(1)}, u32[]{:S(2)}, u32[]{:S(2)}) collective-permute-start(bf16[2,4,48,2688]{3,2,1,0:T(8,128)(2,1)} %maximum_add_fusion.4), channel_id=1, source_target_pairs={{0,1},{1,0},{2,6},{3,7},{4,5},{5,4},{6,2},{7,3},{8,9},{9,8},{10,14... | collective-permute-start | bytes 6193160 | tf_op jit(solution)/shard_map/ppermute | solution.py:635
  114.2 31.9 %collective-permute-start.23 = (bf16[4,48,1920]{2,1,0:T(8,128)(2,1)S(1)}, bf16[4,48,1920]{2,1,0:T(8,128)(2,1)S(1)}, u32[]{:S(2)}, u32[]{:S(2)}) collective-permute-start(bf16[4,48,1920]{2,1,0:T(8,128)(2,1)S(1)} %maximum_add_fusion.18), channel_id=1, source_target_pairs={{0,4},{1,5},{2,3},{3,2},{4,0},{5,1},{6,7},{7,6},{8,12},{9,13},{10,... | collective-permute-start | bytes 2211848 | tf_op jit(solution)/shard_map/ppermute | solution.py:635
  114.3 31.8 %collective-permute-start.20 = (bf16[2,2,48,1536]{3,2,1,0:T(8,128)(2,1)S(1)}, bf16[2,2,48,1536]{3,2,1,0:T(8,128)(2,1)S(1)}, u32[]{:S(2)}, u32[]{:S(2)}) collective-permute-start(bf16[2,2,48,1536]{3,2,1,0:T(8,128)(2,1)S(1)} %maximum_add_fusion.20), channel_id=1, source_target_pairs={{0,8},{8,0},{16,24},{24,16},{1,9},{9,1},{17,25},{25,17},{2,10},{10... | collective-permute-start | bytes 1769480 | tf_op jit(solution)/shard_map/ppermute | solution.py:650
  120.3 25.8 %collective-permute-start.21 = (bf16[2,2,48,1536]{3,2,1,0:T(8,128)(2,1)S(1)}, bf16[2,2,48,1536]{3,2,1,0:T(8,128)(2,1)S(1)}, u32[]{:S(2)}, u32[]{:S(2)}) collective-permute-start(bf16[2,2,48,1536]{3,2,1,0:T(8,128)(2,1)S(1)} %maximum_add_fusion.20), channel_id=1, source_target_pairs={{0,16},{8,24},{16,0},{24,8},{1,17},{9,25},{17,1},{25,9},{2,18},{10... | collective-permute-start | bytes 1769480 | tf_op jit(solution)/shard_map/ppermute | solution.py:650
  149.0 7.5 %collective-permute-start.27 = (bf16[2,2,4,48,2688]{4,3,2,1,0:T(8,128)(2,1)S(1)}, bf16[2,2,4,48,2688]{4,3,2,1,0:T(8,128)(2,1)S(1)}, u32[]{:S(2)}, u32[]{:S(2)}) collective-permute-start(bf16[2,2,4,48,2688]{4,3,2,1,0:T(8,128)(2,1)S(1)} %maximum_add_fusion.refs_0_), channel_id=1, source_target_pairs={{0,2},{2,0},{1,3},{3,1},{4,6},{6,4},{5,7},{7,5},{8,10},{10,8},{9,1... | collective-permute-start | bytes 12386312 | tf_op jit(solution)/shard_map/ppermute | solution.py:627
  150.1 24.5 %collective-permute-start.26 = (bf16[2,4,48,1920]{3,2,1,0:T(8,128)(2,1)S(1)}, bf16[2,4,48,1920]{3,2,1,0:T(8,128)(2,1)S(1)}, u32[]{:S(2)}, u32[]{:S(2)}) collective-permute-start(bf16[2,4,48,1920]{3,2,1,0:T(8,128)(2,1)S(1)} %maximum_add_fusion.8), channel_id=1, source_target_pairs={{0,1},{1,0},{2,6},{3,7},{4,5},{5,4},{6,2},{7,3},{8,9},{9,8},{10,14... | collective-permute-start | bytes 4423688 | tf_op jit(solution)/shard_map/ppermute | solution.py:635
  151.1 23.5 %collective-permute-start.22 = (bf16[2,2,48,1536]{3,2,1,0:T(8,128)(2,1)S(1)}, bf16[2,2,48,1536]{3,2,1,0:T(8,128)(2,1)S(1)}, u32[]{:S(2)}, u32[]{:S(2)}) collective-permute-start(bf16[2,2,48,1536]{3,2,1,0:T(8,128)(2,1)S(1)} %maximum_add_fusion.20), channel_id=1, source_target_pairs={{0,24},{8,16},{16,8},{24,0},{1,25},{9,17},{17,9},{25,1},{2,26},{10... | collective-permute-start | bytes 1769480 | tf_op jit(solution)/shard_map/ppermute | solution.py:650
  177.3 6.2 %collective-permute-start.29 = (bf16[2,2,4,48,1920]{4,3,2,1,0:T(8,128)(2,1)S(1)}, bf16[2,2,4,48,1920]{4,3,2,1,0:T(8,128)(2,1)}, u32[]{:S(2)}, u32[]{:S(2)}) collective-permute-start(bf16[2,2,4,48,1920]{4,3,2,1,0:T(8,128)(2,1)S(1)} %maximum_add_fusion.2.refs_0_.refs_2_), channel_id=1, source_target_pairs={{0,2},{2,0},{1,3},{3,1},{4,6},{6,4},{5,7},{7,5},{8,10},{10,8},{9,1... | collective-permute-start | bytes 8847368 | tf_op jit(solution)/shard_map/ppermute | solution.py:627
  180.1 23.1 %collective-permute-start.28 = (bf16[4,2,2,48,1536]{4,3,2,1,0:T(8,128)(2,1)}, bf16[4,2,2,48,1536]{4,3,2,1,0:T(8,128)(2,1)}, u32[]{:S(2)}, u32[]{:S(2)}) collective-permute-start(bf16[4,2,2,48,1536]{4,3,2,1,0:T(8,128)(2,1)} %maximum_add_fusion.3.refs_0_), channel_id=1, source_target_pairs={{0,2},{2,0},{1,3},{3,1},{4,6},{6,4},{5,7},{7,5},{8,10},{10,8},{9,1... | collective-permute-start | bytes 7077896 | tf_op jit(solution)/shard_map/ppermute | solution.py:627
  265.1 10.9 %collective-permute-start.34 = (bf16[50,768]{1,0:T(8,128)(2,1)S(1)}, bf16[50,768]{1,0:T(8,128)(2,1)S(1)}, u32[]{:S(2)}, u32[]{:S(2)}) collective-permute-start(bf16[50,768]{1,0:T(8,128)(2,1)S(1)} %fusion.7), channel_id=1, source_target_pairs={{0,8},{8,0},{16,24},{24,16},{1,9},{9,1},{17,25},{25,17},{2,10},{10... | collective-permute-start | bytes 230408 | tf_op jit(solution)/shard_map/ppermute | solution.py:650
  274.8 5.8 %collective-permute-start.36 = (bf16[50,768]{1,0:T(8,128)(2,1)S(1)}, bf16[50,768]{1,0:T(8,128)(2,1)S(1)}, u32[]{:S(2)}, u32[]{:S(2)}) collective-permute-start(bf16[50,768]{1,0:T(8,128)(2,1)S(1)} %fusion.7), channel_id=1, source_target_pairs={{0,24},{8,16},{16,8},{24,0},{1,25},{9,17},{17,9},{25,1},{2,26},{10... | collective-permute-start | bytes 230408 | tf_op jit(solution)/shard_map/ppermute | solution.py:650
  280.7 8.6 %collective-permute-start.37 = (bf16[50,768]{1,0:T(8,128)(2,1)S(1)}, bf16[50,768]{1,0:T(8,128)(2,1)S(1)}, u32[]{:S(2)}, u32[]{:S(2)}) collective-permute-start(bf16[50,768]{1,0:T(8,128)(2,1)S(1)} %get-tuple-element.61), channel_id=1, source_target_pairs={{0,2},{2,0},{1,3},{3,1},{4,6},{6,4},{5,7},{7,5},{8,10},{10,8},{9,1... | collective-permute-start | bytes 230408 | tf_op jit(solution)/shard_map/ppermute | solution.py:627
  (41 other events, 461.1 us)

commit v2 on v1

--- a/solution.py
+++ b/solution.py
@@ -25,7 +25,7 @@
 LANES = 128
 TILE = 256
 FORWARD_VMEM = 30 * 2**20
-BACKWARD_VMEM = 41 * 2**20
+BACKWARD_VMEM = 45 * 2**20
 
 TAIL_SLOPE = 0.275
 TAIL_POLY = (
@@ -51,7 +51,7 @@
 
 def gelu_parts(v):
     a = jnp.abs(v)
-    bell = jnp.exp(v * v * -0.5)
+    bell = jnp.exp2(v * v * (-0.5 * math.log2(math.e)))
     t = 1.0 / (1.0 + TAIL_SLOPE * a)
     poly = jnp.full_like(v, TAIL_POLY[-1])
     for factor in TAIL_POLY[-2::-1]:
@@ -105,7 +105,7 @@
     return found
 
 
-def weight_copies(refs, column, width, dest, sems, late=False):
+def weight_copies(refs, column, width, dest, sems, late=False, first=0):
     if refs[0].ndim == 2:
         y_size = dest.shape[-1] // width
         columns = pl.ds(column * y_size, dest.shape[-1])
@@ -114,7 +114,7 @@
     pairs = []
     for ref, (z, x, core, y) in shards(refs, late):
         to_rows = pl.ds(pl.multiple_of((x * 2 + core) * rows, 16), rows)
-        to_columns = pl.ds(pl.multiple_of(y * width, LANES), width)
+        to_columns = pl.ds(pl.multiple_of(y * (dest.shape[-1] // 2) + first, LANES), width)
         pairs.append((ref.at[:, pl.ds(column, width)], dest.at[z, to_rows, to_columns]))
     return Copies(pairs, sems)
 
@@ -243,7 +243,9 @@
         load_down = weight_copies(down_pieces, 0, units // parts, w_down, sem_down).start()
     if takes_riders:
         load_riders = rider_copies(pieces, cut, rider_ref, sem_b).start()
-    load_qkv = weight_copies(qkv_pieces, column, cut, w_qkv, sem_a).start()
+    load_qkv = weight_copies(qkv_pieces, column, cut, w_qkv, sem_a)
+    if not has_down:
+        load_qkv.start()
     fill_bias(bias_ref, seg_ref)
     slots = as_column(slot_ref[...])
     onehot = (slots == base_ref[...]).astype(bf16)
@@ -257,7 +259,7 @@
         load_middle.wait()
         load_active.wait()
         load_down.wait()
-        copies.append(copy_out(w_down, down_out, sem_c.at[3]))
+        load_qkv.start()
         entry_ref[...] = middle_ref[...] + mm_t(active_ref[...], rows_view(w_down))
         x_ref = entry_ref
     for at in range(width // LANES):
@@ -265,9 +267,11 @@
         part = windows[:, at * 8 : (at + 1) * 8, :].reshape(-1, LANES)
         inject = mm(onehot, part.astype(bf16))
         entry_ref[:, lanes] = jnp.where(is_prompt, inject, x_ref[:, lanes].astype(f32))
-    copies.append(copy_out(entry_ref, entry_out, sem_c.at[0]))
     norm_ref[...] = (norm_stats(entry_ref[...])[0] * gain_ref[layer_at, :1]).astype(bf16)
     load_qkv.wait()
+    copies.append(copy_out(entry_ref, entry_out, sem_c.at[0]))
+    if has_down:
+        copies.append(copy_out(w_down, down_out, sem_c.at[3]))
     copies.append(copy_out(w_qkv, weight_out, sem_c.at[1]))
     for at in range(3 * width // TILE):
         columns = slice(at * TILE, (at + 1) * TILE)
@@ -321,6 +325,17 @@
         copy.wait()
 
 
+def top_down_copies(down_pieces, up_pieces, dest, sem_down, sem_rest, width):
+    units = dest.shape[-1]
+    if down_pieces[0].ndim == 2:
+        return weight_copies(down_pieces, 0, units, dest, sem_down).copies
+    here = down_pieces[0].shape[-1]
+    rest = units // 2 - here
+    column = (width + units) // 2
+    copies = weight_copies(down_pieces, 0, here, dest, sem_down, late=True).copies
+    return copies + weight_copies(up_pieces, column, rest, dest, sem_rest, first=here).copies
+
+
 STATE = ("slope", "middle", "qkv", "lse", "entry")
 WEIGHTS = ("down", "up", "out", "qkv_weight")
 TOP = (*STATE, "qkv_weight")
@@ -335,27 +350,29 @@
         sources.append(dict(zip(names, refs)))
         refs = refs[len(names) :]
     active_in, cotangent_ref, slot_ref, seg_ref, gain_ref = refs[:5]
-    out_ref, prompt_ref, block_ref = refs[5:8]
-    refs = refs[8:]
+    (out_ref, prompt_ref, block_ref), refs = refs[5:8], refs[8:]
     held = dict(zip(STATE + WEIGHTS, refs))
     refs = refs[len(held) :]
-    low_ref, before_ref, grad_ref, mixed_ref, dqkv_ref, bias_ref = refs[:6]
-    sem, sem_down, sem_up, sem_out = refs[6:]
+    active_ref, low_ref, before_ref, grad_ref, mixed_ref, dqkv_ref, bias_ref = refs[:7]
+    sem, sem_down, sem_rest, sem_up, sem_out = refs[7:]
     order = list(held)
     tokens, width = grad_ref.shape
     units = before_ref.shape[1]
     parts = 1 if down_pieces[0].ndim == 2 else 2
     top_weights = {
-        "down": (down_pieces, 0, units // parts, sem_down, True),
-        "up": (up_pieces, width // parts, units // parts, sem_up, False),
-        "out": (up_pieces, 0, width // parts, sem_out, False),
+        "up": (up_pieces, width // parts, units // parts, sem_up),
+        "out": (up_pieces, 0, width // parts, sem_out),
     }
 
     class Fetch:
         def __init__(self, name, layer_at):
-            if layer_at == layers - 1 and name in top_weights:
-                refs, column, count, sems, late = top_weights[name]
-                self.copies = weight_copies(refs, column, count, held[name], sems, late).copies
+            if layer_at == layers - 1 and name == "down":
+                self.copies = top_down_copies(
+                    down_pieces, up_pieces, held[name], sem_down, sem_rest, width
+                )
+            elif layer_at == layers - 1 and name in top_weights:
+                refs, column, count, sems = top_weights[name]
+                self.copies = weight_copies(refs, column, count, held[name], sems).copies
             else:
                 source, at = sources[layer_at][name], order.index(name)
                 self.copies = [pltpu.make_async_copy(source, held[name], sem.at[at])]
@@ -377,8 +394,7 @@
             if name in coming:
                 coming.pop(name).wait()
 
-    load_active = copy_out(active_in, before_ref, sem.at[len(order)])
-    fetch(layers - 1, "down", "middle", "slope")
+    fetch(layers - 1, "down", "slope")
     fill_bias(bias_ref, seg_ref)
     low_ref[...] = cotangent_ref[...]
     slot_total = prompt_ref.shape[1]
@@ -391,20 +407,16 @@
         top = layer_at == layers - 1
 
         below = layer_at - 1
-        arrived("down")
-        fetch(layer_at, "up")
-        if top:
-            arrived("middle")
-            load_active.wait()
-            branch = mm_t(before_ref[...], rows_view(held["down"]))
-            block_ref[...] = (held["middle"][...] + branch).astype(bf16)
-        arrived("slope")
+        arrived("down", "slope")
+        fetch(layer_at, *(("up", "middle") if top else ("up",)))
         for at in range(units // TILE):
             columns = slice(at * TILE, (at + 1) * TILE)
             grad_active = mm(low_ref[...], rows_view(held["down"], columns))
             slope = held["slope"][:, columns].astype(f32)
             before_ref[:, columns] = (grad_active * slope).astype(bf16)
         arrived("up", "middle")
+        if top:
+            load_active = copy_out(active_in, active_ref, sem.at[len(order)])
         fetch(layer_at, "out", "qkv", "lse")
         grad_norm = mm_t(before_ref[...], rows_view(held["up"]))
         back = norm_back(grad_norm, held["middle"][...], gain_ref[layer_at, 1:])
@@ -413,9 +425,13 @@
         grad_ref[...] = grad_middle
         low_ref[...] = grad_middle.astype(bf16)
         arrived("out", "qkv", "lse")
+        mixed_ref[...] = mm_t(low_ref[...], rows_view(held["out"])).astype(bf16)
+        if top:
+            load_active.wait()
+            branch = mm_t(active_ref[...], rows_view(held["down"]))
+            block_ref[...] = (held["middle"][...] + branch).astype(bf16)
         fetch(layer_at, "qkv_weight", "entry")
         fetch(below, "down", "slope", "middle")
-        mixed_ref[...] = mm_t(low_ref[...], rows_view(held["out"])).astype(bf16)
         attention_back(held["qkv"], mixed_ref, held["lse"], bias_ref, dqkv_ref)
         arrived("qkv_weight", "entry")
         grad_norm = mm_t(dqkv_ref[...], rows_view(held["qkv_weight"]))
@@ -598,6 +614,7 @@
     held = [kept[0][name] for name in STATE + WEIGHTS]
     scratch = [pltpu.VMEM(a.shape, a.dtype) for a in held]
     scratch += [
+        pltpu.VMEM((tokens, units), bf16),
         pltpu.VMEM((tokens, width), bf16),
         pltpu.VMEM((tokens, units), bf16),
         pltpu.VMEM((tokens, width), f32),
@@ -606,6 +623,7 @@
         pltpu.VMEM((tokens, tokens), f32),
         pltpu.SemaphoreType.DMA((len(held) + 1,)),
         piece_sems(down_pieces),
+        piece_sems(up_pieces),
         piece_sems(up_pieces),
         piece_sems(up_pieces),
     ]
@@ -765,11 +783,15 @@
     out = lax.dynamic_slice(out_weight, (0, 0, y_at * out_cut), (layers, rows, out_cut))
     groups = [jnp.concatenate([qkv[0], window], axis=1)]
     for layer_at in range(layers):
-        groups.append(jnp.concatenate([out[layer_at], up_weight[layer_at]], axis=1))
+        out_up = [out[layer_at], up_weight[layer_at]]
         down = down_weight[layer_at].T
         if layer_at < layers - 1:
             down = jnp.concatenate([down, qkv[layer_at + 1]], axis=1)
-        groups.append(down)
+        else:
+            late = down.shape[1] * 3 // 4
+            out_up.append(down[:, late:])
+            down = down[:, :late]
+        groups += [jnp.concatenate(out_up, axis=1), down]
     return groups
 
 

time: 300 us -> 297 us (0.990)
  starting transfers between devices: 70.9 us -> 63.9 us
    ppermute x18, starting transfers between devices: 46.9 us -> 41 us  [swap_z(): lax.ppermute(value, 'z', [(i, i ^ distance) for i in range(lax.axis_size(...]
    ppermute x18, waiting for transfers between devices: 42.6 us -> 36.9 us  [swap_z(): lax.ppermute(value, 'z', [(i, i ^ distance) for i in range(lax.axis_size(...]
    ppermute x13, waiting for transfers between devices: 19.4 us -> 22.5 us  [move_all(): return lax.ppermute(value, ALL, moves)]
    unnamed x70 -> x90, local copies, waits for them, and re-layouts: 10.5 us -> 12 us
    add x31 -> x32, other arithmetic: 7.22 us -> 7.61 us  [behind(): value + self.zero[0, 0].astype(value.dtype)]
  transfers between devices with their start and end apart: 38 -> 38, of which waited for: 22 -> 21; matrix products, arithmetic and copies ran while one was open for 3% -> 3% of each run, Pallas kernels for 20% -> 20%
where the time goes in v2:
time: 297 us; the launch traced here: 291 us
  Pallas kernels  121 us (41%)
  waiting for transfers between devices  66.1 us (22%)
  starting transfers between devices  63.9 us (22%)
  local copies, waits for them, and re-layouts  17 us (6%)
  between operations  12.6 us (4%)
  other arithmetic  11 us (4%)
    pallas_call x5, Pallas kernels, run(): pl.pallas_call(skipping(body, len(away) + len(near), len(needs), len(resu...  113 us
    ppermute x18, starting transfers between devices, swap_z(): lax.ppermute(value, 'z', [(i, i ^ distance) for i in range(lax.axis_size(...  41 us
    ppermute x18, waiting for transfers between devices, swap_z(): lax.ppermute(value, 'z', [(i, i ^ distance) for i in range(lax.axis_size(...  36.9 us
    ppermute x13, waiting for transfers between devices, move_all(): return lax.ppermute(value, ALL, moves)  22.5 us
    ppermute x7, starting transfers between devices, flip(): return lax.ppermute(value, axis, [(0, 1), (1, 0)])  12.5 us
    unnamed x90, local copies, waits for them, and re-layouts  12 us
    ppermute x13, starting transfers between devices, move_all(): return lax.ppermute(value, ALL, moves)  10.4 us
    pallas_call x7, Pallas kernels, zero_after(): pl.pallas_call(zero_body, out_shape=shape((1, 1), f32), in_specs=[pl.Bloc...  7.98 us
  transfers between devices with their start and end apart: 38, of which 21 were waited for; matrix products, arithmetic and copies ran while one was open for 3% of the time, Pallas kernels for 20%

profile of v2, /device:TPU:1, one launch (start us, length us, event | category | flops | bytes accessed | tf_op | source)
XLA Modules:
  0.0 291.3 jit_solution(11181384892940679185)
XLA Ops:
  2.7 2.2 collective-permute-start
  4.9 2.3 collective-permute-start.1
  7.2 1.7 fusion.11
  9.7 5.4 %collective-permute-done.2.refs_2_ = bf16[48,1280]{1,0:T(8,128)(2,1)S(1)} collective-permute-done((bf16[48,1280]{1,0:T(8,128)(2,1)S(1)}, bf16[48,1280]{1,0:T(8,128)(2,1)S(1)}, u32[]{:S(2)}, u32[]{:S(2)}) %collective-permute-start.2) | collective-permute-done | bytes 122912 | tf_op jit(solution)/shard_map/ppermute | solution.py:668
  18.1 7.5 %collective-permute-done.3.refs_1_ = bf16[48,1152]{1,0:T(8,128)(2,1)S(1)} collective-permute-done((bf16[48,1152]{1,0:T(8,128)(2,1)S(1)}, bf16[48,1152]{1,0:T(8,128)(2,1)S(1)}, u32[]{:S(2)}, u32[]{:S(2)}) %collective-permute-start.3) | collective-permute-done | bytes 110624 | tf_op jit(solution)/shard_map/ppermute | solution.py:653
  28.9 2.6 collective-permute-start.6
  34.8 2.1 collective-permute-done.7.refs_3_
  36.9 6.8 %collective-permute-done.8.refs_4_ = bf16[48,1920]{1,0:T(8,128)(2,1)S(1)} collective-permute-done((bf16[48,1920]{1,0:T(8,128)(2,1)S(1)}, bf16[48,1920]{1,0:T(8,128)(2,1)S(1)}, u32[]{:S(2)}, u32[]{:S(2)}) %collective-permute-start.8) | collective-permute-done | bytes 184352 | tf_op jit(solution)/shard_map/ppermute | solution.py:668
  45.8 5.7 %collective-permute-start.14 = (bf16[2,2,4,48,1280]{4,3,2,1,0:T(8,128)(2,1)S(1)}, bf16[2,2,4,48,1280]{4,3,2,1,0:T(8,128)(2,1)S(1)}, u32[]{:S(2)}, u32[]{:S(2)}) collective-permute-start(bf16[2,2,4,48,1280]{4,3,2,1,0:T(8,128)(2,1)S(1)} %maximum_add_fusion.5.refs_0_), channel_id=1, source_target_pairs={{0,2},{2,0},{1,3},{3,1},{4,6},{6,4},{5,7},{7,5},{8,10},{10,8},{9,1... | collective-permute-start | bytes 5898248 | tf_op jit(solution)/shard_map/ppermute | solution.py:645
  53.1 2.3 collective-permute-start.11
  58.2 12.2 %attn_forward.2 = (bf16[512,768]{1,0:T(8,128)(2,1)S(1)}, f32[128,512]{1,0:T(8,128)S(1)}, f32[512,768]{1,0:T(8,128)S(1)}, bf16[512,2304]{1,0:T(8,128)(2,1)S(1)}, ...) custom-call(bf16[2,2,4,48,1280]{4,3,2,1,0:T(8,128)(2,1)S(1)} %maximum_add_fusion.5.refs_0_, ...), custom_call_target="tpu_custom_call" | custom-call | flops 5033164800 | bytes 13648384 | tf_op jit(solution)/shard_map/attn_forward/pallas_call | solution.py:474
  70.4 1.8 copy-done.26
  73.0 2.5 collective-permute-done.13.refs_3_
  78.7 6.0 %collective-permute-start.17 = (bf16[48,2304]{1,0:T(8,128)(2,1)S(1)}, bf16[48,2304]{1,0:T(8,128)(2,1)S(1)}, u32[]{:S(2)}, u32[]{:S(2)}) collective-permute-start(bf16[48,2304]{1,0:T(8,128)(2,1)S(1)} %maximum_add_fusion.27), channel_id=1, source_target_pairs={{0,8},{8,0},{16,24},{24,16},{1,9},{9,1},{17,25},{25,17},{2,10},{10... | collective-permute-start | bytes 663560 | tf_op jit(solution)/shard_map/ppermute | solution.py:668
  87.4 5.6 %collective-permute-done.17.refs_2_ = bf16[48,2304]{1,0:T(8,128)(2,1)S(1)} collective-permute-done((bf16[48,2304]{1,0:T(8,128)(2,1)S(1)}, bf16[48,2304]{1,0:T(8,128)(2,1)S(1)}, u32[]{:S(2)}, u32[]{:S(2)}) %collective-permute-start.17) | collective-permute-done | bytes 221216 | tf_op jit(solution)/shard_map/ppermute | solution.py:668
  93.2 7.8 %collective-permute-done.19.refs_4_ = bf16[48,2304]{1,0:T(8,128)(2,1)S(1)} collective-permute-done((bf16[48,2304]{1,0:T(8,128)(2,1)S(1)}, bf16[48,2304]{1,0:T(8,128)(2,1)S(1)}, u32[]{:S(2)}, u32[]{:S(2)}) %collective-permute-start.19) | collective-permute-done | bytes 221216 | tf_op jit(solution)/shard_map/ppermute | solution.py:668
  102.4 4.8 %collective-permute-done.15.refs_0_ = bf16[2,4,48,1920]{3,2,1,0:T(8,128)(2,1)S(1)} collective-permute-done((bf16[2,4,48,1920]{3,2,1,0:T(8,128)(2,1)S(1)}, bf16[2,4,48,1920]{3,2,1,0:T(8,128)(2,1)S(1)}, u32[]{:S(2)}, u32[]{:S(2)}) %collective-permute-start.15) | collective-permute-done | bytes 1474592 | tf_op jit(solution)/shard_map/ppermute | solution.py:653
  114.4 5.5 %collective-permute-start.20 = (bf16[2,2,48,1152]{3,2,1,0:T(8,128)(2,1)}, bf16[2,2,48,1152]{3,2,1,0:T(8,128)(2,1)S(1)}, u32[]{:S(2)}, u32[]{:S(2)}) collective-permute-start(bf16[2,2,48,1152]{3,2,1,0:T(8,128)(2,1)} %maximum_add_fusion.22), channel_id=1, source_target_pairs={{0,8},{8,0},{16,24},{24,16},{1,9},{9,1},{17,25},{25,17},{2,10},{10... | collective-permute-start | bytes 1327112 | tf_op jit(solution)/shard_map/ppermute | solution.py:668
  121.6 14.9 %mlp_up.2 = (f32[512,768]{1,0:T(8,128)S(1)}, bf16[512,3072]{1,0:T(8,128)(2,1)S(1)}, bf16[4,192,768]{2,1,0:T(8,128)(2,1)S(1)}, bf16[4,192,3072]{2,1,0:T(8,128)(2,...) custom-call(bf16[2,2,4,48,1920]{4,3,2,1,0:T(8,128)(2,1)S(1)} %maximum_add_fusion.2.refs_0_, ...), custom_call_target="tpu_custom_call" | custom-call | flops 3019898880 | bytes 22032384 | tf_op jit(solution)/shard_map/mlp_up/pallas_call | solution.py:474
  137.6 1.9 collective-permute-done.20.refs_2_
  139.5 5.6 %collective-permute-done.24.refs_0_ = bf16[2,4,48,2688]{3,2,1,0:T(8,128)(2,1)S(1)} collective-permute-done((bf16[2,4,48,2688]{3,2,1,0:T(8,128)(2,1)S(1)}, bf16[2,4,48,2688]{3,2,1,0:T(8,128)(2,1)S(1)}, u32[]{:S(2)}, u32[]{:S(2)}) %collective-permute-start.24) | collective-permute-done | bytes 2064416 | tf_op jit(solution)/shard_map/ppermute | solution.py:653
  150.2 2.6 collective-permute-start.22
  153.1 2.0 collective-permute-done.27.refs_1_
  155.1 16.4 %attn_forward.3 = (bf16[512,768]{1,0:T(8,128)(2,1)S(1)}, f32[128,512]{1,0:T(8,128)S(1)}, f32[512,768]{1,0:T(8,128)S(1)}, bf16[512,2304]{1,0:T(8,128)(2,1)S(1)}, ...) custom-call(bf16[2,2,4,48,2688]{4,3,2,1,0:T(8,128)(2,1)S(1)} %maximum_add_fusion.refs_0_, ...), custom_call_target="tpu_custom_call" | custom-call | flops 5033164800 | bytes 26624512 | tf_op jit(solution)/shard_map/attn_forward/pallas_call | solution.py:474
  176.6 1.8 maximum_add_fusion.6.refs_0_
  178.8 3.7 %collective-permute-done.29.refs_1_.refs_3_ = bf16[2,2,4,48,2304]{4,3,2,1,0:T(8,128)(2,1)} collective-permute-done((bf16[2,2,4,48,2304]{4,3,2,1,0:T(8,128)(2,1)S(1)}, bf16[2,2,4,48,2304]{4,3,2,1,0:T(8,128)(2,1)}, u32[]{:S(2)}, u32[]{:S(2)}) %collective-permute-start.29) | collective-permute-done | bytes 3538976 | tf_op jit(solution)/shard_map/ppermute | solution.py:645
  185.1 13.8 %mlp_up.3 = (f32[512,768]{1,0:T(8,128)S(1)}, bf16[512,3072]{1,0:T(8,128)(2,1)S(1)}, bf16[512,3072]{1,0:T(8,128)(2,1)S(1)}, f32[1,1]{1,0:T(1,128)}) custom-call(bf16[2,2,4,48,2304]{4,3,2,1,0:T(8,128)(2,1)S(1)} %maximum_add_fusion.1.refs_0_.refs_2_, bf16[2,2,4,48,2304]{4,3,2,1,0:T(8,128)(2,1)} %collective-permute-done.29.refs_1_.refs_3_, ...), custom_call_target="tpu_custom_call" | custom-call | flops 3019898880 | bytes 17313792 | tf_op jit(solution)/shard_map/mlp_up/pallas_call | solution.py:474
  202.3 55.5 %backward.1 = (f32[512,768]{1,0:T(8,128)}, f32[2,50,768]{2,1,0:T(8,128)S(1)}, bf16[512,768]{1,0:T(8,128)(2,1)}, f32[1,1]{1,0:T(1,128)}) custom-call(bf16[4,2,2,48,1152]{4,3,2,1,0:T(8,128)(2,1)} %maximum_add_fusion.6.refs_0_, bf16[4,2,2,48,1152]{4,3,2,1,0:T(8,128)(2,1)} %collective-permute-done.28.refs_1_, bf16[2,2,4,48,2304]{4,3,2,1,0:T(8,128)(2,1)} %copy-done, ...), custom_call_target="tpu_custom_call" | custom-call | flops 23353884672 | bytes 52752384 | tf_op jit(solution)/shard_map/backward/pallas_call | solution.py:474
  265.2 5.5 %collective-permute-start.34 = (bf16[50,768]{1,0:T(8,128)(2,1)S(1)}, bf16[50,768]{1,0:T(8,128)(2,1)S(1)}, u32[]{:S(2)}, u32[]{:S(2)}) collective-permute-start(bf16[50,768]{1,0:T(8,128)(2,1)S(1)} %fusion.4), channel_id=1, source_target_pairs={{0,8},{8,0},{16,24},{24,16},{1,9},{9,1},{17,25},{25,17},{2,10},{10... | collective-permute-start | bytes 230408 | tf_op jit(solution)/shard_map/ppermute | solution.py:668
  275.0 2.7 collective-permute-done.36
  277.8 3.9 %collective-permute-start.37 = (bf16[50,768]{1,0:T(8,128)(2,1)S(1)}, bf16[50,768]{1,0:T(8,128)(2,1)S(1)}, u32[]{:S(2)}, u32[]{:S(2)}) collective-permute-start(bf16[50,768]{1,0:T(8,128)(2,1)S(1)} %get-tuple-element.61), channel_id=1, source_target_pairs={{0,2},{2,0},{1,3},{3,1},{4,6},{6,4},{5,7},{7,5},{8,10},{10,8},{9,1... | collective-permute-start | bytes 230408 | tf_op jit(solution)/shard_map/ppermute | solution.py:645
  287.9 1.9 multiply_subtract_fusion
  (207 shorter events, 61.5 us)
Async XLA Ops:
  2.7 7.0 %collective-permute-start = (bf16[48,1280]{1,0:T(8,128)(2,1)S(1)}, bf16[48,1280]{1,0:T(8,128)(2,1)S(1)}, u32[]{:S(2)}, u32[]{:S(2)}) collective-permute-start(bf16[48,1280]{1,0:T(8,128)(2,1)S(1)} %get-tuple-element.86), channel_id=1, source_target_pairs={{0,8},{8,0},{16,24},{24,16},{1,9},{9,1},{17,25},{25,17},{2,10},{10... | collective-permute-start | bytes 368648 | tf_op jit(solution)/shard_map/ppermute | solution.py:668
  7.2 7.9 %collective-permute-start.2 = (bf16[48,1280]{1,0:T(8,128)(2,1)S(1)}, bf16[48,1280]{1,0:T(8,128)(2,1)S(1)}, u32[]{:S(2)}, u32[]{:S(2)}) collective-permute-start(bf16[48,1280]{1,0:T(8,128)(2,1)S(1)} %get-tuple-element.86), channel_id=1, source_target_pairs={{0,24},{8,16},{16,8},{24,0},{1,25},{9,17},{17,9},{25,1},{2,26},{10... | collective-permute-start | bytes 368648 | tf_op jit(solution)/shard_map/ppermute | solution.py:668
  16.4 9.2 %collective-permute-start.4 = (bf16[4,48,1280]{2,1,0:T(8,128)(2,1)S(1)}, bf16[4,48,1280]{2,1,0:T(8,128)(2,1)S(1)}, u32[]{:S(2)}, u32[]{:S(2)}) collective-permute-start(bf16[4,48,1280]{2,1,0:T(8,128)(2,1)S(1)} %maximum_add_fusion.19), channel_id=1, source_target_pairs={{0,4},{1,5},{2,3},{3,2},{4,0},{5,1},{6,7},{7,6},{8,12},{9,13},{10,... | collective-permute-start | bytes 1474568 | tf_op jit(solution)/shard_map/ppermute | solution.py:653
  17.7 7.9 %collective-permute-start.3 = (bf16[48,1152]{1,0:T(8,128)(2,1)S(1)}, bf16[48,1152]{1,0:T(8,128)(2,1)S(1)}, u32[]{:S(2)}, u32[]{:S(2)}) collective-permute-start(bf16[48,1152]{1,0:T(8,128)(2,1)S(1)} %slice_add_fusion), channel_id=1, source_target_pairs={{0,4},{1,5},{2,3},{3,2},{4,0},{5,1},{6,7},{7,6},{8,12},{9,13},{10,... | collective-permute-start | bytes 331784 | tf_op jit(solution)/shard_map/ppermute | solution.py:653
  27.5 16.2 %collective-permute-start.9 = (bf16[2,4,48,1280]{3,2,1,0:T(8,128)(2,1)S(1)}, bf16[2,4,48,1280]{3,2,1,0:T(8,128)(2,1)S(1)}, u32[]{:S(2)}, u32[]{:S(2)}) collective-permute-start(bf16[2,4,48,1280]{3,2,1,0:T(8,128)(2,1)S(1)} %maximum_add_fusion.13), channel_id=1, source_target_pairs={{0,1},{1,0},{2,6},{3,7},{4,5},{5,4},{6,2},{7,3},{8,9},{9,8},{10,14... | collective-permute-start | bytes 2949128 | tf_op jit(solution)/shard_map/ppermute | solution.py:653
  28.9 5.9 %collective-permute-start.6 = (bf16[48,1920]{1,0:T(8,128)(2,1)S(1)}, bf16[48,1920]{1,0:T(8,128)(2,1)S(1)}, u32[]{:S(2)}, u32[]{:S(2)}) collective-permute-start(bf16[48,1920]{1,0:T(8,128)(2,1)S(1)} %maximum_add_fusion.30), channel_id=1, source_target_pairs={{0,8},{8,0},{16,24},{24,16},{1,9},{9,1},{17,25},{25,17},{2,10},{10... | collective-permute-start | bytes 552968 | tf_op jit(solution)/shard_map/ppermute | solution.py:668
  31.6 5.4 %collective-permute-start.7 = (bf16[48,1920]{1,0:T(8,128)(2,1)S(1)}, bf16[48,1920]{1,0:T(8,128)(2,1)S(1)}, u32[]{:S(2)}, u32[]{:S(2)}) collective-permute-start(bf16[48,1920]{1,0:T(8,128)(2,1)S(1)} %maximum_add_fusion.30), channel_id=1, source_target_pairs={{0,16},{8,24},{16,0},{24,8},{1,17},{9,25},{17,1},{25,9},{2,18},{10... | collective-permute-start | bytes 552968 | tf_op jit(solution)/shard_map/ppermute | solution.py:668
  33.1 10.7 %collective-permute-start.8 = (bf16[48,1920]{1,0:T(8,128)(2,1)S(1)}, bf16[48,1920]{1,0:T(8,128)(2,1)S(1)}, u32[]{:S(2)}, u32[]{:S(2)}) collective-permute-start(bf16[48,1920]{1,0:T(8,128)(2,1)S(1)} %maximum_add_fusion.30), channel_id=1, source_target_pairs={{0,24},{8,16},{16,8},{24,0},{1,25},{9,17},{17,9},{25,1},{2,26},{10... | collective-permute-start | bytes 552968 | tf_op jit(solution)/shard_map/ppermute | solution.py:668
  34.2 9.5 %collective-permute-start.5 = (bf16[2,48,1152]{2,1,0:T(8,128)(2,1)S(1)}, bf16[2,48,1152]{2,1,0:T(8,128)(2,1)S(1)}, u32[]{:S(2)}, u32[]{:S(2)}) collective-permute-start(bf16[2,48,1152]{2,1,0:T(8,128)(2,1)S(1)} %maximum_add_fusion.26), channel_id=1, source_target_pairs={{0,1},{1,0},{2,6},{3,7},{4,5},{5,4},{6,2},{7,3},{8,9},{9,8},{10,14... | collective-permute-start | bytes 663560 | tf_op jit(solution)/shard_map/ppermute | solution.py:653
  45.8 12.3 %collective-permute-start.14 = (bf16[2,2,4,48,1280]{4,3,2,1,0:T(8,128)(2,1)S(1)}, bf16[2,2,4,48,1280]{4,3,2,1,0:T(8,128)(2,1)S(1)}, u32[]{:S(2)}, u32[]{:S(2)}) collective-permute-start(bf16[2,2,4,48,1280]{4,3,2,1,0:T(8,128)(2,1)S(1)} %maximum_add_fusion.5.refs_0_), channel_id=1, source_target_pairs={{0,2},{2,0},{1,3},{3,1},{4,6},{6,4},{5,7},{7,5},{8,10},{10,8},{9,1... | collective-permute-start | bytes 5898248 | tf_op jit(solution)/shard_map/ppermute | solution.py:645
  51.7 23.8 %collective-permute-start.10 = (bf16[4,48,1920]{2,1,0:T(8,128)(2,1)S(1)}, bf16[4,48,1920]{2,1,0:T(8,128)(2,1)S(1)}, u32[]{:S(2)}, u32[]{:S(2)}) collective-permute-start(bf16[4,48,1920]{2,1,0:T(8,128)(2,1)S(1)} %maximum_add_fusion.18), channel_id=1, source_target_pairs={{0,4},{1,5},{2,3},{3,2},{4,0},{5,1},{6,7},{7,6},{8,12},{9,13},{10,... | collective-permute-start | bytes 2211848 | tf_op jit(solution)/shard_map/ppermute | solution.py:653
  53.1 19.9 %collective-permute-start.11 = (bf16[48,2688]{1,0:T(8,128)(2,1)S(1)}, bf16[48,2688]{1,0:T(8,128)(2,1)S(1)}, u32[]{:S(2)}, u32[]{:S(2)}) collective-permute-start(bf16[48,2688]{1,0:T(8,128)(2,1)S(1)} %maximum_add_fusion.23), channel_id=1, source_target_pairs={{0,8},{8,0},{16,24},{24,16},{1,9},{9,1},{17,25},{25,17},{2,10},{10... | collective-permute-start | bytes 774152 | tf_op jit(solution)/shard_map/ppermute | solution.py:668
  55.4 17.6 %collective-permute-start.12 = (bf16[48,2688]{1,0:T(8,128)(2,1)S(1)}, bf16[48,2688]{1,0:T(8,128)(2,1)S(1)}, u32[]{:S(2)}, u32[]{:S(2)}) collective-permute-start(bf16[48,2688]{1,0:T(8,128)(2,1)S(1)} %maximum_add_fusion.23), channel_id=1, source_target_pairs={{0,16},{8,24},{16,0},{24,8},{1,17},{9,25},{17,1},{25,9},{2,18},{10... | collective-permute-start | bytes 774152 | tf_op jit(solution)/shard_map/ppermute | solution.py:668
  56.9 18.6 %collective-permute-start.13 = (bf16[48,2688]{1,0:T(8,128)(2,1)S(1)}, bf16[48,2688]{1,0:T(8,128)(2,1)S(1)}, u32[]{:S(2)}, u32[]{:S(2)}) collective-permute-start(bf16[48,2688]{1,0:T(8,128)(2,1)S(1)} %maximum_add_fusion.23), channel_id=1, source_target_pairs={{0,24},{8,16},{16,8},{24,0},{1,25},{9,17},{17,9},{25,1},{2,26},{10... | collective-permute-start | bytes 774152 | tf_op jit(solution)/shard_map/ppermute | solution.py:668
  77.6 29.6 %collective-permute-start.15 = (bf16[2,4,48,1920]{3,2,1,0:T(8,128)(2,1)S(1)}, bf16[2,4,48,1920]{3,2,1,0:T(8,128)(2,1)S(1)}, u32[]{:S(2)}, u32[]{:S(2)}) collective-permute-start(bf16[2,4,48,1920]{3,2,1,0:T(8,128)(2,1)S(1)} %maximum_add_fusion.9), channel_id=1, source_target_pairs={{0,1},{1,0},{2,6},{3,7},{4,5},{5,4},{6,2},{7,3},{8,9},{9,8},{10,14... | collective-permute-start | bytes 4423688 | tf_op jit(solution)/shard_map/ppermute | solution.py:653
  78.0 24.4 %collective-permute-start.16 = (bf16[4,48,2688]{2,1,0:T(8,128)(2,1)S(1)}, bf16[4,48,2688]{2,1,0:T(8,128)(2,1)S(1)}, u32[]{:S(2)}, u32[]{:S(2)}) collective-permute-start(bf16[4,48,2688]{2,1,0:T(8,128)(2,1)S(1)} %maximum_add_fusion.11), channel_id=1, source_target_pairs={{0,4},{1,5},{2,3},{3,2},{4,0},{5,1},{6,7},{7,6},{8,12},{9,13},{10,... | collective-permute-start | bytes 3096584 | tf_op jit(solution)/shard_map/ppermute | solution.py:653
  78.7 14.2 %collective-permute-start.17 = (bf16[48,2304]{1,0:T(8,128)(2,1)S(1)}, bf16[48,2304]{1,0:T(8,128)(2,1)S(1)}, u32[]{:S(2)}, u32[]{:S(2)}) collective-permute-start(bf16[48,2304]{1,0:T(8,128)(2,1)S(1)} %maximum_add_fusion.27), channel_id=1, source_target_pairs={{0,8},{8,0},{16,24},{24,16},{1,9},{9,1},{17,25},{25,17},{2,10},{10... | collective-permute-start | bytes 663560 | tf_op jit(solution)/shard_map/ppermute | solution.py:668
  84.6 8.5 %collective-permute-start.18 = (bf16[48,2304]{1,0:T(8,128)(2,1)S(1)}, bf16[48,2304]{1,0:T(8,128)(2,1)S(1)}, u32[]{:S(2)}, u32[]{:S(2)}) collective-permute-start(bf16[48,2304]{1,0:T(8,128)(2,1)S(1)} %maximum_add_fusion.27), channel_id=1, source_target_pairs={{0,16},{8,24},{16,0},{24,8},{1,17},{9,25},{17,1},{25,9},{2,18},{10... | collective-permute-start | bytes 663560 | tf_op jit(solution)/shard_map/ppermute | solution.py:668
  86.1 15.0 %collective-permute-start.19 = (bf16[48,2304]{1,0:T(8,128)(2,1)S(1)}, bf16[48,2304]{1,0:T(8,128)(2,1)S(1)}, u32[]{:S(2)}, u32[]{:S(2)}) collective-permute-start(bf16[48,2304]{1,0:T(8,128)(2,1)S(1)} %maximum_add_fusion.27), channel_id=1, source_target_pairs={{0,24},{8,16},{16,8},{24,0},{1,25},{9,17},{17,9},{25,1},{2,26},{10... | collective-permute-start | bytes 663560 | tf_op jit(solution)/shard_map/ppermute | solution.py:668
  109.4 12.1 %collective-permute-start.25 = (bf16[2,2,4,48,1920]{4,3,2,1,0:T(8,128)(2,1)S(1)}, bf16[2,2,4,48,1920]{4,3,2,1,0:T(8,128)(2,1)S(1)}, u32[]{:S(2)}, u32[]{:S(2)}) collective-permute-start(bf16[2,2,4,48,1920]{4,3,2,1,0:T(8,128)(2,1)S(1)} %maximum_add_fusion.2.refs_0_), channel_id=1, source_target_pairs={{0,2},{2,0},{1,3},{3,1},{4,6},{6,4},{5,7},{7,5},{8,10},{10,8},{9,1... | collective-permute-start | bytes 8847368 | tf_op jit(solution)/shard_map/ppermute | solution.py:645
  110.8 34.4 %collective-permute-start.24 = (bf16[2,4,48,2688]{3,2,1,0:T(8,128)(2,1)S(1)}, bf16[2,4,48,2688]{3,2,1,0:T(8,128)(2,1)S(1)}, u32[]{:S(2)}, u32[]{:S(2)}) collective-permute-start(bf16[2,4,48,2688]{3,2,1,0:T(8,128)(2,1)S(1)} %maximum_add_fusion.3), channel_id=1, source_target_pairs={{0,1},{1,0},{2,6},{3,7},{4,5},{5,4},{6,2},{7,3},{8,9},{9,8},{10,14... | collective-permute-start | bytes 6193160 | tf_op jit(solution)/shard_map/ppermute | solution.py:653
  113.5 26.0 %collective-permute-start.23 = (bf16[4,48,2304]{2,1,0:T(8,128)(2,1)}, bf16[4,48,2304]{2,1,0:T(8,128)(2,1)S(1)}, u32[]{:S(2)}, u32[]{:S(2)}) collective-permute-start(bf16[4,48,2304]{2,1,0:T(8,128)(2,1)} %maximum_add_fusion.16), channel_id=1, source_target_pairs={{0,4},{1,5},{2,3},{3,2},{4,0},{5,1},{6,7},{7,6},{8,12},{9,13},{10,... | collective-permute-start | bytes 2654216 | tf_op jit(solution)/shard_map/ppermute | solution.py:653
  114.4 25.1 %collective-permute-start.20 = (bf16[2,2,48,1152]{3,2,1,0:T(8,128)(2,1)}, bf16[2,2,48,1152]{3,2,1,0:T(8,128)(2,1)S(1)}, u32[]{:S(2)}, u32[]{:S(2)}) collective-permute-start(bf16[2,2,48,1152]{3,2,1,0:T(8,128)(2,1)} %maximum_add_fusion.22), channel_id=1, source_target_pairs={{0,8},{8,0},{16,24},{24,16},{1,9},{9,1},{17,25},{25,17},{2,10},{10... | collective-permute-start | bytes 1327112 | tf_op jit(solution)/shard_map/ppermute | solution.py:668
  119.8 19.7 %collective-permute-start.21 = (bf16[2,2,48,1152]{3,2,1,0:T(8,128)(2,1)}, bf16[2,2,48,1152]{3,2,1,0:T(8,128)(2,1)S(1)}, u32[]{:S(2)}, u32[]{:S(2)}) collective-permute-start(bf16[2,2,48,1152]{3,2,1,0:T(8,128)(2,1)} %maximum_add_fusion.22), channel_id=1, source_target_pairs={{0,16},{8,24},{16,0},{24,8},{1,17},{9,25},{17,1},{25,9},{2,18},{10... | collective-permute-start | bytes 1327112 | tf_op jit(solution)/shard_map/ppermute | solution.py:668
  147.5 7.6 %collective-permute-start.27 = (bf16[2,2,4,48,2688]{4,3,2,1,0:T(8,128)(2,1)S(1)}, bf16[2,2,4,48,2688]{4,3,2,1,0:T(8,128)(2,1)S(1)}, u32[]{:S(2)}, u32[]{:S(2)}) collective-permute-start(bf16[2,2,4,48,2688]{4,3,2,1,0:T(8,128)(2,1)S(1)} %maximum_add_fusion.refs_0_), channel_id=1, source_target_pairs={{0,2},{2,0},{1,3},{3,1},{4,6},{6,4},{5,7},{7,5},{8,10},{10,8},{9,1... | collective-permute-start | bytes 12386312 | tf_op jit(solution)/shard_map/ppermute | solution.py:645
  148.7 24.5 %collective-permute-start.26 = (bf16[2,4,48,2304]{3,2,1,0:T(8,128)(2,1)S(1)}, bf16[2,4,48,2304]{3,2,1,0:T(8,128)(2,1)S(1)}, u32[]{:S(2)}, u32[]{:S(2)}) collective-permute-start(bf16[2,4,48,2304]{3,2,1,0:T(8,128)(2,1)S(1)} %maximum_add_fusion.7), channel_id=1, source_target_pairs={{0,1},{1,0},{2,6},{3,7},{4,5},{5,4},{6,2},{7,3},{8,9},{9,8},{10,14... | collective-permute-start | bytes 5308424 | tf_op jit(solution)/shard_map/ppermute | solution.py:653
  150.2 23.0 %collective-permute-start.22 = (bf16[2,2,48,1152]{3,2,1,0:T(8,128)(2,1)}, bf16[2,2,48,1152]{3,2,1,0:T(8,128)(2,1)S(1)}, u32[]{:S(2)}, u32[]{:S(2)}) collective-permute-start(bf16[2,2,48,1152]{3,2,1,0:T(8,128)(2,1)} %maximum_add_fusion.22), channel_id=1, source_target_pairs={{0,24},{8,16},{16,8},{24,0},{1,25},{9,17},{17,9},{25,1},{2,26},{10... | collective-permute-start | bytes 1327112 | tf_op jit(solution)/shard_map/ppermute | solution.py:668
  176.1 6.4 %collective-permute-start.29 = (bf16[2,2,4,48,2304]{4,3,2,1,0:T(8,128)(2,1)S(1)}, bf16[2,2,4,48,2304]{4,3,2,1,0:T(8,128)(2,1)}, u32[]{:S(2)}, u32[]{:S(2)}) collective-permute-start(bf16[2,2,4,48,2304]{4,3,2,1,0:T(8,128)(2,1)S(1)} %maximum_add_fusion.1.refs_0_.refs_2_), channel_id=1, source_target_pairs={{0,2},{2,0},{1,3},{3,1},{4,6},{6,4},{5,7},{7,5},{8,10},{10,8},{9,1... | collective-permute-start | bytes 10616840 | tf_op jit(solution)/shard_map/ppermute | solution.py:645
  178.4 23.8 %collective-permute-start.28 = (bf16[4,2,2,48,1152]{4,3,2,1,0:T(8,128)(2,1)}, bf16[4,2,2,48,1152]{4,3,2,1,0:T(8,128)(2,1)}, u32[]{:S(2)}, u32[]{:S(2)}) collective-permute-start(bf16[4,2,2,48,1152]{4,3,2,1,0:T(8,128)(2,1)} %maximum_add_fusion.6.refs_0_), channel_id=1, source_target_pairs={{0,2},{2,0},{1,3},{3,1},{4,6},{6,4},{5,7},{7,5},{8,10},{10,8},{9,1... | collective-permute-start | bytes 5308424 | tf_op jit(solution)/shard_map/ppermute | solution.py:645
  265.2 8.2 %collective-permute-start.34 = (bf16[50,768]{1,0:T(8,128)(2,1)S(1)}, bf16[50,768]{1,0:T(8,128)(2,1)S(1)}, u32[]{:S(2)}, u32[]{:S(2)}) collective-permute-start(bf16[50,768]{1,0:T(8,128)(2,1)S(1)} %fusion.4), channel_id=1, source_target_pairs={{0,8},{8,0},{16,24},{24,16},{1,9},{9,1},{17,25},{25,17},{2,10},{10... | collective-permute-start | bytes 230408 | tf_op jit(solution)/shard_map/ppermute | solution.py:668
  272.3 5.4 %collective-permute-start.36 = (bf16[50,768]{1,0:T(8,128)(2,1)S(1)}, bf16[50,768]{1,0:T(8,128)(2,1)S(1)}, u32[]{:S(2)}, u32[]{:S(2)}) collective-permute-start(bf16[50,768]{1,0:T(8,128)(2,1)S(1)} %fusion.4), channel_id=1, source_target_pairs={{0,24},{8,16},{16,8},{24,0},{1,25},{9,17},{17,9},{25,1},{2,26},{10... | collective-permute-start | bytes 230408 | tf_op jit(solution)/shard_map/ppermute | solution.py:668
  277.8 8.6 %collective-permute-start.37 = (bf16[50,768]{1,0:T(8,128)(2,1)S(1)}, bf16[50,768]{1,0:T(8,128)(2,1)S(1)}, u32[]{:S(2)}, u32[]{:S(2)}) collective-permute-start(bf16[50,768]{1,0:T(8,128)(2,1)S(1)} %get-tuple-element.61), channel_id=1, source_target_pairs={{0,2},{2,0},{1,3},{3,1},{4,6},{6,4},{5,7},{7,5},{8,10},{10,8},{9,1... | collective-permute-start | bytes 230408 | tf_op jit(solution)/shard_map/ppermute | solution.py:645
  (51 other events, 478.6 us)

commit v3 on v2

--- a/solution.py
+++ b/solution.py
@@ -456,31 +456,22 @@
     return jax.ShapeDtypeStruct(dims, dtype)
 
 
-def skipping(body, taken, needed, results):
-    def kernel(*refs):
-        ends = taken + needed, taken + needed + results
-        body(*refs[:taken], *refs[ends[0] : ends[1]], *refs[ends[1] + 1 :])
-        refs[ends[1]][...] = jnp.zeros((1, 1), f32)
-
-    return kernel
-
-
-def run(body, away, near, outputs, outputs_away, scratch, flops, name, needs=(), vmem=FORWARD_VMEM):
+def run(body, away, near, outputs, outputs_away, scratch, flops, name, vmem=FORWARD_VMEM):
     here = pl.BlockSpec(memory_space=pltpu.VMEM)
     hbm = pl.BlockSpec(memory_space=pltpu.HBM)
     anywhere = pl.BlockSpec(memory_space=pl.ANY)
     results = (*outputs, *outputs_away)
     moved = sum(math.prod(a.shape) * a.dtype.itemsize for a in (*away, *near, *results))
     return pl.pallas_call(
-        skipping(body, len(away) + len(near), len(needs), len(results)),
-        out_shape=(*results, shape((1, 1), f32)),
-        in_specs=[anywhere] * len(away) + [here] * len(near) + [anywhere] * len(needs),
-        out_specs=[here] * len(outputs) + [hbm] * len(outputs_away) + [here],
+        body,
+        out_shape=results,
+        in_specs=[anywhere] * len(away) + [here] * len(near),
+        out_specs=[here] * len(outputs) + [hbm] * len(outputs_away),
         scratch_shapes=scratch,
         compiler_params=pltpu.CompilerParams(vmem_limit_bytes=vmem),
         cost_estimate=pl.CostEstimate(flops=flops, transcendentals=0, bytes_accessed=moved),
         name=name,
-    )(*away, *near, *needs)
+    )(*away, *near)
 
 
 def zero_body(*refs):
@@ -508,7 +499,7 @@
     return (width, columns) if pieces[0].ndim == 2 else (4, width // 4, columns)
 
 
-def attn_forward(pieces, layer_at, slot_total, x, below, riders, marks, gains, needs=()):
+def attn_forward(pieces, layer_at, slot_total, x, below, riders, marks, gains):
     tokens = marks["seg"].shape[1]
     width = gains.shape[2]
     takes_riders, has_down = riders is None, below is not None
@@ -553,7 +544,7 @@
     ]
     flops = 2 * tokens * width * (7 * width + 2 * tokens)
     body = partial(attn_forward_body, (len(pieces), layer_at, slot_total, takes_riders, has_down))
-    found = run(body, away, near, near_out, away_out, scratch, flops, "attn_forward", needs)
+    found = run(body, away, near, near_out, away_out, scratch, flops, "attn_forward")
     names = ("mixed", "lse", "entry", "qkv", "qkv_weight")
     layer = dict(zip(names, found))
     found = found[5:]
@@ -561,10 +552,10 @@
         riders, found = found[0], found[1:]
     if has_down:
         below["down"], found = found[0], found[1:]
-    return layer, riders, found[0]
-
-
-def mlp_up(pieces, layer_at, layer, gains, units, top, needs=()):
+    return layer, riders
+
+
+def mlp_up(pieces, layer_at, layer, gains, units, top):
     tokens, width = layer["mixed"].shape
     out_shape, up_shape = (weight_shape(pieces, width, n) for n in (width, units))
     state = {
@@ -592,9 +583,8 @@
     away = (*pieces, layer["entry"])
     near = (layer["mixed"], gains)
     body = partial(mlp_up_body, layer_at, top)
-    found = run(body, away, near, outputs, away_out, scratch, flops, "mlp_up", needs)
+    found = run(body, away, near, outputs, away_out, scratch, flops, "mlp_up")
     layer.update(zip(results, found))
-    return found[-1]
 
 
 def backward(down_pieces, up_pieces, kept, cotangent, marks, gains, slot_total):
@@ -629,8 +619,7 @@
     ]
     flops = 2 * layers * tokens * width * (4 * width + 3 * units + 5 * tokens)
     body = partial(backward_body, layers, (len(down_pieces), len(up_pieces)))
-    found = run(body, away, near, outputs, (), scratch, flops, "backward", vmem=BACKWARD_VMEM)
-    return found[:3]
+    return run(body, away, near, outputs, (), scratch, flops, "backward", vmem=BACKWARD_VMEM)
 
 
 def axis_sizes():
@@ -672,9 +661,6 @@
     def __init__(self):
         self.zero = None
 
-    def needs(self):
-        return [] if self.zero is None else [self.zero]
-
     def behind(self, value):
         return value if self.zero is None else value + self.zero[0, 0].astype(value.dtype)
 
@@ -682,7 +668,7 @@
         return self.behind(jnp.stack(parts))
 
     def wait(self, arrays):
-        self.zero = zero_after([*arrays, *self.needs()])
+        self.zero = zero_after(arrays)
 
 
 class Gather:
@@ -826,12 +812,13 @@
     pieces = []
     state = {"riders": None}
 
-    def forward_step(at, needs=()):
+    def forward_step(at):
         layer_at, part = divmod(at, 2)
         if part == 1:
             top = layer_at == layers - 1
-            return mlp_up(pieces[at], layer_at, kept[layer_at], norm_gains, units, top, needs)
-        layer, state["riders"], zero = attn_forward(
+            mlp_up(pieces[at], layer_at, kept[layer_at], norm_gains, units, top)
+            return
+        layer, state["riders"] = attn_forward(
             pieces[at],
             layer_at,
             slot_total,
@@ -840,10 +827,8 @@
             state["riders"],
             marks,
             norm_gains,
-            needs,
         )
         kept.append(layer)
-        return zero
 
     block = is_block()
     if block:
@@ -854,7 +839,8 @@
 
         def kernel(at):
             pieces.append(gathers[at].pieces)
-            steps.zero = forward_step(at, steps.needs())
+            forward_step(at)
+            return [kept[at // 2][("entry", "middle")[at % 2]]]
 
         ring, first, second, last = (
             Gather.start_ring,
@@ -867,18 +853,17 @@
         for moves, beside in (
             ([(ring, 0)], None),
             ([(first, 0), (late_first, 4)], None),
-            ([(second, 0), (second, 4), (ring, 1)], None),
-            ([(last, 0), (first, 1), (ring, 2)], 0),
-            ([(second, 1), (first, 2), (ring, 3)], None),
+            ([(ring, 1), (second, 0), (second, 4)], None),
+            ([(ring, 2), (last, 0), (first, 1)], 0),
+            ([(ring, 3), (second, 1), (first, 2)], None),
             ([(last, 1), (second, 2), (first, 3), (partial(late_ring, distances=(1, 2)), 4)], 1),
             ([(last, 2), (second, 3), (partial(late_ring, distances=(3,)), 4)], 2),
             ([(last, 3), (last, 4)], 3),
         ):
             coming = [array for move, at in moves for array in move(gathers[at])]
-            if beside is not None:
-                kernel(beside)
+            beside = [] if beside is None else kernel(beside)
             if coming:
-                steps.wait(coming)
+                steps.wait(coming + beside)
         pieces.append(gathers[4].pieces)
     else:
         state["riders"] = lax.all_gather(window, ALL)

time: 297 us -> 291 us (0.980)
  Pallas kernels: 121 us -> 112 us
  waiting for transfers between devices: 66.1 us -> 70.3 us
    pallas_call x5, Pallas kernels: 113 us -> 108 us  [run(): pl.pallas_call(body, out_shape=results, in_specs=[anywhere] * len(away) +...]
    pallas_call x7, Pallas kernels: 7.98 us -> 3.65 us  [zero_after(): pl.pallas_call(zero_body, out_shape=shape((1, 1), f32), in_specs=[pl.Bloc...]
    unnamed x90 -> x76, local copies, waits for them, and re-layouts: 12 us -> 13.1 us
  transfers between devices with their start and end apart: 38 -> 38, of which waited for: 21 -> 22; matrix products, arithmetic and copies ran while one was open for 3% -> 3% of each run, Pallas kernels for 20% -> 18%
where the time goes in v3:
time: 291 us; the launch traced here: 286 us
  Pallas kernels  112 us (38%)
  waiting for transfers between devices  70.3 us (24%)
  starting transfers between devices  63.9 us (22%)
  local copies, waits for them, and re-layouts  17.4 us (6%)
  between operations  12.8 us (4%)
  other arithmetic  9.46 us (3%)
    pallas_call x5, Pallas kernels, run(): pl.pallas_call(body, out_shape=results, in_specs=[anywhere] * len(away) +...  108 us
    ppermute x18, starting transfers between devices, swap_z(): lax.ppermute(value, 'z', [(i, i ^ distance) for i in range(lax.axis_size(...  41.1 us
    ppermute x18, waiting for transfers between devices, swap_z(): lax.ppermute(value, 'z', [(i, i ^ distance) for i in range(lax.axis_size(...  38.4 us
    ppermute x13, waiting for transfers between devices, move_all(): return lax.ppermute(value, ALL, moves)  25 us
    unnamed x76, local copies, waits for them, and re-layouts  13.1 us
    ppermute x7, starting transfers between devices, flip(): return lax.ppermute(value, axis, [(0, 1), (1, 0)])  12.3 us
    ppermute x13, starting transfers between devices, move_all(): return lax.ppermute(value, ALL, moves)  10.5 us
    ppermute x7, waiting for transfers between devices, flip(): return lax.ppermute(value, axis, [(0, 1), (1, 0)])  6.8 us
  transfers between devices with their start and end apart: 38, of which 22 were waited for; matrix products, arithmetic and copies ran while one was open for 3% of the time, Pallas kernels for 18%

profile of v3, /device:TPU:1, one launch (start us, length us, event | category | flops | bytes accessed | tf_op | source)
XLA Modules:
  0.0 285.6 jit_solution(13982783959884410020)
XLA Ops:
  2.7 2.2 collective-permute-start
  4.9 2.3 collective-permute-start.1
  9.6 5.5 %collective-permute-done.2.refs_2_ = bf16[48,1280]{1,0:T(8,128)(2,1)S(1)} collective-permute-done((bf16[48,1280]{1,0:T(8,128)(2,1)S(1)}, bf16[48,1280]{1,0:T(8,128)(2,1)S(1)}, u32[]{:S(2)}, u32[]{:S(2)}) %collective-permute-start.2) | collective-permute-done | bytes 122912 | tf_op jit(solution)/shard_map/ppermute | solution.py:657
  18.1 7.5 %collective-permute-done.3.refs_1_ = bf16[48,1152]{1,0:T(8,128)(2,1)S(1)} collective-permute-done((bf16[48,1152]{1,0:T(8,128)(2,1)S(1)}, bf16[48,1152]{1,0:T(8,128)(2,1)S(1)}, u32[]{:S(2)}, u32[]{:S(2)}) %collective-permute-start.3) | collective-permute-done | bytes 110624 | tf_op jit(solution)/shard_map/ppermute | solution.py:642
  28.3 2.6 collective-permute-start.6
  34.2 2.1 collective-permute-done.7.refs_1_
  36.3 6.8 %collective-permute-done.8.refs_2_ = bf16[48,1920]{1,0:T(8,128)(2,1)S(1)} collective-permute-done((bf16[48,1920]{1,0:T(8,128)(2,1)S(1)}, bf16[48,1920]{1,0:T(8,128)(2,1)S(1)}, u32[]{:S(2)}, u32[]{:S(2)}) %collective-permute-start.8) | collective-permute-done | bytes 184352 | tf_op jit(solution)/shard_map/ppermute | solution.py:657
  44.5 5.7 %collective-permute-start.14 = (bf16[2,2,4,48,1280]{4,3,2,1,0:T(8,128)(2,1)S(1)}, bf16[2,2,4,48,1280]{4,3,2,1,0:T(8,128)(2,1)S(1)}, u32[]{:S(2)}, u32[]{:S(2)}) collective-permute-start(bf16[2,2,4,48,1280]{4,3,2,1,0:T(8,128)(2,1)S(1)} %maximum_add_fusion.5.refs_0_), channel_id=1, source_target_pairs={{0,2},{2,0},{1,3},{3,1},{4,6},{6,4},{5,7},{7,5},{8,10},{10,8},{9,1... | collective-permute-start | bytes 5898248 | tf_op jit(solution)/shard_map/ppermute | solution.py:634
  51.8 2.3 collective-permute-start.10
  56.9 10.9 %attn_forward.2 = (bf16[512,768]{1,0:T(8,128)(2,1)S(1)}, f32[128,512]{1,0:T(8,128)S(1)}, f32[512,768]{1,0:T(8,128)S(1)}, bf16[512,2304]{1,0:T(8,128)(2,1)S(1)}, ...) custom-call(bf16[2,2,4,48,1280]{4,3,2,1,0:T(8,128)(2,1)S(1)} %maximum_add_fusion.5.refs_0_, ...), custom_call_target="tpu_custom_call" | custom-call | flops 5033164800 | bytes 13648384 | tf_op jit(solution)/shard_map/attn_forward/pallas_call | solution.py:465
  69.3 4.9 %collective-permute-done.12.refs_2_ = bf16[48,2688]{1,0:T(8,128)(2,1)S(1)} collective-permute-done((bf16[48,2688]{1,0:T(8,128)(2,1)S(1)}, bf16[48,2688]{1,0:T(8,128)(2,1)S(1)}, u32[]{:S(2)}, u32[]{:S(2)}) %collective-permute-start.12) | collective-permute-done | bytes 258080 | tf_op jit(solution)/shard_map/ppermute | solution.py:657
  76.2 6.0 %collective-permute-start.15 = (bf16[48,2304]{1,0:T(8,128)(2,1)S(1)}, bf16[48,2304]{1,0:T(8,128)(2,1)S(1)}, u32[]{:S(2)}, u32[]{:S(2)}) collective-permute-start(bf16[48,2304]{1,0:T(8,128)(2,1)S(1)} %maximum_add_fusion.27), channel_id=1, source_target_pairs={{0,8},{8,0},{16,24},{24,16},{1,9},{9,1},{17,25},{25,17},{2,10},{10... | collective-permute-start | bytes 663560 | tf_op jit(solution)/shard_map/ppermute | solution.py:657
  84.9 4.5 %collective-permute-done.15.refs_0_ = bf16[48,2304]{1,0:T(8,128)(2,1)S(1)} collective-permute-done((bf16[48,2304]{1,0:T(8,128)(2,1)S(1)}, bf16[48,2304]{1,0:T(8,128)(2,1)S(1)}, u32[]{:S(2)}, u32[]{:S(2)}) %collective-permute-start.15) | collective-permute-done | bytes 221216 | tf_op jit(solution)/shard_map/ppermute | solution.py:657
  90.3 7.9 %collective-permute-done.17.refs_2_ = bf16[48,2304]{1,0:T(8,128)(2,1)S(1)} collective-permute-done((bf16[48,2304]{1,0:T(8,128)(2,1)S(1)}, bf16[48,2304]{1,0:T(8,128)(2,1)S(1)}, u32[]{:S(2)}, u32[]{:S(2)}) %collective-permute-start.17) | collective-permute-done | bytes 221216 | tf_op jit(solution)/shard_map/ppermute | solution.py:657
  98.2 2.1 collective-permute-done.19.refs_4_
  100.3 5.0 %collective-permute-done.18.refs_3_ = bf16[2,4,48,1920]{3,2,1,0:T(8,128)(2,1)S(1)} collective-permute-done((bf16[2,4,48,1920]{3,2,1,0:T(8,128)(2,1)S(1)}, bf16[2,4,48,1920]{3,2,1,0:T(8,128)(2,1)S(1)}, u32[]{:S(2)}, u32[]{:S(2)}) %collective-permute-start.18) | collective-permute-done | bytes 1474592 | tf_op jit(solution)/shard_map/ppermute | solution.py:642
  110.1 5.5 %collective-permute-start.20 = (bf16[2,2,48,1152]{3,2,1,0:T(8,128)(2,1)S(1)}, bf16[2,2,48,1152]{3,2,1,0:T(8,128)(2,1)S(1)}, u32[]{:S(2)}, u32[]{:S(2)}) collective-permute-start(bf16[2,2,48,1152]{3,2,1,0:T(8,128)(2,1)S(1)} %maximum_add_fusion.22), channel_id=1, source_target_pairs={{0,8},{8,0},{16,24},{24,16},{1,9},{9,1},{17,25},{25,17},{2,10},{10... | collective-permute-start | bytes 1327112 | tf_op jit(solution)/shard_map/ppermute | solution.py:657
  117.5 13.7 %mlp_up.2 = (f32[512,768]{1,0:T(8,128)S(1)}, bf16[512,3072]{1,0:T(8,128)(2,1)S(1)}, bf16[4,192,768]{2,1,0:T(8,128)(2,1)S(1)}, bf16[4,192,3072]{2,1,0:T(8,128)(2,1)S(1)}, bf16[512,3072]{1,0:T(8,128)(2,1)S(1)}) custom-call(bf16[2,2,4,48,1920]{4,3,2,1,0:T(8,128)(2,1)S(1)} %maximum_add_fusion.2.refs_0_, ...), custom_call_target="tpu_custom_call" | custom-call | flops 3019898880 | bytes 22032384 | tf_op jit(solution)/shard_map/mlp_up/pallas_call | solution.py:465
  131.2 2.2 copy-done.17
  135.1 7.3 %collective-permute-done.24.refs_0_ = bf16[2,4,48,2688]{3,2,1,0:T(8,128)(2,1)S(1)} collective-permute-done((bf16[2,4,48,2688]{3,2,1,0:T(8,128)(2,1)S(1)}, bf16[2,4,48,2688]{3,2,1,0:T(8,128)(2,1)S(1)}, u32[]{:S(2)}, u32[]{:S(2)}) %collective-permute-start.24) | collective-permute-done | bytes 2064416 | tf_op jit(solution)/shard_map/ppermute | solution.py:642
  146.8 2.6 collective-permute-start.22
  149.8 2.0 collective-permute-done.27.refs_1_
  151.7 15.3 %attn_forward.3 = (bf16[512,768]{1,0:T(8,128)(2,1)S(1)}, f32[128,512]{1,0:T(8,128)S(1)}, f32[512,768]{1,0:T(8,128)S(1)}, bf16[512,2304]{1,0:T(8,128)(2,1)S(1)}, ...) custom-call(bf16[2,2,4,48,2688]{4,3,2,1,0:T(8,128)(2,1)S(1)} %maximum_add_fusion.refs_0_, ...), custom_call_target="tpu_custom_call" | custom-call | flops 5033164800 | bytes 26624512 | tf_op jit(solution)/shard_map/attn_forward/pallas_call | solution.py:465
  171.6 1.8 maximum_add_fusion.6.refs_0_
  173.6 3.9 %collective-permute-done.29.refs_1_.refs_3_ = bf16[2,2,4,48,2304]{4,3,2,1,0:T(8,128)(2,1)} collective-permute-done((bf16[2,2,4,48,2304]{4,3,2,1,0:T(8,128)(2,1)S(1)}, bf16[2,2,4,48,2304]{4,3,2,1,0:T(8,128)(2,1)}, u32[]{:S(2)}, u32[]{:S(2)}) %collective-permute-start.29) | collective-permute-done | bytes 3538976 | tf_op jit(solution)/shard_map/ppermute | solution.py:634
  180.0 12.8 %mlp_up.3 = (f32[512,768]{1,0:T(8,128)S(1)}, bf16[512,3072]{1,0:T(8,128)(2,1)S(1)}, bf16[512,3072]{1,0:T(8,128)(2,1)S(1)}) custom-call(bf16[2,2,4,48,2304]{4,3,2,1,0:T(8,128)(2,1)S(1)} %maximum_add_fusion.1.refs_0_.refs_2_, bf16[2,2,4,48,2304]{4,3,2,1,0:T(8,128)(2,1)} %collective-permute-done.29.refs_1_.refs_3_, f32[512,768]{1,0:T(8,128)S(1)} %copy-done.6, ...), custom_call_target="tpu_custom_call" | custom-call | flops 3019898880 | bytes 17313792 | tf_op jit(solution)/shard_map/mlp_up/pallas_call | solution.py:465
  192.9 1.7 copy-done.15
  196.3 55.4 %backward.1 = (f32[512,768]{1,0:T(8,128)}, f32[2,50,768]{2,1,0:T(8,128)S(1)}, bf16[512,768]{1,0:T(8,128)(2,1)}) custom-call(bf16[4,2,2,48,1152]{4,3,2,1,0:T(8,128)(2,1)} %maximum_add_fusion.6.refs_0_, bf16[4,2,2,48,1152]{4,3,2,1,0:T(8,128)(2,1)} %collective-permute-done.28.refs_1_, bf16[2,2,4,48,2304]{4,3,2,1,0:T(8,128)(2,1)} %copy-done, ...), custom_call_target="tpu_custom_call" | custom-call | flops 23353884672 | bytes 52752384 | tf_op jit(solution)/shard_map/backward/pallas_call | solution.py:465
  259.1 5.6 %collective-permute-start.34 = (bf16[50,768]{1,0:T(8,128)(2,1)S(1)}, bf16[50,768]{1,0:T(8,128)(2,1)S(1)}, u32[]{:S(2)}, u32[]{:S(2)}) collective-permute-start(bf16[50,768]{1,0:T(8,128)(2,1)S(1)} %fusion.4), channel_id=1, source_target_pairs={{0,8},{8,0},{16,24},{24,16},{1,9},{9,1},{17,25},{25,17},{2,10},{10... | collective-permute-start | bytes 230408 | tf_op jit(solution)/shard_map/ppermute | solution.py:657
  269.0 2.6 collective-permute-done.36
  271.7 3.9 %collective-permute-start.37 = (bf16[50,768]{1,0:T(8,128)(2,1)S(1)}, bf16[50,768]{1,0:T(8,128)(2,1)S(1)}, u32[]{:S(2)}, u32[]{:S(2)}) collective-permute-start(bf16[50,768]{1,0:T(8,128)(2,1)S(1)} %get-tuple-element.55), channel_id=1, source_target_pairs={{0,2},{2,0},{1,3},{3,1},{4,6},{6,4},{5,7},{7,5},{8,10},{10,8},{9,1... | collective-permute-start | bytes 230408 | tf_op jit(solution)/shard_map/ppermute | solution.py:634
  282.2 2.0 multiply_subtract_fusion
  (193 shorter events, 56.1 us)
Async XLA Ops:
  2.7 6.3 %collective-permute-start = (bf16[48,1280]{1,0:T(8,128)(2,1)S(1)}, bf16[48,1280]{1,0:T(8,128)(2,1)S(1)}, u32[]{:S(2)}, u32[]{:S(2)}) collective-permute-start(bf16[48,1280]{1,0:T(8,128)(2,1)S(1)} %get-tuple-element.80), channel_id=1, source_target_pairs={{0,8},{8,0},{16,24},{24,16},{1,9},{9,1},{17,25},{25,17},{2,10},{10... | collective-permute-start | bytes 368648 | tf_op jit(solution)/shard_map/ppermute | solution.py:657
  7.2 7.9 %collective-permute-start.2 = (bf16[48,1280]{1,0:T(8,128)(2,1)S(1)}, bf16[48,1280]{1,0:T(8,128)(2,1)S(1)}, u32[]{:S(2)}, u32[]{:S(2)}) collective-permute-start(bf16[48,1280]{1,0:T(8,128)(2,1)S(1)} %get-tuple-element.80), channel_id=1, source_target_pairs={{0,24},{8,16},{16,8},{24,0},{1,25},{9,17},{17,9},{25,1},{2,26},{10... | collective-permute-start | bytes 368648 | tf_op jit(solution)/shard_map/ppermute | solution.py:657
  16.4 9.2 %collective-permute-start.4 = (bf16[4,48,1280]{2,1,0:T(8,128)(2,1)S(1)}, bf16[4,48,1280]{2,1,0:T(8,128)(2,1)S(1)}, u32[]{:S(2)}, u32[]{:S(2)}) collective-permute-start(bf16[4,48,1280]{2,1,0:T(8,128)(2,1)S(1)} %maximum_add_fusion.19), channel_id=1, source_target_pairs={{0,4},{1,5},{2,3},{3,2},{4,0},{5,1},{6,7},{7,6},{8,12},{9,13},{10,... | collective-permute-start | bytes 1474568 | tf_op jit(solution)/shard_map/ppermute | solution.py:642
  17.7 7.9 %collective-permute-start.3 = (bf16[48,1152]{1,0:T(8,128)(2,1)S(1)}, bf16[48,1152]{1,0:T(8,128)(2,1)S(1)}, u32[]{:S(2)}, u32[]{:S(2)}) collective-permute-start(bf16[48,1152]{1,0:T(8,128)(2,1)S(1)} %slice_add_fusion), channel_id=1, source_target_pairs={{0,4},{1,5},{2,3},{3,2},{4,0},{5,1},{6,7},{7,6},{8,12},{9,13},{10,... | collective-permute-start | bytes 331784 | tf_op jit(solution)/shard_map/ppermute | solution.py:642
  26.9 16.2 %collective-permute-start.9 = (bf16[2,4,48,1280]{3,2,1,0:T(8,128)(2,1)S(1)}, bf16[2,4,48,1280]{3,2,1,0:T(8,128)(2,1)S(1)}, u32[]{:S(2)}, u32[]{:S(2)}) collective-permute-start(bf16[2,4,48,1280]{3,2,1,0:T(8,128)(2,1)S(1)} %maximum_add_fusion.13), channel_id=1, source_target_pairs={{0,1},{1,0},{2,6},{3,7},{4,5},{5,4},{6,2},{7,3},{8,9},{9,8},{10,14... | collective-permute-start | bytes 2949128 | tf_op jit(solution)/shard_map/ppermute | solution.py:642
  28.3 5.9 %collective-permute-start.6 = (bf16[48,1920]{1,0:T(8,128)(2,1)S(1)}, bf16[48,1920]{1,0:T(8,128)(2,1)S(1)}, u32[]{:S(2)}, u32[]{:S(2)}) collective-permute-start(bf16[48,1920]{1,0:T(8,128)(2,1)S(1)} %maximum_add_fusion.29), channel_id=1, source_target_pairs={{0,8},{8,0},{16,24},{24,16},{1,9},{9,1},{17,25},{25,17},{2,10},{10... | collective-permute-start | bytes 552968 | tf_op jit(solution)/shard_map/ppermute | solution.py:657
  30.9 5.4 %collective-permute-start.7 = (bf16[48,1920]{1,0:T(8,128)(2,1)S(1)}, bf16[48,1920]{1,0:T(8,128)(2,1)S(1)}, u32[]{:S(2)}, u32[]{:S(2)}) collective-permute-start(bf16[48,1920]{1,0:T(8,128)(2,1)S(1)} %maximum_add_fusion.29), channel_id=1, source_target_pairs={{0,16},{8,24},{16,0},{24,8},{1,17},{9,25},{17,1},{25,9},{2,18},{10... | collective-permute-start | bytes 552968 | tf_op jit(solution)/shard_map/ppermute | solution.py:657
  32.5 10.7 %collective-permute-start.8 = (bf16[48,1920]{1,0:T(8,128)(2,1)S(1)}, bf16[48,1920]{1,0:T(8,128)(2,1)S(1)}, u32[]{:S(2)}, u32[]{:S(2)}) collective-permute-start(bf16[48,1920]{1,0:T(8,128)(2,1)S(1)} %maximum_add_fusion.29), channel_id=1, source_target_pairs={{0,24},{8,16},{16,8},{24,0},{1,25},{9,17},{17,9},{25,1},{2,26},{10... | collective-permute-start | bytes 552968 | tf_op jit(solution)/shard_map/ppermute | solution.py:657
  33.6 9.5 %collective-permute-start.5 = (bf16[2,48,1152]{2,1,0:T(8,128)(2,1)S(1)}, bf16[2,48,1152]{2,1,0:T(8,128)(2,1)S(1)}, u32[]{:S(2)}, u32[]{:S(2)}) collective-permute-start(bf16[2,48,1152]{2,1,0:T(8,128)(2,1)S(1)} %maximum_add_fusion.26), channel_id=1, source_target_pairs={{0,1},{1,0},{2,6},{3,7},{4,5},{5,4},{6,2},{7,3},{8,9},{9,8},{10,14... | collective-permute-start | bytes 663560 | tf_op jit(solution)/shard_map/ppermute | solution.py:642
  44.5 12.3 %collective-permute-start.14 = (bf16[2,2,4,48,1280]{4,3,2,1,0:T(8,128)(2,1)S(1)}, bf16[2,2,4,48,1280]{4,3,2,1,0:T(8,128)(2,1)S(1)}, u32[]{:S(2)}, u32[]{:S(2)}) collective-permute-start(bf16[2,2,4,48,1280]{4,3,2,1,0:T(8,128)(2,1)S(1)} %maximum_add_fusion.5.refs_0_), channel_id=1, source_target_pairs={{0,2},{2,0},{1,3},{3,1},{4,6},{6,4},{5,7},{7,5},{8,10},{10,8},{9,1... | collective-permute-start | bytes 5898248 | tf_op jit(solution)/shard_map/ppermute | solution.py:634
  50.4 23.8 %collective-permute-start.13 = (bf16[4,48,1920]{2,1,0:T(8,128)(2,1)S(1)}, bf16[4,48,1920]{2,1,0:T(8,128)(2,1)S(1)}, u32[]{:S(2)}, u32[]{:S(2)}) collective-permute-start(bf16[4,48,1920]{2,1,0:T(8,128)(2,1)S(1)} %maximum_add_fusion.17), channel_id=1, source_target_pairs={{0,4},{1,5},{2,3},{3,2},{4,0},{5,1},{6,7},{7,6},{8,12},{9,13},{10,... | collective-permute-start | bytes 2211848 | tf_op jit(solution)/shard_map/ppermute | solution.py:642
  51.8 17.5 %collective-permute-start.10 = (bf16[48,2688]{1,0:T(8,128)(2,1)S(1)}, bf16[48,2688]{1,0:T(8,128)(2,1)S(1)}, u32[]{:S(2)}, u32[]{:S(2)}) collective-permute-start(bf16[48,2688]{1,0:T(8,128)(2,1)S(1)} %maximum_add_fusion.23), channel_id=1, source_target_pairs={{0,8},{8,0},{16,24},{24,16},{1,9},{9,1},{17,25},{25,17},{2,10},{10... | collective-permute-start | bytes 774152 | tf_op jit(solution)/shard_map/ppermute | solution.py:657
  54.1 15.2 %collective-permute-start.11 = (bf16[48,2688]{1,0:T(8,128)(2,1)S(1)}, bf16[48,2688]{1,0:T(8,128)(2,1)S(1)}, u32[]{:S(2)}, u32[]{:S(2)}) collective-permute-start(bf16[48,2688]{1,0:T(8,128)(2,1)S(1)} %maximum_add_fusion.23), channel_id=1, source_target_pairs={{0,16},{8,24},{16,0},{24,8},{1,17},{9,25},{17,1},{25,9},{2,18},{10... | collective-permute-start | bytes 774152 | tf_op jit(solution)/shard_map/ppermute | solution.py:657
  55.6 18.6 %collective-permute-start.12 = (bf16[48,2688]{1,0:T(8,128)(2,1)S(1)}, bf16[48,2688]{1,0:T(8,128)(2,1)S(1)}, u32[]{:S(2)}, u32[]{:S(2)}) collective-permute-start(bf16[48,2688]{1,0:T(8,128)(2,1)S(1)} %maximum_add_fusion.23), channel_id=1, source_target_pairs={{0,24},{8,16},{16,8},{24,0},{1,25},{9,17},{17,9},{25,1},{2,26},{10... | collective-permute-start | bytes 774152 | tf_op jit(solution)/shard_map/ppermute | solution.py:657
  75.6 29.6 %collective-permute-start.18 = (bf16[2,4,48,1920]{3,2,1,0:T(8,128)(2,1)S(1)}, bf16[2,4,48,1920]{3,2,1,0:T(8,128)(2,1)S(1)}, u32[]{:S(2)}, u32[]{:S(2)}) collective-permute-start(bf16[2,4,48,1920]{3,2,1,0:T(8,128)(2,1)S(1)} %maximum_add_fusion.9), channel_id=1, source_target_pairs={{0,1},{1,0},{2,6},{3,7},{4,5},{5,4},{6,2},{7,3},{8,9},{9,8},{10,14... | collective-permute-start | bytes 4423688 | tf_op jit(solution)/shard_map/ppermute | solution.py:642
  76.0 24.3 %collective-permute-start.19 = (bf16[4,48,2688]{2,1,0:T(8,128)(2,1)S(1)}, bf16[4,48,2688]{2,1,0:T(8,128)(2,1)S(1)}, u32[]{:S(2)}, u32[]{:S(2)}) collective-permute-start(bf16[4,48,2688]{2,1,0:T(8,128)(2,1)S(1)} %maximum_add_fusion.11), channel_id=1, source_target_pairs={{0,4},{1,5},{2,3},{3,2},{4,0},{5,1},{6,7},{7,6},{8,12},{9,13},{10,... | collective-permute-start | bytes 3096584 | tf_op jit(solution)/shard_map/ppermute | solution.py:642
  76.2 13.2 %collective-permute-start.15 = (bf16[48,2304]{1,0:T(8,128)(2,1)S(1)}, bf16[48,2304]{1,0:T(8,128)(2,1)S(1)}, u32[]{:S(2)}, u32[]{:S(2)}) collective-permute-start(bf16[48,2304]{1,0:T(8,128)(2,1)S(1)} %maximum_add_fusion.27), channel_id=1, source_target_pairs={{0,8},{8,0},{16,24},{24,16},{1,9},{9,1},{17,25},{25,17},{2,10},{10... | collective-permute-start | bytes 663560 | tf_op jit(solution)/shard_map/ppermute | solution.py:657
  82.2 8.1 %collective-permute-start.16 = (bf16[48,2304]{1,0:T(8,128)(2,1)S(1)}, bf16[48,2304]{1,0:T(8,128)(2,1)S(1)}, u32[]{:S(2)}, u32[]{:S(2)}) collective-permute-start(bf16[48,2304]{1,0:T(8,128)(2,1)S(1)} %maximum_add_fusion.27), channel_id=1, source_target_pairs={{0,16},{8,24},{16,0},{24,8},{1,17},{9,25},{17,1},{25,9},{2,18},{10... | collective-permute-start | bytes 663560 | tf_op jit(solution)/shard_map/ppermute | solution.py:657
  83.6 14.5 %collective-permute-start.17 = (bf16[48,2304]{1,0:T(8,128)(2,1)S(1)}, bf16[48,2304]{1,0:T(8,128)(2,1)S(1)}, u32[]{:S(2)}, u32[]{:S(2)}) collective-permute-start(bf16[48,2304]{1,0:T(8,128)(2,1)S(1)} %maximum_add_fusion.27), channel_id=1, source_target_pairs={{0,24},{8,16},{16,8},{24,0},{1,25},{9,17},{17,9},{25,1},{2,26},{10... | collective-permute-start | bytes 663560 | tf_op jit(solution)/shard_map/ppermute | solution.py:657
  106.8 10.7 %collective-permute-start.25 = (bf16[2,2,4,48,1920]{4,3,2,1,0:T(8,128)(2,1)S(1)}, bf16[2,2,4,48,1920]{4,3,2,1,0:T(8,128)(2,1)S(1)}, u32[]{:S(2)}, u32[]{:S(2)}) collective-permute-start(bf16[2,2,4,48,1920]{4,3,2,1,0:T(8,128)(2,1)S(1)} %maximum_add_fusion.2.refs_0_), channel_id=1, source_target_pairs={{0,2},{2,0},{1,3},{3,1},{4,6},{6,4},{5,7},{7,5},{8,10},{10,8},{9,1... | collective-permute-start | bytes 8847368 | tf_op jit(solution)/shard_map/ppermute | solution.py:634
  108.1 34.4 %collective-permute-start.24 = (bf16[2,4,48,2688]{3,2,1,0:T(8,128)(2,1)S(1)}, bf16[2,4,48,2688]{3,2,1,0:T(8,128)(2,1)S(1)}, u32[]{:S(2)}, u32[]{:S(2)}) collective-permute-start(bf16[2,4,48,2688]{3,2,1,0:T(8,128)(2,1)S(1)} %maximum_add_fusion.3), channel_id=1, source_target_pairs={{0,1},{1,0},{2,6},{3,7},{4,5},{5,4},{6,2},{7,3},{8,9},{9,8},{10,14... | collective-permute-start | bytes 6193160 | tf_op jit(solution)/shard_map/ppermute | solution.py:642
  110.0 25.1 %collective-permute-start.23 = (bf16[4,48,2304]{2,1,0:T(8,128)(2,1)S(1)}, bf16[4,48,2304]{2,1,0:T(8,128)(2,1)S(1)}, u32[]{:S(2)}, u32[]{:S(2)}) collective-permute-start(bf16[4,48,2304]{2,1,0:T(8,128)(2,1)S(1)} %maximum_add_fusion.16), channel_id=1, source_target_pairs={{0,4},{1,5},{2,3},{3,2},{4,0},{5,1},{6,7},{7,6},{8,12},{9,13},{10,... | collective-permute-start | bytes 2654216 | tf_op jit(solution)/shard_map/ppermute | solution.py:642
  110.1 25.0 %collective-permute-start.20 = (bf16[2,2,48,1152]{3,2,1,0:T(8,128)(2,1)S(1)}, bf16[2,2,48,1152]{3,2,1,0:T(8,128)(2,1)S(1)}, u32[]{:S(2)}, u32[]{:S(2)}) collective-permute-start(bf16[2,2,48,1152]{3,2,1,0:T(8,128)(2,1)S(1)} %maximum_add_fusion.22), channel_id=1, source_target_pairs={{0,8},{8,0},{16,24},{24,16},{1,9},{9,1},{17,25},{25,17},{2,10},{10... | collective-permute-start | bytes 1327112 | tf_op jit(solution)/shard_map/ppermute | solution.py:657
  115.7 19.5 %collective-permute-start.21 = (bf16[2,2,48,1152]{3,2,1,0:T(8,128)(2,1)S(1)}, bf16[2,2,48,1152]{3,2,1,0:T(8,128)(2,1)S(1)}, u32[]{:S(2)}, u32[]{:S(2)}) collective-permute-start(bf16[2,2,48,1152]{3,2,1,0:T(8,128)(2,1)S(1)} %maximum_add_fusion.22), channel_id=1, source_target_pairs={{0,16},{8,24},{16,0},{24,8},{1,17},{9,25},{17,1},{25,9},{2,18},{10... | collective-permute-start | bytes 1327112 | tf_op jit(solution)/shard_map/ppermute | solution.py:657
  144.1 7.6 %collective-permute-start.27 = (bf16[2,2,4,48,2688]{4,3,2,1,0:T(8,128)(2,1)S(1)}, bf16[2,2,4,48,2688]{4,3,2,1,0:T(8,128)(2,1)S(1)}, u32[]{:S(2)}, u32[]{:S(2)}) collective-permute-start(bf16[2,2,4,48,2688]{4,3,2,1,0:T(8,128)(2,1)S(1)} %maximum_add_fusion.refs_0_), channel_id=1, source_target_pairs={{0,2},{2,0},{1,3},{3,1},{4,6},{6,4},{5,7},{7,5},{8,10},{10,8},{9,1... | collective-permute-start | bytes 12386312 | tf_op jit(solution)/shard_map/ppermute | solution.py:634
  145.3 22.4 %collective-permute-start.26 = (bf16[2,4,48,2304]{3,2,1,0:T(8,128)(2,1)S(1)}, bf16[2,4,48,2304]{3,2,1,0:T(8,128)(2,1)S(1)}, u32[]{:S(2)}, u32[]{:S(2)}) collective-permute-start(bf16[2,4,48,2304]{3,2,1,0:T(8,128)(2,1)S(1)} %maximum_add_fusion.7), channel_id=1, source_target_pairs={{0,1},{1,0},{2,6},{3,7},{4,5},{5,4},{6,2},{7,3},{8,9},{9,8},{10,14... | collective-permute-start | bytes 5308424 | tf_op jit(solution)/shard_map/ppermute | solution.py:642
  146.8 20.9 %collective-permute-start.22 = (bf16[2,2,48,1152]{3,2,1,0:T(8,128)(2,1)S(1)}, bf16[2,2,48,1152]{3,2,1,0:T(8,128)(2,1)S(1)}, u32[]{:S(2)}, u32[]{:S(2)}) collective-permute-start(bf16[2,2,48,1152]{3,2,1,0:T(8,128)(2,1)S(1)} %maximum_add_fusion.22), channel_id=1, source_target_pairs={{0,24},{8,16},{16,8},{24,0},{1,25},{9,17},{17,9},{25,1},{2,26},{10... | collective-permute-start | bytes 1327112 | tf_op jit(solution)/shard_map/ppermute | solution.py:657
  171.1 6.4 %collective-permute-start.29 = (bf16[2,2,4,48,2304]{4,3,2,1,0:T(8,128)(2,1)S(1)}, bf16[2,2,4,48,2304]{4,3,2,1,0:T(8,128)(2,1)}, u32[]{:S(2)}, u32[]{:S(2)}) collective-permute-start(bf16[2,2,4,48,2304]{4,3,2,1,0:T(8,128)(2,1)S(1)} %maximum_add_fusion.1.refs_0_.refs_2_), channel_id=1, source_target_pairs={{0,2},{2,0},{1,3},{3,1},{4,6},{6,4},{5,7},{7,5},{8,10},{10,8},{9,1... | collective-permute-start | bytes 10616840 | tf_op jit(solution)/shard_map/ppermute | solution.py:634
  173.4 22.8 %collective-permute-start.28 = (bf16[4,2,2,48,1152]{4,3,2,1,0:T(8,128)(2,1)}, bf16[4,2,2,48,1152]{4,3,2,1,0:T(8,128)(2,1)}, u32[]{:S(2)}, u32[]{:S(2)}) collective-permute-start(bf16[4,2,2,48,1152]{4,3,2,1,0:T(8,128)(2,1)} %maximum_add_fusion.6.refs_0_), channel_id=1, source_target_pairs={{0,2},{2,0},{1,3},{3,1},{4,6},{6,4},{5,7},{7,5},{8,10},{10,8},{9,1... | collective-permute-start | bytes 5308424 | tf_op jit(solution)/shard_map/ppermute | solution.py:634
  259.1 8.2 %collective-permute-start.34 = (bf16[50,768]{1,0:T(8,128)(2,1)S(1)}, bf16[50,768]{1,0:T(8,128)(2,1)S(1)}, u32[]{:S(2)}, u32[]{:S(2)}) collective-permute-start(bf16[50,768]{1,0:T(8,128)(2,1)S(1)} %fusion.4), channel_id=1, source_target_pairs={{0,8},{8,0},{16,24},{24,16},{1,9},{9,1},{17,25},{25,17},{2,10},{10... | collective-permute-start | bytes 230408 | tf_op jit(solution)/shard_map/ppermute | solution.py:657
  266.2 5.4 %collective-permute-start.36 = (bf16[50,768]{1,0:T(8,128)(2,1)S(1)}, bf16[50,768]{1,0:T(8,128)(2,1)S(1)}, u32[]{:S(2)}, u32[]{:S(2)}) collective-permute-start(bf16[50,768]{1,0:T(8,128)(2,1)S(1)} %fusion.4), channel_id=1, source_target_pairs={{0,24},{8,16},{16,8},{24,0},{1,25},{9,17},{17,9},{25,1},{2,26},{10... | collective-permute-start | bytes 230408 | tf_op jit(solution)/shard_map/ppermute | solution.py:657
  271.7 8.9 %collective-permute-start.37 = (bf16[50,768]{1,0:T(8,128)(2,1)S(1)}, bf16[50,768]{1,0:T(8,128)(2,1)S(1)}, u32[]{:S(2)}, u32[]{:S(2)}) collective-permute-start(bf16[50,768]{1,0:T(8,128)(2,1)S(1)} %get-tuple-element.55), channel_id=1, source_target_pairs={{0,2},{2,0},{1,3},{3,1},{4,6},{6,4},{5,7},{7,5},{8,10},{10,8},{9,1... | collective-permute-start | bytes 230408 | tf_op jit(solution)/shard_map/ppermute | solution.py:634
  (44 other events, 460.3 us)
